TPU v7x, 32 devices: a whole 2x2x4 slice. The times are simulated.
32 devices in a mesh: dp: 8 (over z, y), mp: 4 (over x, core).
Axes of the slice: x: 2, y: 2, z: 4, core: 2. Of those that a mesh axis runs over, the one named last changes fastest.
Arguments:
- patches: bfloat16 [16384, 768], P('dp'), may hold values from -6 to 6
- image_ids: int32 [16384], P('dp'), may hold values from 0 to 7, as said below
- patch_grid: int32 [2, 16384], P(None, 'dp'), may hold values from 0 to 31, as said below
- first_norm_gain: float32 [768], replicated, may hold values from 0.1 to 1.9
- first_norm_bias: float32 [768], replicated, may hold values from -1.8 to 1.8
- qkv_weight: bfloat16 [768, 3, 768], P(None, None, 'mp'), may hold values from -0.3125 to 0.3125
- qkv_bias: float32 [3, 768], P(None, 'mp'), may hold values from -1.8 to 1.8
- rope_freq: float32 [12, 64], P('mp'), may hold values from -1 to 1
- out_weight: bfloat16 [768, 768], P('mp'), may hold values from -0.625 to 0.625
- out_bias: float32 [768], replicated, may hold values from -1.8 to 1.8
- second_norm_gain: float32 [768], replicated, may hold values from 0.1 to 1.9
- second_norm_bias: float32 [768], replicated, may hold values from -1.8 to 1.8
- up_weight: bfloat16 [768, 3072], P(None, 'mp'), may hold values from -0.21875 to 0.21875
- up_bias: float32 [3072], P('mp'), may hold values from -1.8 to 1.8
- down_weight: bfloat16 [3072, 768], P('mp'), may hold values from -0.109375 to 0.109375
- down_bias: float32 [768], replicated, may hold values from -1.8 to 1.8
- out_grad: bfloat16 [16384, 768], P('dp'), may hold values from -6 to 6
Outputs:
- out: bfloat16 [16384, 768], P(('dp', 'mp'))
- patches_grad: bfloat16 [16384, 768], P(('dp', 'mp'))
- first_norm_gain_gradient: float32 [768], replicated
- ln1_bias_grad: float32 [768], replicated
- qkv_weight_grad: float32 [768, 3, 768], P(None, None, 'mp')
- qkv_bias_grad: float32 [3, 768], P(None, 'mp')
- rope_freq_grad: float32 [12, 64], P('mp')
- out_weight_grad: float32 [768, 768], P('mp')
- out_bias_grad: float32 [768], replicated
- second_norm_gain_gradient: float32 [768], replicated
- ln2_bias_grad: float32 [768], replicated
- up_weight_grad: float32 [768, 3072], P(None, 'mp')
- up_bias_grad: float32 [3072], P('mp')
- down_weight_grad: float32 [3072, 768], P('mp')
- down_bias_grad: float32 [768], replicated
Inputs may be any that keep to these rules, and one draw needn't show every extreme that they name: `image_ids`: each sequence of 1024 consecutive patches holds 8 images as contiguous runs with ids 0 to 7 in order. `patch_grid`: within an image the patches come in row-major order over a grid of 8 to 32 columns; its last row may be partial.
All inputs are finite; a program needn't handle non-finite values.
Results may differ from a plain program's by a relative error of at most 0.018.
The roundings to bfloat16 on the way count: a program that leaves them out, or rounds other values in their place, can miss the bound.
Values may be sent and summed in bfloat16 or wider, within the bound.
No kernel may reach another device: no remote copies, remote signals or barrier semaphores. Data moves between devices by JAX's collectives and lax.ppermute only.
A program may use at most 192 MiB of HBM per device.

v0:
```python
import jax
import jax.numpy as jnp
from jax import lax
from jax.sharding import PartitionSpec as P

LEN = 1024


masked_score = -1e30
epsilon = 1e-06


def standardize_rows(values):
    center = jnp.mean(values, axis=-1, keepdims=True)
    centered = values - center
    spread = jnp.mean(centered * centered, axis=-1, keepdims=True)
    inverse_deviation = lax.rsqrt(spread + epsilon)
    return (centered * inverse_deviation, inverse_deviation)


def layer_norm_backward(normalized_gradient, unit_variance_rows, inverse_deviation, norm_gain):
    scaled_rows = normalized_gradient * norm_gain
    return inverse_deviation * (
        scaled_rows
        - jnp.mean(scaled_rows, axis=-1, keepdims=True)
        - unit_variance_rows * jnp.mean(scaled_rows * unit_variance_rows, axis=-1, keepdims=True)
    )


def rotary(values, frequency, row_pos, col_pos):
    half_dim = values.shape[-1] // 2
    angles = (
        col_pos[:, None, None] * frequency[None, :, :half_dim]
        + row_pos[:, None, None] * frequency[None, :, half_dim:]
    )
    cosine = jnp.cos(angles)
    sine_of = jnp.sin(angles)
    first_half = values[..., :half_dim]
    second_half = values[..., half_dim:]
    return jnp.concatenate(
        [first_half * cosine - second_half * sine_of, first_half * sine_of + second_half * cosine],
        axis=-1,
    )


def gelu_exact(values):
    return jax.nn.gelu(values, approximate=False)


def attend(query, keys, values, image_ids):
    all_rows, heads_here, head_dim = query.shape
    seq_count = all_rows // LEN
    span_rows = min(512, LEN)
    inverse_deviation = head_dim ** (-0.5)

    def one_sequence(pieces_in):
        query_seq, keys_seq, values_seq, ids_seq = pieces_in
        context_parts = []
        total_parts = []
        for offset in range(0, LEN, span_rows):
            query_part = query_seq[offset : offset + span_rows]
            ids_part = ids_seq[offset : offset + span_rows]
            scores = (
                jnp.einsum("qhd,khd->hqk", query_part, keys_seq, preferred_element_type=jnp.float32)
                * inverse_deviation
            )
            scores = jnp.where((ids_part[:, None] == ids_seq[None, :])[None], scores, masked_score)
            row_max = jnp.max(scores, axis=-1, keepdims=True)
            expo_vals = jnp.exp(scores - row_max)
            row_total = jnp.sum(expo_vals, axis=-1, keepdims=True)
            probs_low = (expo_vals / row_total).astype(jnp.bfloat16)
            context_parts.append(
                jnp.einsum(
                    "hqk,khd->qhd", probs_low, values_seq, preferred_element_type=jnp.float32
                )
            )
            total_parts.append((row_max + jnp.log(row_total))[..., 0])
        return (jnp.concatenate(context_parts, axis=0), jnp.concatenate(total_parts, axis=1))

    shaped = (
        query.reshape(seq_count, LEN, heads_here, head_dim),
        keys.reshape(seq_count, LEN, heads_here, head_dim),
        values.reshape(seq_count, LEN, heads_here, head_dim),
        image_ids.reshape(seq_count, LEN),
    )
    context, log_total = lax.map(one_sequence, shaped)
    return (context.reshape(all_rows, heads_here * head_dim).astype(jnp.bfloat16), log_total)


def attend_back(query, keys, values, log_total, context_grad, image_ids):
    all_rows, heads_here, head_dim = query.shape
    seq_count = all_rows // LEN
    span_rows = min(512, LEN)
    inverse_deviation = head_dim ** (-0.5)

    def one_sequence(pieces_in):
        query_seq, keys_seq, values_seq, total_seq, grad_seq, ids_seq = pieces_in
        key_acc = jnp.zeros(keys_seq.shape, jnp.float32)
        value_acc = jnp.zeros(values_seq.shape, jnp.float32)
        query_parts = []
        for offset in range(0, LEN, span_rows):
            query_part = query_seq[offset : offset + span_rows]
            ids_part = ids_seq[offset : offset + span_rows]
            grad_part = grad_seq[offset : offset + span_rows]
            scores = (
                jnp.einsum("qhd,khd->hqk", query_part, keys_seq, preferred_element_type=jnp.float32)
                * inverse_deviation
            )
            scores = jnp.where((ids_part[:, None] == ids_seq[None, :])[None], scores, masked_score)
            weights = jnp.exp(scores - total_seq[:, offset : offset + span_rows, None])
            prob_grad = jnp.einsum(
                "qhd,khd->hqk", grad_part, values_seq, preferred_element_type=jnp.float32
            )
            centre = jnp.sum(weights * prob_grad, axis=-1, keepdims=True)
            score_grad = (weights * (prob_grad - centre)).astype(jnp.bfloat16)
            query_parts.append(
                jnp.einsum("hqk,khd->qhd", score_grad, keys_seq, preferred_element_type=jnp.float32)
                * inverse_deviation
            )
            key_acc = (
                key_acc
                + jnp.einsum(
                    "hqk,qhd->khd", score_grad, query_part, preferred_element_type=jnp.float32
                )
                * inverse_deviation
            )
            value_acc = value_acc + jnp.einsum(
                "hqk,qhd->khd",
                weights.astype(jnp.bfloat16),
                grad_part,
                preferred_element_type=jnp.float32,
            )
        return (jnp.concatenate(query_parts, axis=0), key_acc, value_acc)

    shaped = (
        query.reshape(seq_count, LEN, heads_here, head_dim),
        keys.reshape(seq_count, LEN, heads_here, head_dim),
        values.reshape(seq_count, LEN, heads_here, head_dim),
        log_total,
        context_grad.reshape(seq_count, LEN, heads_here, head_dim),
        image_ids.reshape(seq_count, LEN),
    )
    query_grad, key_grad, value_grad = lax.map(one_sequence, shaped)
    return (
        query_grad.reshape(all_rows, heads_here, head_dim),
        key_grad.reshape(all_rows, heads_here, head_dim),
        value_grad.reshape(all_rows, heads_here, head_dim),
    )


def sum_feed(feed_local):
    return lax.psum((feed_local[0], feed_local[1], feed_local[2]), "dp")


def local(
    patches,
    image_ids,
    patch_grid,
    first_norm_gain,
    first_norm_bias,
    qkv_weight,
    qkv_bias,
    rope_freq,
    out_weight,
    out_bias,
    second_norm_gain,
    second_norm_bias,
    up_weight,
    up_bias,
    down_weight,
    down_bias,
    out_grad,
):
    all_rows = patches.shape[0]
    pieces = lax.axis_size("mp")
    my_rows = all_rows // pieces
    row_start = lax.axis_index("mp") * my_rows
    heads_here = rope_freq.shape[0]
    head_dim = rope_freq.shape[1]
    input_tokens = patches.astype(jnp.float32)
    rows_pos = patch_grid[0].astype(jnp.float32)
    cols_pos = patch_grid[1].astype(jnp.float32)
    first_unit_variance_rows, inverse_deviation_first = standardize_rows(input_tokens)
    first_normalized_rows = (first_unit_variance_rows * first_norm_gain + first_norm_bias).astype(
        jnp.bfloat16
    )
    mixed = (
        jnp.einsum(
            "td,dce->tce", first_normalized_rows, qkv_weight, preferred_element_type=jnp.float32
        )
        + qkv_bias[None]
    )
    query_pre = mixed[:, 0].reshape(all_rows, heads_here, head_dim)
    key_pre = mixed[:, 1].reshape(all_rows, heads_here, head_dim)
    value = mixed[:, 2].reshape(all_rows, heads_here, head_dim).astype(jnp.bfloat16)

    def rotate_pair(query_in, key_in, frequency):
        return (
            rotary(query_in, frequency, rows_pos, cols_pos),
            rotary(key_in, frequency, rows_pos, cols_pos),
        )

    (query_rot, key_rot), rotate_pull = jax.vjp(rotate_pair, query_pre, key_pre, rope_freq)
    query = query_rot.astype(jnp.bfloat16)
    keys = key_rot.astype(jnp.bfloat16)
    context, log_total = attend(query, keys, value, image_ids)
    partial_attn = jnp.dot(context, out_weight, preferred_element_type=jnp.float32)
    attn_out = lax.psum(partial_attn.astype(jnp.bfloat16), "mp").astype(jnp.float32) + out_bias
    first_residual_stream = input_tokens + attn_out
    second_unit_variance_rows, inverse_deviation_second = standardize_rows(first_residual_stream)
    local_normalized_rows = (
        second_unit_variance_rows * second_norm_gain + second_norm_bias
    ).astype(jnp.bfloat16)
    hidden_pre = (
        jnp.dot(local_normalized_rows, up_weight, preferred_element_type=jnp.float32) + up_bias
    )
    hidden_full, gelu_pull = jax.vjp(gelu_exact, hidden_pre)
    hidden = hidden_full.astype(jnp.bfloat16)
    partial_mlp = jnp.dot(hidden, down_weight, preferred_element_type=jnp.float32)
    result = (
        first_residual_stream
        + lax.psum(partial_mlp.astype(jnp.bfloat16), "mp").astype(jnp.float32)
        + down_bias
    )
    result_rows = lax.dynamic_slice_in_dim(result, row_start, my_rows, 0)
    out_rows = result_rows.astype(jnp.bfloat16)
    upstream_gradient = out_grad.astype(jnp.float32)
    down_bias_grad = jnp.sum(upstream_gradient, axis=0)
    down_weight_grad = jnp.einsum("tf,td->fd", hidden, out_grad, preferred_element_type=jnp.float32)
    hidden_grad = jnp.einsum("td,fd->tf", out_grad, down_weight, preferred_element_type=jnp.float32)
    pre_grad = gelu_pull(hidden_grad)[0].astype(jnp.bfloat16)
    up_bias_grad = jnp.sum(pre_grad.astype(jnp.float32), axis=0)
    up_weight_grad = jnp.einsum(
        "td,tf->df", local_normalized_rows, pre_grad, preferred_element_type=jnp.float32
    )
    partial_norm = jnp.einsum("tf,df->td", pre_grad, up_weight, preferred_element_type=jnp.float32)
    feed_local = (up_weight_grad, up_bias_grad, down_weight_grad)
    second_normalized_gradient = lax.psum(partial_norm.astype(jnp.bfloat16), "mp").astype(
        jnp.float32
    )
    second_norm_gain_gradient = jnp.sum(
        second_normalized_gradient * second_unit_variance_rows, axis=0
    )
    ln2_bias_grad = jnp.sum(second_normalized_gradient, axis=0)
    residual_gradient = upstream_gradient + layer_norm_backward(
        second_normalized_gradient,
        second_unit_variance_rows,
        inverse_deviation_second,
        second_norm_gain,
    )
    branch_local = residual_gradient.astype(jnp.bfloat16)
    out_bias_grad = jnp.sum(branch_local.astype(jnp.float32), axis=0)
    out_weight_grad = jnp.einsum(
        "te,td->ed", context, branch_local, preferred_element_type=jnp.float32
    )
    context_grad = jnp.einsum(
        "td,ed->te", branch_local, out_weight, preferred_element_type=jnp.float32
    ).astype(jnp.bfloat16)
    context_grad = context_grad.reshape(all_rows, heads_here, head_dim)
    query_grad, key_grad, value_grad = attend_back(
        query, keys, value, log_total, context_grad, image_ids
    )
    query_pre_grad, key_pre_grad, rope_freq_grad = rotate_pull((query_grad, key_grad))
    mixed_grad = jnp.stack(
        [
            query_pre_grad.reshape(all_rows, heads_here * head_dim),
            key_pre_grad.reshape(all_rows, heads_here * head_dim),
            value_grad.reshape(all_rows, heads_here * head_dim),
        ],
        axis=1,
    ).astype(jnp.bfloat16)
    qkv_bias_grad = jnp.sum(mixed_grad.astype(jnp.float32), axis=0)
    qkv_weight_grad = jnp.einsum(
        "td,tce->dce", first_normalized_rows, mixed_grad, preferred_element_type=jnp.float32
    )
    partial_input = jnp.einsum(
        "tce,dce->td", mixed_grad, qkv_weight, preferred_element_type=jnp.float32
    )
    first_normalized_gradient = lax.psum(partial_input.astype(jnp.bfloat16), "mp").astype(
        jnp.float32
    )
    first_norm_gain_gradient = jnp.sum(first_normalized_gradient * first_unit_variance_rows, axis=0)
    ln1_bias_grad = jnp.sum(first_normalized_gradient, axis=0)
    input_gradient = residual_gradient + layer_norm_backward(
        first_normalized_gradient,
        first_unit_variance_rows,
        inverse_deviation_first,
        first_norm_gain,
    )
    input_rows = lax.dynamic_slice_in_dim(input_gradient, row_start, my_rows, 0)
    grad_rows = input_rows.astype(jnp.bfloat16)
    feed_total = sum_feed(feed_local)
    (
        qkv_weight_grad,
        qkv_bias_grad,
        rope_freq_grad,
        out_weight_grad,
        first_norm_gain_gradient,
        ln1_bias_grad,
        out_bias_grad,
        second_norm_gain_gradient,
        ln2_bias_grad,
        down_bias_grad,
    ) = lax.psum(
        (
            qkv_weight_grad,
            qkv_bias_grad,
            rope_freq_grad,
            out_weight_grad,
            first_norm_gain_gradient,
            ln1_bias_grad,
            out_bias_grad,
            second_norm_gain_gradient,
            ln2_bias_grad,
            down_bias_grad,
        ),
        "dp",
    )
    return (
        out_rows,
        grad_rows,
        first_norm_gain_gradient,
        ln1_bias_grad,
        qkv_weight_grad,
        qkv_bias_grad,
        rope_freq_grad,
        out_weight_grad,
        out_bias_grad,
        second_norm_gain_gradient,
        ln2_bias_grad,
        feed_total[0],
        feed_total[1],
        feed_total[2],
        down_bias_grad,
    )


def solution(mesh):
    placed = (
        P("dp", None),
        P("dp"),
        P(None, "dp"),
        P(),
        P(),
        P(None, None, "mp"),
        P(None, "mp"),
        P("mp", None),
        P("mp", None),
        P(),
        P(),
        P(),
        P(None, "mp"),
        P("mp"),
        P("mp", None),
        P(),
        P("dp", None),
    )
    return jax.shard_map(
        local,
        mesh=mesh,
        in_specs=placed,
        out_specs=(
            P(("dp", "mp"), None),
            P(("dp", "mp"), None),
            P(),
            P(),
            P(None, None, "mp"),
            P(None, "mp"),
            P("mp", None),
            P("mp", None),
            P(),
            P(),
            P(),
            P(None, "mp"),
            P("mp"),
            P("mp", None),
            P(),
        ),
        check_vma=False,
    )
```

profile of v0, /device:TPU:0, one launch (start us, length us, event | category | flops | bytes accessed | tf_op | source)
XLA Modules:
  0.0 811.3 jit_solution(4869842192127060645)
XLA Ops:
  7.3 2.5 convert_reduce_fusion.2
  9.8 2.9 fusion.85
  12.9 2.3 fusion.104
  20.7 2.2 copy.36
  23.0 6.5 subtract_convert_fusion
  37.1 31.7 %while.26 = (s32[]{:T(128)}, bf16[2,1024,3,64]{1,3,2,0:T(8,128)(2,1)S(1)}, f32[2,3,1024]{2,1,0:T(4,128)S(1)}, bf16[2,1024,3,64]{1,3,2,0:T(8,128)(2,1)}, s32[2,10...) while((s32[]{:T(128)}, ...), condition=%wide.region_7.8_spmd, body=%wide.region_2.7_spmd.sunk | while | flops 844890112 | bytes 45247124 | solution.py:86
  37.8 2.3 fusion.174
  40.2 2.3 fusion.175
  42.5 3.5 fusion.176
  46.0 3.3 fusion.178
  49.3 3.3 fusion.177
  53.4 2.3 fusion.174
  55.7 2.3 fusion.175
  58.1 3.5 fusion.176
  61.6 3.3 fusion.178
  64.8 3.3 fusion.177
  70.7 2.7 convolution_convert_fusion.2
  73.5 71.2 %all-reduce.16.cloned.1.call-done = bf16[2048,768]{1,0:T(8,128)(2,1)} async-done(((bf16[2048,768]{1,0:T(8,128)(2,1)}), bf16[2048,768]{1,0:T(8,128)(2,1)}) %all-reduce.16.cloned.1.call-update) | async-done | bytes 3145744 | tf_op jit(solution)/shard_map/psum | solution.py:208
  144.7 3.9 fusion.113
  151.7 2.6 fusion.117
  154.7 19.1 %convert_reduce_fusion.4 = (f32[768]{0:T(1024)}, bf16[2048,768]{1,0:T(8,128)(2,1)S(1)}, f32[2048,768]{1,0:T(8,128)}) fusion(f32[2048,768]{1,0:T(8,128)S(1)} %fusion.117, f32[768]{0:T(1024)S(1)} %copy-done.46, bf16[2048,768]{1,0:T(8,128)(2,1)S(1)} %copy-done.13, bf16[768,768]{1,0:T(8,128)(2,1)S(1)} %copy-done), kind=kOutput, calls=%fused_computation.132 | convolution fusion | flops 2533883136 | bytes 20060160 | tf_op jit(solution)/shard_map/td,fd->tf/dot_general | solution.py:230
  175.5 4.0 convolution_convert_fusion
  179.6 5.5 multiply_convert_fusion.2
  186.9 4.0 convolution_convert_fusion.1
  190.9 57.4 %all-reduce.18.cloned.1.call-done = bf16[2048,768]{1,0:T(8,128)(2,1)} async-done(((bf16[2048,768]{1,0:T(8,128)(2,1)}), bf16[2048,768]{1,0:T(8,128)(2,1)}) %all-reduce.18.cloned.1.call-update) | async-done | bytes 3145744 | tf_op jit(solution)/shard_map/psum | solution.py:238
  248.3 5.9 fusion.90
  254.2 5.9 convert_reduce_fusion.5
  260.2 2.6 copy-done.4
  266.7 137.7 %while.27 = (s32[]{:T(128)}, f32[2,1024,3,64]{1,0,3,2:T(2,128)}, f32[2,1024,3,64]{1,0,3,2:T(2,128)}, bf16[2,1024,3,64]{1,3,2,0:T(8,128)(2,1)}, bf16[2,1024,3,64]...) while((s32[]{:T(128)}, f32[2,1024,3,64]{1,0,3,2:T(2,128)}, ...), condition=%wide.region_18.19_spmd, body=%wide.region_15.18_spmd.sunk | while | flops 2062480384 | bytes 128592088 | solution.py:143
  267.6 2.0 fusion.193
  269.6 2.0 fusion.191
  271.6 2.8 fusion.198
  274.4 3.6 fusion.199
  278.0 6.0 multiply_reduce_fusion.10
  284.1 6.0 multiply_reduce_fusion.11
  290.1 7.6 multiply_convert_fusion.4
  298.8 3.0 fusion.195
  306.7 14.4 %dynamic_update_slice.28 = f32[2,1024,3,64]{1,0,3,2:T(2,128)} dynamic-update-slice(f32[2,1024,3,64]{1,0,3,2:T(2,128)} %get-tuple-element.455, f32[1,1024,3,64]{1,0,3,2:T(1,128)S(1)} %copy.82, s32[]{:T(128)S(6)} %copy.104, s32[]{:T(128)} %constant.63.clone.1..sunk.1, s32[]{:T(128)} %constant.63.clone.1..sunk.1, s32[]{:T(128)} %constant.63.clone.1..sunk.1) | dynamic-update-slice | bytes 1572868 | tf_op jit(solution)/shard_map/while/body/jit(dynamic_update_index_in_dim)/dynamic_update_slice | solution.py:86
  321.1 14.4 %dynamic_update_slice.29 = f32[2,1024,3,64]{1,0,3,2:T(2,128)} dynamic-update-slice(f32[2,1024,3,64]{1,0,3,2:T(2,128)} %get-tuple-element.456, f32[1,1024,3,64]{1,0,3,2:T(1,128)S(1)} %copy.83, s32[]{:T(128)S(6)} %copy.104, s32[]{:T(128)} %constant.63.clone.1..sunk.1, s32[]{:T(128)} %constant.63.clone.1..sunk.1, s32[]{:T(128)} %constant.63.clone.1..sunk.1) | dynamic-update-slice | bytes 1572868 | tf_op jit(solution)/shard_map/while/body/jit(dynamic_update_index_in_dim)/dynamic_update_slice | solution.py:86
  336.2 1.9 fusion.193
  338.2 2.0 fusion.191
  340.1 2.8 fusion.198
  343.0 3.6 fusion.199
  346.6 6.0 multiply_reduce_fusion.10
  352.6 6.0 multiply_reduce_fusion.11
  358.7 7.6 multiply_convert_fusion.4
  367.3 3.0 fusion.195
  375.3 14.4 %dynamic_update_slice.28 = f32[2,1024,3,64]{1,0,3,2:T(2,128)} dynamic-update-slice(f32[2,1024,3,64]{1,0,3,2:T(2,128)} %get-tuple-element.455, f32[1,1024,3,64]{1,0,3,2:T(1,128)S(1)} %copy.82, s32[]{:T(128)S(6)} %copy.104, s32[]{:T(128)} %constant.63.clone.1..sunk.1, s32[]{:T(128)} %constant.63.clone.1..sunk.1, s32[]{:T(128)} %constant.63.clone.1..sunk.1) | dynamic-update-slice | bytes 1572868 | tf_op jit(solution)/shard_map/while/body/jit(dynamic_update_index_in_dim)/dynamic_update_slice | solution.py:86
  389.6 14.4 %dynamic_update_slice.29 = f32[2,1024,3,64]{1,0,3,2:T(2,128)} dynamic-update-slice(f32[2,1024,3,64]{1,0,3,2:T(2,128)} %get-tuple-element.456, f32[1,1024,3,64]{1,0,3,2:T(1,128)S(1)} %copy.83, s32[]{:T(128)S(6)} %copy.104, s32[]{:T(128)} %constant.63.clone.1..sunk.1, s32[]{:T(128)} %constant.63.clone.1..sunk.1, s32[]{:T(128)} %constant.63.clone.1..sunk.1) | dynamic-update-slice | bytes 1572868 | tf_op jit(solution)/shard_map/while/body/jit(dynamic_update_index_in_dim)/dynamic_update_slice | solution.py:86
  404.4 2.0 copy.46
  407.9 3.5 reshape.283
  411.4 5.9 multiply_add_fusion
  417.3 3.4 reshape.284
  420.7 6.4 multiply_add_fusion.1
  430.3 4.0 bitcast_convert_fusion
  434.4 7.1 fusion.118
  441.5 4.3 fusion.119
  448.7 3.6 fusion.103
  453.8 100.5 %all-reduce.22.cloned.1.call-done = (bf16[2048,768]{1,0:T(8,128)(2,1)}, bf16[2048,768]{1,0:T(8,128)(2,1)}) async-done(((bf16[2048,768]{1,0:T(8,128)(2,1)}, bf16[2048,768]{1,0:T(8,128)(2,1)}), (bf16[2048,768]{1,0:T(8,128)(2,1)}, bf16[2048,768]{1,0:T(8,128)(2,1)})) %all-reduce.22.cloned.1.call-update) | async-done | bytes 6291472 | tf_op jit(solution)/shard_map/psum | solution.py:222
  554.4 8.2 %fusion.91 = (f32[768]{0:T(1024)S(1)}, f32[2048]{0:T(1024)S(1)}, f32[2048]{0:T(1024)S(1)}, f32[768]{0:T(1024)S(1)}, f32[2048,768]{1,0:T(8,128)}, /*index=5*/f32[2048,768]{1,0:T(8,128)}) fusion(bf16[2048,768]{1,0:T(8,128)(2,1)} %get-tuple-element.208, f32[2048]{0:T(1024)S(1)} %copy-done.33, f32[2048]{0:T(1024)S(1)} %copy-done.31, ...), kind=kLoop, calls=%fused_computation.130 | loop fusion | flops 17295872 | bytes 18916352 | tf_op jit(solution)/shard_map/reduce_sum | solution.py:282
  562.8 40.8 %all-reduce.8 = (f32[768]{0:T(1024)}, f32[768]{0:T(1024)}, f32[3,192]{1,0:T(4,128)}, f32[3,64]{1,0:T(4,128)}, f32[768]{0:T(1024)}, /*index=5*/f32[768]{0:T(1024)}, f32[768]{0:T(1024)}, f32[768]{0:T(1024)}, f32[768]{0:T(1024)}) all-reduce(f32[768]{0:T(1024)S(1)} %get-tuple-element.148, ...), channel_id=1, replica_groups=mesh['dp'=8,'mp'=4] {'dp'}, use_global_device_ids=true, to_apply=%region_23.24 | all-reduce | flops 6144 | bytes 49152 | tf_op jit(solution)/shard_map/psum | solution.py:304
  603.6 4.6 fusion.98
  608.2 188.8 %all-reduce.20.cloned.1.call-done = (f32[768,3,192]{0,2,1:T(8,128)}, f32[192,768]{1,0:T(8,128)}, f32[768,768]{1,0:T(8,128)}, f32[768,768]{1,0:T(8,128)}) async-done(((f32[768,3,192]{0,2,1:T(8,128)}, f32[192,768]{1,0:T(8,128)}, f32[768,768]{1,0:T(8,128)}, f32[768,768]{1,0:T(8,128)}), (f32[768,3,192]{0,2,1:T(8,128)}, f32[192,768]{1,0:T(8,128)}, f32[768,768]{1,0:T(8,128)}, ...) | async-done | bytes 7077904 | tf_op jit(solution)/shard_map/psum | solution.py:304
  797.0 2.9 copy.118
  (212 shorter events, 55.0 us)
Async XLA Ops:
  7.2 147.2 %copy-start = (bf16[768,768]{1,0:T(8,128)(2,1)S(1)}, bf16[768,768]{1,0:T(8,128)(2,1)}, u32[]{:S(2)}) copy-start(bf16[768,768]{1,0:T(8,128)(2,1)} %param.35) | copy-start | bytes 3538948
  7.2 5.6 copy-start.47
  7.2 5.6 copy-start.54
  7.2 5.6 copy-start.52
  7.2 137.5 %all-reduce.16.cloned.1.call-start = ((), (), s32[]{:S(2)}) async-start(), calls=%async_computation | async-start | bytes 6291456 | tf_op jit(solution)/shard_map/psum | solution.py:208
  7.3 5.6 copy-start.5
  9.8 5.3 copy-start.30
  12.8 2.4 copy-start.32
  12.9 2.3 copy-start.44
  15.6 1.6 copy-start.42
  15.6 2.3 copy-start.41
  17.1 13.9 %copy-start.7 = (f32[2048,1,192]{0,2,1:T(8,128)}, f32[2048,1,192]{0,2,1:T(8,128)S(1)}, u32[]{:S(2)}) copy-start(f32[2048,1,192]{0,2,1:T(8,128)S(1)} %get-tuple-element.240) | copy-start | bytes 4718596
  19.3 13.0 %copy-start.26 = (f32[1,2048]{1,0:T(1,128)}, f32[1,2048]{1,0:T(1,128)S(1)}, u32[]{:S(2)}) copy-start(f32[1,2048]{1,0:T(1,128)S(1)} %get-tuple-element.257) | copy-start | bytes 24580
  32.0 5.0 copy-start.29
  37.1 33.6 %copy-start.25 = (bf16[192,768]{1,0:T(8,128)(2,1)S(1)}, bf16[192,768]{1,0:T(8,128)(2,1)}, u32[]{:S(2)}) copy-start(bf16[192,768]{1,0:T(8,128)(2,1)} %param.29) | copy-start | bytes 884740
  69.6 75.1 %copy-start.43 = (f32[768]{0:T(1024)S(1)}, f32[768]{0:T(1024)}, u32[]{:S(2)}) copy-start(f32[768]{0:T(1024)} %param.30) | copy-start | bytes 9220
  69.8 0.9 copy-start.10
  73.4 174.9 %all-reduce.18.cloned.1.call-start = ((), (), s32[]{:S(2)}) async-start(), calls=%async_computation.1 | async-start | bytes 6291456 | tf_op jit(solution)/shard_map/psum | solution.py:238
  148.6 25.2 %copy-start.3 = (f32[2048,768]{1,0:T(8,128)}, f32[2048,768]{1,0:T(8,128)S(1)}, u32[]{:S(2)}) copy-start(f32[2048,768]{1,0:T(8,128)S(1)} %get-tuple-element.217) | copy-start | bytes 18874372
  148.6 0.9 copy-start.34
  148.6 0.9 copy-start.45
  149.5 2.2 copy-start.51
  151.7 2.6 copy-start.17
  151.7 3.0 copy-start.13
  151.7 3.0 copy-start.46
  154.7 19.1 %copy-start.12 = (f32[2048,768]{1,0:T(8,128)}, f32[2048,768]{1,0:T(8,128)S(1)}, u32[]{:S(2)}) copy-start(f32[2048,768]{1,0:T(8,128)S(1)} %fusion.117) | copy-start | bytes 18874372
  173.9 1.6 copy-start.56
  179.6 374.8 %all-reduce.22.cloned.1.call-start = ((), (), s32[]{:S(2)}) async-start(), calls=%async_computation.3 | async-start | bytes 12582912 | tf_op jit(solution)/shard_map/psum | solution.py:222
  185.1 1.8 copy-start.18
  248.3 6.0 copy-start.9
  248.3 6.0 copy-start.14
  260.1 2.6 copy-start.4
  297.7 4.1 copy-start.2
  366.2 4.1 copy-start.2
  404.4 7.0 copy-start.27
  404.4 7.0 copy-start.28
  404.4 7.0 copy-start.35
  404.4 7.0 copy-start.36
  407.9 12.8 %copy-start.8 = (f32[2048,1,192]{0,2,1:T(8,128)S(1)}, f32[2048,1,192]{0,2,1:T(8,128)}, u32[]{:S(2)}) copy-start(f32[2048,1,192]{0,2,1:T(8,128)} %copy-done.7) | copy-start | bytes 4718596
  420.7 7.7 copy-start.20
  420.7 9.6 %copy-start.53 = (bf16[768,3,192]{0,2,1:T(8,128)(2,1)S(1)}, bf16[768,3,192]{0,2,1:T(8,128)(2,1)}, u32[]{:S(2)}) copy-start(bf16[768,3,192]{0,2,1:T(8,128)(2,1)} %param.26) | copy-start | bytes 2654212
  428.9 1.4 copy-start.23
  434.3 362.6 %all-reduce.20.cloned.1.call-start = ((), (), s32[]{:S(2)}) async-start(), calls=%async_computation.2 | async-start | bytes 14155776 | tf_op jit(solution)/shard_map/psum | solution.py:304
  434.4 7.1 copy-start.15
  434.4 7.1 copy-start.19
  434.4 11.4 %slice-start = ((s8[6291456]{0:T(1024)(128)(4,1)}), s8[4194304]{0:T(1024)(128)(4,1)S(1)}, s32[]{:S(2)}) async-start(s8[6291456]{0:T(1024)(128)(4,1)} %bitcast.237), calls=%async_computation.4 | async-start | bytes 8388608
  441.5 4.3 slice-start.1
  441.5 4.3 copy-start.11
  445.8 2.0 copy-start.6
  445.8 2.9 copy-start.24
  445.8 2.9 copy-start.31
  445.8 2.9 copy-start.33
  445.8 2.9 copy-start.48
  445.8 2.9 copy-start.55
  452.3 1.1 copy-start.16
  554.4 8.4 %copy-start.37 = (f32[768]{0:T(1024)S(1)}, f32[768]{0:T(1024)}, u32[]{:S(2)}) copy-start(f32[768]{0:T(1024)} %get-tuple-element.146) | copy-start | bytes 9220
  554.4 8.4 %copy-start.38 = (f32[768]{0:T(1024)S(1)}, f32[768]{0:T(1024)}, u32[]{:S(2)}) copy-start(f32[768]{0:T(1024)} %get-tuple-element.152) | copy-start | bytes 9220
  554.4 8.4 %copy-start.39 = (f32[768]{0:T(1024)S(1)}, f32[768]{0:T(1024)}, u32[]{:S(2)}) copy-start(f32[768]{0:T(1024)} %get-tuple-element.212) | copy-start | bytes 9220
  554.4 8.4 %copy-start.40 = (f32[768]{0:T(1024)S(1)}, f32[768]{0:T(1024)}, u32[]{:S(2)}) copy-start(f32[768]{0:T(1024)} %get-tuple-element.244) | copy-start | bytes 9220
  554.4 8.4 %copy-start.50 = (f32[768]{0:T(1024)S(1)}, f32[768]{0:T(1024)}, u32[]{:S(2)}) copy-start(f32[768]{0:T(1024)} %get-tuple-element.209) | copy-start | bytes 9220
  554.4 49.2 %copy-start.49 = (f32[768]{0:T(1024)S(1)}, f32[768]{0:T(1024)}, u32[]{:S(2)}) copy-start(f32[768]{0:T(1024)} %param.36) | copy-start | bytes 9220
  797.0 4.9 copy-start.22
  797.0 6.3 copy-start.21
  797.0 7.7 copy-start.1
Sparse Core Ops, SparseCore 0:
  73.5 71.1 all-reduce.15
  179.7 68.5 all-reduce.17
  434.4 119.8 all-reduce.21
  559.8 237.0 all-reduce.19
where the time goes:
time: 821 us; the launch traced here: 811 us
  waiting for transfers between devices  418 us (51%)
  matrix products  138 us (17%)
  local copies, waits for them, and re-layouts  107 us (13%)
  other arithmetic  91.3 us (11%)
  blocking collectives  40.8 us (5%)
  between operations  14.6 us (2%)
    psum x1, waiting for transfers between devices, local(): lax.psum((qkv_weight_grad, qkv_bias_grad, rope_freq_grad, out_weight_grad...  189 us
    psum x1, waiting for transfers between devices, local(): lax.psum(partial_mlp.astype(jnp.bfloat16), 'mp').astype(jnp.float32)  101 us
    psum x1, waiting for transfers between devices, local(): lax.psum(partial_attn.astype(jnp.bfloat16), 'mp').astype(jnp.float32)  71.2 us
    dynamic_update_slice x8, local copies, waits for them, and re-layouts, attend(): context, log_total = lax.map(one_sequence, shaped)  60.7 us
    psum x1, waiting for transfers between devices, local(): lax.psum(partial_norm.astype(jnp.bfloat16), 'mp').astype(jnp.float32)  57.4 us
    psum x1, blocking collectives, local(): lax.psum((qkv_weight_grad, qkv_bias_grad, rope_freq_grad, out_weight_grad...  40.8 us
    dot_general x4, matrix products, one_sequence(): jnp.einsum('qhd,khd->hqk', grad_part, values_seq, preferred_element_type=...  24.1 us
    unnamed x121, local copies, waits for them, and re-layouts  20 us
  transfers between devices with their start and end apart: 4, of which 4 were waited for; matrix products, arithmetic and copies ran while one was open for 5% of the time, Pallas kernels for 0%

commit v1 on v0

v1 whole, which is shorter than its diff:
```python
import functools
import math

import jax
import jax.numpy as jnp
from jax import lax
from jax.experimental import pallas as pl
from jax.experimental.pallas import tpu as pltpu
from jax.sharding import PartitionSpec as P

LEN = 1024
HD = 64
HALF = HD // 2
RB = 256
KB = 256

masked_score = -1e30
epsilon = 1e-06
SCALE = HD ** (-0.5)
SCALE2 = SCALE * math.log2(math.e)
SQRT_HALF = math.sqrt(0.5)
INV_SQRT_2PI = 1.0 / math.sqrt(2.0 * math.pi)

f32 = jnp.float32
bf16 = jnp.bfloat16

NN = (((1,), (0,)), ((), ()))
NT = (((1,), (1,)), ((), ()))
TN = (((0,), (0,)), ((), ()))


def mm(a, b, dims=NN):
    return lax.dot_general(a, b, dims, preferred_element_type=f32)


ANY = pl.BlockSpec(memory_space=pl.ANY)


def ignoring(count, kernel):
    return lambda c_ref, *refs: kernel(c_ref, *refs[count:])


def params(mib):
    return pltpu.CompilerParams(
        dimension_semantics=("arbitrary",), vmem_limit_bytes=mib * 1024 * 1024
    )


def hbm(shape, dtype):
    return pltpu.HBM(shape, dtype)


def stay(*arrays):
    return [pltpu.with_memory_space_constraint(a, pltpu.HBM) for a in arrays]


def cost(flops, nbytes, trans=0):
    return pl.CostEstimate(flops=int(flops), bytes_accessed=int(nbytes), transcendentals=int(trans))


def standardize(values):
    center = jnp.mean(values, axis=-1, keepdims=True)
    centered = values - center
    spread = jnp.mean(centered * centered, axis=-1, keepdims=True)
    inverse = lax.rsqrt(spread + epsilon)
    return centered * inverse, inverse


def column(row):
    n = row.shape[1]
    here = lax.broadcasted_iota(jnp.int32, (n, n), 0) == lax.broadcasted_iota(jnp.int32, (n, n), 1)
    return jnp.sum(jnp.where(here, row, 0.0), axis=1, keepdims=True)


def prepare_kernel(freq_ref, bias_ref, tab_ref, cols_ref):
    heads = freq_ref.shape[0]
    n = heads * HALF
    lane = lax.broadcasted_iota(jnp.int32, (HALF, 128), 1)
    spot = (lane & 31).astype(f32)
    part = lane >> 5
    for h in range(heads):
        freq = column(freq_ref[h : h + 1, :])
        for axis in range(2):
            angle = spot * freq[axis * HALF : (axis + 1) * HALF]
            for k, val in enumerate((jnp.cos(angle), jnp.sin(angle))):
                high = val.astype(bf16).astype(f32)
                rest = val - high
                mid = rest.astype(bf16).astype(f32)
                low = (rest - mid).astype(bf16).astype(f32)
                out = jnp.where(part == 0, high, jnp.where(part == 1, mid, jnp.where(part == 2, low, 0.0)))
                at = (axis * 2 + k) * n + h * HALF
                tab_ref[at : at + HALF, :] = out.astype(bf16)
    width = bias_ref.shape[1]
    for k in range(3):
        for h in range(heads):
            col = column(bias_ref[k : k + 1, h * HD : (h + 1) * HD])
            cols_ref[k * width + h * HD : k * width + (h + 1) * HD, :] = jnp.broadcast_to(col, (HD, 128))


def prepare(freq, bias):
    heads = freq.shape[0]
    return pl.pallas_call(
        prepare_kernel,
        out_shape=[
            jax.ShapeDtypeStruct((4 * heads * HALF, 128), bf16),
            jax.ShapeDtypeStruct((bias.shape[0] * bias.shape[1], 128), f32),
        ],
        name="prepare",
    )(freq, bias)


def lookup(tab_ref, grid_blk):
    n = tab_ref.shape[0] // 4
    rows = grid_blk.shape[1]
    spot = lax.broadcasted_iota(jnp.int32, (128, rows), 0) & 31
    one_r = jnp.where(spot == grid_blk[0:1, :], 1.0, 0.0).astype(bf16)
    one_c = jnp.where(spot == grid_blk[1:2, :], 1.0, 0.0).astype(bf16)
    by_c = mm(tab_ref[0 : 2 * n, :], one_c)
    by_r = mm(tab_ref[2 * n : 4 * n, :], one_r)
    cc, sc = by_c[:n], by_c[n:]
    cr, sr = by_r[:n], by_r[n:]
    return cc * cr - sc * sr, sc * cr + cc * sr


def proj_kernel(c_ref, x_ref, grid_ref, tab_ref, wt_ref, bias_ref, gain_ref, beta_ref, xhat_ref, q_ref, k_ref, v_ref):
    width = q_ref.shape[0]
    xhat, _ = standardize(x_ref[...].astype(f32))
    xhat_ref[...] = xhat.astype(bf16)
    normed = (xhat * gain_ref[...] + beta_ref[...]).astype(bf16)
    mixed = mm(wt_ref[...], normed, NT) + bias_ref[:, 0:1]
    cosine, sine = lookup(tab_ref, grid_ref[...])
    for which, ref in ((0, q_ref), (1, k_ref)):
        for h in range(width // HD):
            at = which * width + h * HD
            a1 = mixed[at : at + HALF]
            a2 = mixed[at + HALF : at + HD]
            c = cosine[h * HALF : (h + 1) * HALF]
            s = sine[h * HALF : (h + 1) * HALF]
            ref[h * HD : h * HD + HALF, :] = (a1 * c - a2 * s).astype(bf16)
            ref[h * HD + HALF : (h + 1) * HD, :] = (a1 * s + a2 * c).astype(bf16)
    v_ref[...] = mixed[2 * width : 3 * width].astype(bf16)


def project(seq, core, patches, grid, tab, wt, bias_cols, gain, beta, wait=()):
    d = patches.shape[1]
    wide = wt.shape[0]
    width = wide // 3
    steps = LEN // RB
    whole = lambda *shape: pl.BlockSpec(shape, lambda i, c: (0,) * len(shape), pipeline_mode=pl.Buffered(1))
    tall = pl.BlockSpec((width, RB), lambda i, c: (0, i))
    return pl.pallas_call(
        ignoring(len(wait), proj_kernel),
        grid_spec=pltpu.PrefetchScalarGridSpec(
            num_scalar_prefetch=1,
            grid=(steps,),
            in_specs=[ANY] * len(wait)
            + [
                pl.BlockSpec((RB, d), lambda i, c: (seq * steps + i, 0)),
                pl.BlockSpec((2, RB), lambda i, c: (0, seq * steps + i)),
                whole(*tab.shape),
                whole(*wt.shape),
                whole(*bias_cols.shape),
                whole(1, d),
                whole(1, d),
            ],
            out_specs=[pl.BlockSpec((RB, d), lambda i, c: (i, 0)), tall, tall, tall],
        ),
        out_shape=[hbm((LEN, d), bf16)] + [jax.ShapeDtypeStruct((width, LEN), bf16)] * 3,
        compiler_params=params(10),
        cost_estimate=cost(2 * LEN * d * wide, 2 * (2 * LEN * d + wide * (d + LEN))),
        name="project",
    )(core, *wait, *stay(patches), grid, tab, wt, bias_cols, gain, beta)


def key_range(ids_all, ids_blk):
    first = jnp.min(ids_blk)
    last = jnp.max(ids_blk)
    start = jnp.sum((ids_all < first).astype(jnp.int32))
    stop = jnp.sum((ids_all <= last).astype(jnp.int32))
    return start // KB, (stop + KB - 1) // KB


def same_image(idc_ref, at, ids_blk):
    ids_k = idc_ref[pl.ds(at, KB), :]
    ids_k = jnp.concatenate([ids_k] * (ids_blk.shape[1] // 128), axis=1)
    return ids_k == ids_blk


def rows_of(ref, h):
    return ref[h * HD : (h + 1) * HD, :]


def attend_kernel(c_ref, q_ref, k_ref, v_ref, idr_ref, idq_ref, idc_ref,
                  send_ref, keep_ref, ctx_ref, lse_ref, keys, scores, acc):
    step = pl.program_id(0)
    heads = q_ref.shape[0] // HD
    half = pl.num_programs(0) // 2

    @pl.when(step == 0)
    def _():
        for h in range(heads):
            keys[h] = jnp.transpose(rows_of(k_ref, h))

    ids_q = idq_ref[...]
    lo, hi = key_range(idr_ref[...], ids_q)

    def first_pass(kb, tops):
        at = pl.multiple_of(kb * KB, KB)
        same = same_image(idc_ref, at, ids_q)
        new = []
        for h in range(heads):
            s = mm(keys[h, pl.ds(at, KB), :], rows_of(q_ref, h))
            s = jnp.where(same, s, masked_score)
            scores[h, pl.ds(at, KB), :] = s
            new.append(jnp.maximum(tops[h], jnp.max(s, axis=0, keepdims=True)))
        return tuple(new)

    tops = lax.fori_loop(lo, hi, first_pass, tuple(jnp.full((1, RB), masked_score, f32) for _ in range(heads)))
    tops = tuple(top * SCALE2 for top in tops)
    acc[...] = jnp.zeros_like(acc)

    def second_pass(kb, totals):
        at = pl.multiple_of(kb * KB, KB)
        new = []
        for h in range(heads):
            p = jnp.exp2(scores[h, pl.ds(at, KB), :] * SCALE2 - tops[h])
            new.append(totals[h] + jnp.sum(p, axis=0, keepdims=True))
            acc[h * HD : (h + 1) * HD, :] += mm(v_ref[h * HD : (h + 1) * HD, pl.ds(at, KB)], p.astype(bf16))
        return tuple(new)

    totals = lax.fori_loop(lo, hi, second_pass, tuple(jnp.zeros((1, RB), f32) for _ in range(heads)))
    lse = jnp.zeros((8, RB), f32)
    row = lax.broadcasted_iota(jnp.int32, (8, RB), 0)
    for h in range(heads):
        ctx_ref[h * HD : (h + 1) * HD, :] = acc[h * HD : (h + 1) * HD, :] * (1.0 / totals[h])
        lse = jnp.where(row == h, tops[h] + jnp.log2(totals[h]), lse)
    lse_ref[...] = lse
    partial = ctx_ref[...].astype(bf16)

    @pl.when(step < half)
    def _():
        send_ref[...] = partial

    @pl.when(step >= half)
    def _():
        keep_ref[...] = partial


def attend(seq, core, q, k, v, ids_rows, ids_cols, wait=()):
    width = q.shape[0]
    steps = LEN // RB
    half = steps // 2
    heads = width // HD
    blk = lambda i, c: lax.rem(i + half * (1 - c[0]), steps)
    whole = lambda *shape: pl.BlockSpec(shape, lambda i, c: (0,) * len(shape), pipeline_mode=pl.Buffered(1))
    return pl.pallas_call(
        ignoring(len(wait), attend_kernel),
        grid_spec=pltpu.PrefetchScalarGridSpec(
            num_scalar_prefetch=1,
            grid=(steps,),
            in_specs=[ANY] * len(wait)
            + [
                pl.BlockSpec((width, RB), lambda i, c: (0, blk(i, c))),
                whole(width, LEN),
                whole(width, LEN),
                pl.BlockSpec((None, 1, LEN), lambda i, c: (seq, 0, 0)),
                pl.BlockSpec((None, 1, RB), lambda i, c: (seq, 0, blk(i, c))),
                pl.BlockSpec((LEN, 128), lambda i, c: (seq, 0)),
            ],
            out_specs=[
                pl.BlockSpec((width, RB), lambda i, c: (0, jnp.minimum(i, half - 1))),
                pl.BlockSpec((width, RB), lambda i, c: (0, jnp.maximum(i - half, 0))),
                pl.BlockSpec((width, RB), lambda i, c: (0, blk(i, c))),
                pl.BlockSpec((8, RB), lambda i, c: (0, blk(i, c))),
            ],
            scratch_shapes=[
                pltpu.VMEM((heads, LEN, HD), bf16),
                pltpu.VMEM((heads, LEN, RB), f32),
                pltpu.VMEM((width, RB), f32),
            ],
        ),
        out_shape=[
            jax.ShapeDtypeStruct((width, LEN // 2), bf16),
            jax.ShapeDtypeStruct((width, LEN // 2), bf16),
            hbm((width, LEN), f32),
            hbm((8, LEN), f32),
        ],
        compiler_params=params(10),
        cost_estimate=cost(8 * LEN * LEN * width, 12 * LEN * width, heads * LEN * LEN),
        name="attend",
    )(core, *wait, q, k, v, ids_rows, ids_rows, ids_cols)


def norm_two_kernel(c_ref, x_ref, *refs):
    groups = (len(refs) - 5) // 2
    ctx_refs, wo_refs = refs[:groups], refs[groups : 2 * groups]
    bias_ref, gain_ref, beta_ref, resid_ref, normed_ref = refs[2 * groups :]
    attn = bias_ref[...]
    for ctx_ref, wo_ref in zip(ctx_refs, wo_refs):
        attn = attn + mm(ctx_ref[...], wo_ref[...], TN).astype(bf16).astype(f32)
    resid = x_ref[...].astype(f32) + attn
    resid_ref[...] = resid
    xhat, _ = standardize(resid)
    normed_ref[...] = (xhat * gain_ref[...] + beta_ref[...]).astype(bf16)


def norm_two(seq, core, patches, ctxs, wos, bias, gain, beta, wait=()):
    width, rows = ctxs[0].shape
    d = patches.shape[1]
    steps = rows // RB
    blk = pl.BlockSpec((RB, d), lambda i, c: (i, 0))
    whole = lambda *shape: pl.BlockSpec(shape, lambda i, c: (0,) * len(shape), pipeline_mode=pl.Buffered(1))
    return pl.pallas_call(
        ignoring(len(wait), norm_two_kernel),
        grid_spec=pltpu.PrefetchScalarGridSpec(
            num_scalar_prefetch=1,
            grid=(steps,),
            in_specs=[ANY] * len(wait)
            + [pl.BlockSpec((RB, d), lambda i, c: ((2 * seq + c[0]) * steps + i, 0))]
            + [pl.BlockSpec((width, RB), lambda i, c: (0, i))] * len(ctxs)
            + [whole(width, d)] * len(wos)
            + [whole(1, d)] * 3,
            out_specs=[blk, blk],
        ),
        out_shape=[hbm((rows, d), f32), jax.ShapeDtypeStruct((rows, d), bf16)],
        compiler_params=params(10),
        cost_estimate=cost(2 * len(ctxs) * rows * d * width, 12 * rows * d),
        name="norm_two",
    )(core, *wait, *stay(patches), *ctxs, *wos, bias, gain, beta)


def store_halves(mine, outs, sums):
    count = outs[0].shape[0]
    for out, half in zip(outs, (1 - mine, mine)):
        for k in range(count):
            at = 0
            for acc in sums:
                rows = acc.shape[0] // (2 * count)
                spot = pl.ds(pl.multiple_of((half * count + k) * rows, 8), rows)
                out[k, at : at + rows, :] = acc[spot, :].astype(bf16)
                at += rows


def feed_kernel(first, last, c_ref, *refs):
    refs = list(refs)
    own_ref, other_ref, og_ref, up_ref, upb_ref, down_ref = refs[:6]
    refs = refs[6:]
    if not first:
        small0_ref, up0_ref, down0_ref = refs[:3]
        refs = refs[3:]
    mlp_send, mlp_keep, n2_send, n2_keep, small_out = refs[:5]
    outs = refs[5:-4]
    up_acc, down_acc, up_sum, down_sum = refs[-4:]
    step = pl.program_id(0)
    steps = pl.num_programs(0)
    half = steps // 2

    @pl.when(step == 0)
    def _():
        if first:
            up_acc[...] = jnp.zeros_like(up_acc)
            down_acc[...] = jnp.zeros_like(down_acc)
            up_sum[...] = jnp.zeros_like(up_sum)
            down_sum[...] = jnp.zeros_like(down_sum)
        else:
            up_acc[...] = up0_ref[...]
            down_acc[...] = down0_ref[...]
            up_sum[...] = small0_ref[0:1, :]
            down_sum[...] = small0_ref[1:2, :]

    normed = jnp.where(step < half, other_ref[...], own_ref[...])
    og = og_ref[...]
    pre = mm(normed, up_ref[...]) + upb_ref[...]
    phi_cap = 0.5 * (1.0 + lax.erf(pre * SQRT_HALF))
    hidden = (pre * phi_cap).astype(bf16)
    mlp = mm(hidden, down_ref[...]).astype(bf16)
    slope = phi_cap + pre * (jnp.exp(-0.5 * pre * pre) * INV_SQRT_2PI)
    grad = mm(og, down_ref[...], NT)
    pre_grad = (grad * slope).astype(bf16)
    n2 = mm(pre_grad, up_ref[...], NT).astype(bf16)
    down_acc[...] += mm(hidden, og, TN)
    up_acc[...] += mm(normed, pre_grad, TN)
    up_sum[...] += jnp.sum(pre_grad.astype(f32), axis=0, keepdims=True)
    down_sum[...] += jnp.sum(og.astype(f32), axis=0, keepdims=True)

    @pl.when(step < half)
    def _():
        mlp_send[...] = mlp
        n2_send[...] = n2

    @pl.when(step >= half)
    def _():
        mlp_keep[...] = mlp
        n2_keep[...] = n2

    @pl.when(step == steps - 1)
    def _():
        if last:
            store_halves(c_ref[1], outs, (up_acc, down_acc))
        else:
            outs[0][...] = up_acc[...]
            outs[1][...] = down_acc[...]
        small_out[0:1, :] = up_sum[...]
        small_out[1:2, :] = down_sum[...]
        small_out[2:8, :] = jnp.zeros((6, up_sum.shape[1]), f32)


def feed(seq, core, own, other, out_grad, up, up_bias, down, before=None, last=0, wait=()):
    d, units = up.shape
    steps = LEN // RB
    half = steps // 2
    first = before is None
    whole = lambda *shape: pl.BlockSpec(shape, lambda i, c: (0,) * len(shape), pipeline_mode=pl.Buffered(1))
    low = pl.BlockSpec((RB, d), lambda i, c: (jnp.minimum(i, half - 1), 0))
    high = pl.BlockSpec((RB, d), lambda i, c: (jnp.maximum(i - half, 0), 0))
    blk = lambda i, c: seq * steps + lax.rem(i + half * (1 - c[0]), steps)
    in_specs = [ANY] * len(wait) + [
        high, low,
        pl.BlockSpec((RB, d), lambda i, c: (blk(i, c), 0)),
        whole(d, units), whole(1, units), whole(units, d),
    ]
    args = [core, *wait, own, other, *stay(out_grad), up, up_bias, down]
    if not first:
        in_specs += [whole(8, d), whole(d, units), whole(units, d)]
        args += list(before)
    if last:
        grads = [(last, (d + units) // (2 * last), d)] * 2
        kind = bf16
    else:
        grads = [(d, units), (units, d)]
        kind = f32
    rows = jax.ShapeDtypeStruct((LEN // 2, d), bf16)
    return pl.pallas_call(
        ignoring(len(wait), functools.partial(feed_kernel, first, last)),
        grid_spec=pltpu.PrefetchScalarGridSpec(
            num_scalar_prefetch=1,
            grid=(steps,),
            in_specs=in_specs,
            out_specs=[low, high, low, high, whole(8, d)] + [whole(*g) for g in grads],
            scratch_shapes=[
                pltpu.VMEM((d, units), f32),
                pltpu.VMEM((units, d), f32),
                pltpu.VMEM((1, units), f32),
                pltpu.VMEM((1, d), f32),
            ],
        ),
        out_shape=[hbm(rows.shape, bf16), hbm(rows.shape, bf16), rows, rows, hbm((8, d), f32)]
        + [hbm(g, kind) for g in grads],
        compiler_params=params(28),
        cost_estimate=cost(12 * LEN * d * units, 2 * LEN * d * 4 + 12 * d * units, 2 * LEN * units),
        name="feed",
    )(*args)


def norm_two_back_kernel(first, c_ref, *refs):
    refs = list(refs)
    mine_ref, theirs_ref, resid_ref, og_ref, gain_ref = refs[:5]
    refs = refs[5:]
    if not first:
        small0_ref = refs[0]
        refs = refs[1:]
    rgrad_ref, branch_ref, small_ref = refs
    step = pl.program_id(0)

    @pl.when(step == 0)
    def _():
        if first:
            small_ref[...] = jnp.zeros_like(small_ref)
        else:
            small_ref[...] = small0_ref[...]

    grad = mine_ref[...].astype(f32) + theirs_ref[...].astype(f32)
    xhat, inverse = standardize(resid_ref[...])
    e = grad * gain_ref[...]
    back = inverse * (
        e - jnp.mean(e, axis=-1, keepdims=True) - xhat * jnp.mean(e * xhat, axis=-1, keepdims=True)
    )
    rgrad = og_ref[...].astype(f32) + back
    rgrad_ref[...] = rgrad
    branch = rgrad.astype(bf16)
    branch_ref[...] = branch
    small_ref[0:1, :] += jnp.sum(grad * xhat, axis=0, keepdims=True)
    small_ref[1:2, :] += jnp.sum(grad, axis=0, keepdims=True)
    small_ref[2:3, :] += jnp.sum(branch.astype(f32), axis=0, keepdims=True)


def norm_two_back(seq, core, mine, theirs, resid, out_grad, gain, before=None, wait=()):
    rows, d = mine.shape
    steps = rows // RB
    first = before is None
    blk = pl.BlockSpec((RB, d), lambda i, c: (i, 0))
    vec = pl.BlockSpec((1, d), lambda i, c: (0, 0))
    small = pl.BlockSpec((8, d), lambda i, c: (0, 0))
    in_specs = [ANY] * len(wait) + [blk, blk, blk, pl.BlockSpec((RB, d), lambda i, c: ((2 * seq + c[0]) * steps + i, 0)), vec]
    args = [core, *wait, mine, theirs, *stay(resid, out_grad), gain]
    if not first:
        in_specs.append(small)
        args.append(before)
    return pl.pallas_call(
        ignoring(len(wait), functools.partial(norm_two_back_kernel, first)),
        grid_spec=pltpu.PrefetchScalarGridSpec(
            num_scalar_prefetch=1, grid=(steps,), in_specs=in_specs, out_specs=[blk, blk, small]
        ),
        out_shape=[
            hbm((rows, d), f32),
            jax.ShapeDtypeStruct((rows, d), bf16),
            hbm((8, d), f32),
        ],
        compiler_params=params(12),
        cost_estimate=cost(20 * rows * d, 16 * rows * d),
        name="norm_two_back",
    )(*args)


def attend_back_kernel(first, pieces, c_ref, *refs):
    refs = list(refs)
    (own_ref, other_ref, q_ref, k_ref, v_ref, ctx_ref, lse_ref, idr_ref, idq_ref, idc_ref, wo_ref,
     wt_ref, tab_ref, grid_ref, xhat_ref, gain_ref, beta_ref) = refs[:17]
    refs = refs[17:]
    if not first:
        dwt0_ref, dwo0_ref, row0_ref, col0_ref, rope0_ref = refs[:5]
        refs = refs[5:]
    if pieces:
        small_two_ref, small_feed_ref, send_ref, keep_ref, small_ref = refs[:5]
        outs = refs[5:7]
        bucket = refs[7]
        refs = refs[8:]
        keys, vals, dq, dk, dv, dwt_acc, dwo_acc, row_acc, col_acc, rope_acc = refs
    else:
        send_ref, keep_ref, dwt_acc, dwo_acc, row_acc, col_acc, rope_acc = refs[:7]
        refs = refs[7:]
        keys, vals, dq, dk, dv = refs
    step = pl.program_id(0)
    steps = pl.num_programs(0) // 2
    half = steps // 2
    width = q_ref.shape[0]
    heads = width // HD
    c = c_ref[0]
    blk = lax.rem(step + half * (1 - c), steps)
    here = pl.ds(pl.multiple_of(blk * RB, RB), RB)

    @pl.when(step == 0)
    def _():
        for h in range(heads):
            keys[h] = jnp.transpose(rows_of(k_ref, h))
            vals[h] = jnp.transpose(rows_of(v_ref, h))
        dq[...] = jnp.zeros_like(dq)
        dk[...] = jnp.zeros_like(dk)
        dv[...] = jnp.zeros_like(dv)
        if first:
            dwt_acc[...] = jnp.zeros_like(dwt_acc)
            dwo_acc[...] = jnp.zeros_like(dwo_acc)
            row_acc[...] = jnp.zeros_like(row_acc)
            col_acc[...] = jnp.zeros_like(col_acc)
            rope_acc[...] = jnp.zeros_like(rope_acc)
        else:
            dwt_acc[...] = dwt0_ref[...]
            dwo_acc[...] = dwo0_ref[...]
            row_acc[...] = row0_ref[...]
            col_acc[...] = col0_ref[...]
            rope_acc[...] = rope0_ref[...]

    @pl.when(step < steps)
    def _():
        branch = jnp.where(step < half, other_ref[...], own_ref[...])
        ctx = ctx_ref[:, here]
        dctx = mm(wo_ref[...], branch, NT).astype(bf16)
        dwo_acc[...] += mm(ctx.astype(bf16), branch)
        prod = dctx.astype(f32) * ctx
        lse = lse_ref[:, here]
        ids_q = idq_ref[...]
        lo, hi = key_range(idr_ref[...], ids_q)
        parts = []
        for h in range(heads):
            sl = slice(h * HD, (h + 1) * HD)
            parts.append((q_ref[sl, here], dctx[sl], jnp.sum(prod[sl], axis=0, keepdims=True), lse[h : h + 1]))

        def body(kb, carry):
            at = pl.multiple_of(kb * KB, KB)
            there = pl.ds(at, KB)
            same = same_image(idc_ref, at, ids_q)
            for h in range(heads):
                sl = slice(h * HD, (h + 1) * HD)
                q_h, do_h, delta, lse_h = parts[h]
                s = mm(keys[h, there, :], q_h)
                p = jnp.exp2(jnp.where(same, s * SCALE2 - lse_h, masked_score))
                dp = mm(vals[h, there, :], do_h)
                ds = (p * (dp - delta)).astype(bf16)
                dq[sl, here] += mm(k_ref[sl, there], ds)
                dk[sl, there] += mm(q_h, ds, NT)
                dv[sl, there] += mm(do_h, p.astype(bf16), NT)
            return carry

        lax.fori_loop(lo, hi, body, 0)

    @pl.when(step >= steps)
    def _():
        place = grid_ref[...]
        cosine, sine = lookup(tab_ref, place)
        pieces = []
        angle = [None] * heads
        for turned, grads in ((q_ref, dq), (k_ref, dk)):
            for h in range(heads):
                b = grads[h * HD : (h + 1) * HD, here] * SCALE
                a = turned[h * HD : (h + 1) * HD, here].astype(f32)
                b1, b2 = b[:HALF], b[HALF:]
                co = cosine[h * HALF : (h + 1) * HALF]
                si = sine[h * HALF : (h + 1) * HALF]
                pieces.append((b1 * co + b2 * si).astype(bf16))
                pieces.append((b2 * co - b1 * si).astype(bf16))
                term = b2 * a[:HALF] - b1 * a[HALF:]
                angle[h] = term if angle[h] is None else angle[h] + term
        pieces.append(dv[:, here].astype(bf16))
        mixed_grad = jnp.concatenate(pieces, axis=0)
        angle = jnp.concatenate(angle, axis=0)
        rope_acc[...] += lax.dot_general(
            place.astype(f32), angle, NT, precision=lax.Precision.HIGHEST, preferred_element_type=f32
        )
        row_acc[...] += mm(jnp.ones((8, RB), bf16), mixed_grad, NT)
        col_acc[...] += mm(mixed_grad, jnp.ones((RB, 128), bf16))
        dwt_acc[...] += mm(mixed_grad, xhat_ref[...])
        partial = mm(mixed_grad, wt_ref[...], TN).astype(bf16)

        @pl.when(step < steps + half)
        def _():
            send_ref[...] = partial

        @pl.when(step >= steps + half)
        def _():
            keep_ref[...] = partial

    if pieces:
        @pl.when(step == 2 * steps - 1)
        def _():
            raw = dwt_acc[...]
            col = col_acc[:, 0:1]
            wt = wt_ref[...].astype(f32)
            bucket[...] = raw * gain_ref[...] + col * beta_ref[...]
            store_halves(c_ref[1], outs, (bucket, dwo_acc))
            small_ref[0:1, :] = jnp.sum(wt * raw, axis=0, keepdims=True)
            small_ref[1:2, :] = jnp.sum(wt * col, axis=0, keepdims=True)
            small_ref[2:5, :] = 0.5 * small_two_ref[0:3, :]
            small_ref[5:7, :] = small_feed_ref[0:2, :]
            small_ref[7:8, :] = jnp.concatenate(
                [row_acc[0:1, :], rope_acc[1:2, :], rope_acc[0:1, :]], axis=1
            )


def attend_back(seq, core, own, other, q, k, v, ctx, lse, ids_rows, ids_cols, wo, wt, tab, grid, xhat,
                gain, beta, before=None, pieces=0, small_two=None, small_feed=None, wait=()):
    width, d = wo.shape
    heads = width // HD
    steps = LEN // RB
    half = steps // 2
    first = before is None
    whole = lambda *shape: pl.BlockSpec(shape, lambda i, c: (0,) * len(shape), pipeline_mode=pl.Buffered(1))
    blk = lambda i, c: lax.rem(i + half * (1 - c[0]), steps)
    in_specs = [ANY] * len(wait) + [
        pl.BlockSpec((RB, d), lambda i, c: (jnp.clip(i - half, 0, half - 1), 0)),
        pl.BlockSpec((RB, d), lambda i, c: (jnp.minimum(i, half - 1), 0)),
        whole(width, LEN), whole(width, LEN), whole(width, LEN), whole(width, LEN), whole(8, LEN),
        pl.BlockSpec((None, 1, LEN), lambda i, c: (seq, 0, 0)),
        pl.BlockSpec((None, 1, RB), lambda i, c: (seq, 0, blk(i, c))),
        pl.BlockSpec((LEN, 128), lambda i, c: (seq, 0)),
        whole(width, d), whole(3 * width, d), whole(*tab.shape),
        pl.BlockSpec((2, RB), lambda i, c: (0, seq * steps + blk(i, c))),
        pl.BlockSpec((RB, d), lambda i, c: (jnp.where(i < steps, blk(0, c), blk(i, c)), 0)),
        whole(1, d), whole(1, d),
    ]
    args = [core, *wait, own, other, q, k, v, ctx, lse, ids_rows, ids_rows, ids_cols, wo, wt, tab, grid, xhat, gain, beta]
    sums = [(3 * width, d), (width, d), (8, 3 * width), (3 * width, 128), (2, heads * HALF)]
    if not first:
        in_specs += [whole(*s) for s in sums]
        args += list(before)
    if pieces:
        in_specs += [whole(8, d)] * 2
        args += [small_two, small_feed]
    out_specs = [
        pl.BlockSpec((RB, d), lambda i, c: (jnp.clip(i - steps, 0, half - 1), 0)),
        pl.BlockSpec((RB, d), lambda i, c: (jnp.clip(i - steps - half, 0, half - 1), 0)),
    ]
    out_shape = [jax.ShapeDtypeStruct((LEN // 2, d), bf16)] * 2
    scratch = [
        pltpu.VMEM((heads, LEN, HD), bf16),
        pltpu.VMEM((heads, LEN, HD), bf16),
        pltpu.VMEM((width, LEN), f32),
        pltpu.VMEM((width, LEN), f32),
        pltpu.VMEM((width, LEN), f32),
    ]
    if pieces:
        cut = (pieces, 4 * width // (2 * pieces), d)
        out_specs += [whole(8, d), whole(*cut), whole(*cut)]
        out_shape += [hbm((8, d), f32), hbm(cut, bf16), hbm(cut, bf16)]
        scratch = [pltpu.VMEM((3 * width, d), f32)] + scratch + [pltpu.VMEM(s, f32) for s in sums]
    else:
        out_specs += [whole(*s) for s in sums]
        out_shape += [hbm(s, f32) for s in sums]
    return pl.pallas_call(
        ignoring(len(wait), functools.partial(attend_back_kernel, first, pieces)),
        grid_spec=pltpu.PrefetchScalarGridSpec(
            num_scalar_prefetch=1, grid=(2 * steps,), in_specs=in_specs, out_specs=out_specs, scratch_shapes=scratch
        ),
        out_shape=out_shape,
        compiler_params=params(28),
        cost_estimate=cost(
            20 * LEN * LEN * width + 20 * LEN * d * width, 2 * LEN * (6 * width + 3 * d) + 16 * d * width,
            heads * LEN * LEN,
        ),
        name="attend_back",
    )(*args)


def norm_one_back_kernel(m_ref, mine_ref, theirs_ref, x_ref, rg0_ref, rg1_ref, gain_ref, out_ref):
    f = (mine_ref[...].astype(f32) + theirs_ref[...].astype(f32)) * gain_ref[...]
    xhat, inverse = standardize(x_ref[...].astype(f32))
    back = inverse * (
        f - jnp.mean(f, axis=-1, keepdims=True) - xhat * jnp.mean(f * xhat, axis=-1, keepdims=True)
    )
    rgrad = jnp.where(m_ref[0] < 2, rg0_ref[...], rg1_ref[...])
    out_ref[...] = (rgrad + back).astype(bf16)


def norm_one_back(place, mine, theirs, patches, rg0, rg1, gain):
    rows, d = mine.shape
    steps = rows // RB
    blk = pl.BlockSpec((RB, d), lambda i, m: (i, 0))
    return pl.pallas_call(
        norm_one_back_kernel,
        grid_spec=pltpu.PrefetchScalarGridSpec(
            num_scalar_prefetch=1,
            grid=(steps,),
            in_specs=[
                blk, blk, pl.BlockSpec((RB, d), lambda i, m: (m[0] * steps + i, 0)), blk, blk,
                pl.BlockSpec((1, d), lambda i, m: (0, 0)),
            ],
            out_specs=blk,
        ),
        out_shape=jax.ShapeDtypeStruct((rows, d), bf16),
        compiler_params=params(12),
        cost_estimate=cost(20 * rows * d, 16 * rows * d),
        name="norm_one_back",
    )(place, mine, theirs, *stay(patches, rg0, rg1), gain)


CORE_SWAP = [(i, i ^ 1) for i in range(4)]
CHIP_SWAP = [(i, i ^ 2) for i in range(4)]


def core_swap(value):
    return lax.ppermute(value, "mp", CORE_SWAP)


def chip_swap(value):
    return lax.ppermute(value, "mp", CHIP_SWAP)


def after(value, *events):
    return lax.optimization_barrier((value, *events))[0]


def add_low(a, b):
    return (a.astype(f32) + b.astype(f32)).astype(bf16)


def add_kernel(c_ref, a_ref, b_ref, out_ref):
    out_ref[...] = (a_ref[...].astype(f32) + b_ref[...].astype(f32)).astype(bf16)


def full(shape):
    return pl.BlockSpec(shape, lambda i, c: (0,) * len(shape))


def add_parts(core, a, b, wait=()):
    return pl.pallas_call(
        ignoring(len(wait), add_kernel),
        grid_spec=pltpu.PrefetchScalarGridSpec(
            num_scalar_prefetch=1, grid=(1,), in_specs=[ANY] * len(wait) + [full(a.shape)] * 2, out_specs=full(a.shape),
        ),
        out_shape=jax.ShapeDtypeStruct(a.shape, bf16),
        compiler_params=params(12),
        cost_estimate=cost(a.size, 6 * a.size),
        name="add_parts",
    )(core, *wait, a, b)


def sum_parts_kernel(c_ref, parts_ref, *refs):
    out_ref = refs[-1]
    total = parts_ref[0].astype(f32)
    for k in range(1, parts_ref.shape[0]):
        total = total + parts_ref[k].astype(f32)
    rows = total.shape[0]
    total = total.astype(bf16)
    for k in range(out_ref.shape[0]):
        out_ref[k, 0:rows, :] = total
    if len(refs) > 1:
        small = refs[0][...]
        high = small.astype(bf16)
        low = (small - high.astype(f32)).astype(bf16)
        for k in range(out_ref.shape[0]):
            out_ref[k, rows : rows + 8, :] = high
            out_ref[k, rows + 8 : rows + 16, :] = low


def sum_parts(core, parts, small=None, copies=None, wait=()):
    count, rows, d = parts.shape
    extra = () if small is None else (small,)
    out = (copies or count, rows + 16 * len(extra), d)
    return pl.pallas_call(
        ignoring(len(wait), sum_parts_kernel),
        grid_spec=pltpu.PrefetchScalarGridSpec(
            num_scalar_prefetch=1, grid=(1,),
            in_specs=[ANY] * len(wait) + [full(parts.shape)] + [full(e.shape) for e in extra],
            out_specs=full(out),
        ),
        out_shape=jax.ShapeDtypeStruct(out, bf16),
        compiler_params=params(12),
        cost_estimate=cost(count * rows * d, 4 * count * rows * d),
        name="sum_parts",
    )(core, *wait, parts, *extra)


def place_parts_kernel(with_small, c_ref, mine_ref, theirs_ref, *refs):
    outs = refs[: len(refs) - with_small]
    count = mine_ref.shape[0]
    small = None
    for ref, half in ((mine_ref, c_ref[1]), (theirs_ref, 1 - c_ref[1])):
        for k in range(count):
            at = 0
            for out in outs:
                rows = out.shape[0] // (2 * count)
                spot = pl.ds(pl.multiple_of((half * count + k) * rows, 8), rows)
                out[spot, :] = ref[k, at : at + rows, :].astype(f32)
                at += rows
            if with_small:
                part = ref[k, at : at + 8, :].astype(f32) + ref[k, at + 8 : at + 16, :].astype(f32)
                small = part if small is None else small + part
    if with_small:
        refs[-1][...] = small


def place_parts(core, mine, theirs, splits, with_small=False):
    d = mine.shape[2]
    shapes = [(rows, d) for rows in splits] + [(8, d)] * with_small
    return pl.pallas_call(
        functools.partial(place_parts_kernel, with_small),
        grid_spec=pltpu.PrefetchScalarGridSpec(
            num_scalar_prefetch=1, grid=(1,), in_specs=[full(mine.shape)] * 2, out_specs=[full(t) for t in shapes],
        ),
        out_shape=[jax.ShapeDtypeStruct(t, f32) for t in shapes],
        compiler_params=params(20),
        cost_estimate=cost(sum(splits) * d, 6 * sum(splits) * d),
        name="place_parts",
    )(core, mine, theirs)


def place_all_kernel(parts_ref, *outs):
    count = parts_ref.shape[0]
    for k in range(count):
        piece = (k % 2) * (count // 2) + k // 2
        at = 0
        for out in outs:
            rows = out.shape[0] // count
            out[piece * rows : (piece + 1) * rows, :] = parts_ref[k, at : at + rows, :].astype(f32)
            at += rows


def place_all(parts, splits):
    d = parts.shape[2]
    return pl.pallas_call(
        place_all_kernel,
        out_shape=[jax.ShapeDtypeStruct((rows, d), f32) for rows in splits],
        compiler_params=pltpu.CompilerParams(vmem_limit_bytes=20 * 1024 * 1024),
        cost_estimate=cost(sum(splits) * d, 6 * sum(splits) * d),
        name="place_all",
    )(parts)


def half_swap(value):
    return lax.ppermute(value, "dp", [(i, i ^ 1) for i in range(lax.axis_size("dp"))])


def quarter_trade(parts):
    return lax.all_to_all(parts, "dp", 0, 0, axis_index_groups=[[0, 2, 4, 6], [1, 3, 5, 7]])


def hold(values, *events):
    return list(lax.optimization_barrier((*values, *events))[: len(values)])


def local(patches, image_ids, patch_grid, first_norm_gain, first_norm_bias, qkv_weight, qkv_bias, rope_freq,
          out_weight, out_bias, second_norm_gain, second_norm_bias, up_weight, up_bias, down_weight, down_bias,
          out_grad):
    all_rows, d = patches.shape
    seqs = all_rows // LEN
    assert lax.axis_size("mp") == 4 and seqs == 2
    devices = lax.axis_size("dp")
    tree = devices == 8
    pieces = 4 if tree else 1
    heads = rope_freq.shape[0]
    width = heads * HD
    units = up_weight.shape[1]
    place = lax.axis_index("mp").astype(jnp.int32)
    half = lax.axis_index("dp").astype(jnp.int32) % 2 if tree else jnp.int32(0)
    core = jnp.stack([place % 2, half])
    place_arr = place.reshape(1)
    far = place >= 2
    row = lambda v: v.reshape(1, -1)

    tab, bias_cols = prepare(rope_freq, qkv_bias)
    wt = qkv_weight.transpose(1, 2, 0).reshape(3 * width, d)
    ids_rows = image_ids.reshape(seqs, 1, LEN)
    ids_cols = jnp.broadcast_to(image_ids[:, None], (all_rows, 128))
    gain1, beta1 = row(first_norm_gain), row(first_norm_bias)
    gain2, beta2 = row(second_norm_gain), row(second_norm_bias)

    wo_core = core_swap(out_weight)
    proj_args = (patches, patch_grid, tab, wt, bias_cols, gain1, beta1)
    made0 = project(0, core, *proj_args)
    send0, keep0, ctx0, lse0 = attend(0, core, *made0[1:], ids_rows, ids_cols)
    core0, far_keep0 = core_swap(send0), chip_swap(keep0)
    made1 = project(1, core, *proj_args, wait=[keep0, wo_core])
    far_core0, wo_far = chip_swap(core0), chip_swap(out_weight)
    send1, keep1, ctx1, lse1 = attend(1, core, *made1[1:], ids_rows, ids_cols, wait=[core0, far_keep0])
    core1, far_keep1 = core_swap(send1), chip_swap(keep1)
    wos = [out_weight, wo_core, wo_far, core_swap(wo_far)]
    norm_args = (row(out_bias), gain2, beta2)
    resid0, normed0 = norm_two(
        0, core, patches, [keep0, core0, far_keep0, far_core0], wos, *norm_args, wait=[keep1]
    )
    far_core1 = chip_swap(core1)
    feed_args = (out_grad, up_weight, row(up_bias), down_weight)
    mlp_send0, mlp_keep0, n2_send0, n2_keep0, *sums = feed(
        0, core, normed0, core_swap(normed0), *feed_args, wait=[core1, far_keep1]
    )
    n20 = add_low(n2_keep0, core_swap(n2_send0))
    resid1, normed1 = norm_two(
        1, core, patches, [keep1, core1, far_keep1, far_core1], wos, *norm_args, wait=[n2_keep0]
    )
    n2_far0 = chip_swap(n20)
    mlp_send1, mlp_keep1, n2_send1, n2_keep1, small_feed, feed_send, feed_keep = feed(
        1, core, normed1, core_swap(normed1), *feed_args, before=sums, last=pieces, wait=[n20]
    )
    if tree:
        feed_got = half_swap(feed_send)
    n21 = add_low(n2_keep1, core_swap(n2_send1))
    mlp0 = add_low(mlp_keep0, core_swap(mlp_send0))
    mlp1 = add_low(mlp_keep1, core_swap(mlp_send1))
    mlp_away, mlp_mine = jnp.where(far, mlp0, mlp1), jnp.where(far, mlp1, mlp0)
    rgrad0, branch0, small_two = norm_two_back(
        0, core, n20, n2_far0, resid0, out_grad, gain2, wait=[n2_keep1]
    )
    n2_far1 = chip_swap(n21)
    shared_args = (ids_rows, ids_cols, out_weight, wt, tab, patch_grid)
    n1_send0, n1_keep0, *sums = attend_back(
        0, core, branch0, core_swap(branch0), *made0[1:], ctx0, lse0, *shared_args, made0[0], gain1, beta1,
        wait=[n21],
    )
    n1_core0 = core_swap(n1_send0)
    after_first = [n1_keep0]
    if tree:
        feed_part = add_parts(core, feed_keep, feed_got, wait=[n1_keep0])
        after_first = [feed_part]
        feed_got = quarter_trade(feed_part)
    rgrad1, branch1, small_two = norm_two_back(
        1, core, n21, n2_far1, resid1, out_grad, gain2, before=small_two, wait=after_first
    )
    mlp_theirs = chip_swap(mlp_away)
    n1_send1, n1_keep1, *sums = attend_back(
        1, core, branch1, core_swap(branch1), *made1[1:], ctx1, lse1, *shared_args, made1[0], gain1, beta1,
        before=sums, pieces=pieces, small_two=small_two, small_feed=small_feed, wait=[n1_core0, mlp_away],
    )
    small, grad_send, grad_keep = hold(sums, mlp_theirs)
    halves = [add_low(n1_keep0, n1_core0), add_low(n1_keep1, core_swap(n1_send1))]
    shared = lax.broadcasted_iota(jnp.int32, small.shape, 0) < 5
    for swap in (core_swap, chip_swap):
        small = small + jnp.where(shared, swap(small), 0.0)
    away = after(jnp.where(far, halves[0], halves[1]), small)
    mine = jnp.where(far, halves[1], halves[0])
    theirs = chip_swap(away)
    if tree:
        grad_got = half_swap(grad_send)
        feed_all = lax.all_gather(sum_parts(core, feed_got, copies=1, wait=[grad_keep]), "dp", axis=0, tiled=True)
        grad_got = quarter_trade(add_parts(core, grad_keep, grad_got))
        grad_sum = quarter_trade(sum_parts(core, grad_got, small))
        grad_other = half_swap(grad_sum)
    else:
        small, grad_send, grad_keep, feed_send, feed_keep = lax.psum(
            (small, grad_send, grad_keep, feed_send, feed_keep), "dp"
        )
        feed_all = jnp.concatenate([feed_keep, feed_send])
        grad_sum = sum_parts(core, grad_keep, small)
        grad_other = sum_parts(core, grad_send, jnp.zeros_like(small))

    out_rows = (
        jnp.where(far, resid1, resid0)
        + (mlp_mine.astype(f32) + mlp_theirs.astype(f32))
        + row(down_bias)
    ).astype(bf16)
    grad_rows = norm_one_back(place_arr, mine, theirs, patches, rgrad0, rgrad1, gain1)
    up_grad, down_grad = place_all(feed_all, (d, units))
    (grad_other,) = hold([grad_other], grad_rows)
    qkv_grad, out_grad_w, small = place_parts(core, grad_sum, grad_other, (3 * width, width), True)
    turns = heads * HALF
    by_col = small[7, 3 * width : 3 * width + turns].reshape(heads, HALF)
    by_row = small[7, 3 * width + turns : 3 * width + 2 * turns].reshape(heads, HALF)
    return (
        out_rows,
        grad_rows,
        small[0],
        small[1],
        qkv_grad.reshape(3, width, d).transpose(2, 0, 1),
        small[7, : 3 * width].reshape(3, width),
        jnp.concatenate([by_col, by_row], axis=-1),
        out_grad_w,
        small[4],
        small[2],
        small[3],
        up_grad,
        small[5],
        down_grad,
        small[6],
    )


def solution(mesh):
    placed = (
        P("dp", None),
        P("dp"),
        P(None, "dp"),
        P(),
        P(),
        P(None, None, "mp"),
        P(None, "mp"),
        P("mp", None),
        P("mp", None),
        P(),
        P(),
        P(),
        P(None, "mp"),
        P("mp"),
        P("mp", None),
        P(),
        P("dp", None),
    )
    return jax.shard_map(
        local,
        mesh=mesh,
        in_specs=placed,
        out_specs=(
            P(("dp", "mp"), None),
            P(("dp", "mp"), None),
            P(),
            P(),
            P(None, None, "mp"),
            P(None, "mp"),
            P("mp", None),
            P("mp", None),
            P(),
            P(),
            P(),
            P(None, "mp"),
            P("mp"),
            P("mp", None),
            P(),
        ),
        check_vma=False,
    )
```

time: 821 us -> 292 us (0.36); the launches traced: 811 us -> 291 us
  waiting for transfers between devices: 418 us -> 88.8 us
  matrix products: 138 us -> 0 us
  Pallas kernels: 0 us -> 129 us
  local copies, waits for them, and re-layouts: 107 us -> 17.2 us
  other arithmetic: 91.3 us -> 11.3 us
  blocking collectives: 40.8 us -> 0 us
  starting transfers between devices: 0.16 us -> 30.6 us
    psum x4 -> x0, waiting for transfers between devices: 418 us -> none  [the longest x1 189 us: local(): lax.psum((qkv_weight_grad, qkv_bias_grad, rope_freq_grad, out_weight_grad...]
    dot_general x38 -> x0, matrix products: 133 us -> none  [the longest x4 24.1 us: one_sequence(): jnp.einsum('qhd,khd->hqk', grad_part, values_seq, preferred_element_type=...]
    pallas_call x0 -> x20, Pallas kernels: none -> 129 us  [the longest x2 40.5 us: attend_back(): pl.pallas_call(ignoring(len(wait), functools.partial(attend_back_kernel,...]
    dynamic_update_slice x8 -> x0, local copies, waits for them, and re-layouts: 60.7 us -> none  [attend(): context, log_total = lax.map(one_sequence, shaped)]
    ppermute x0 -> x28, waiting for transfers between devices: none -> 53.7 us  [the longest x3 30.8 us: half_swap(): lax.ppermute(value, 'dp', [(i, i ^ 1) for i in range(lax.axis_size('dp'))])]
    psum x1 -> x0, blocking collectives: 40.8 us -> none  [local(): lax.psum((qkv_weight_grad, qkv_bias_grad, rope_freq_grad, out_weight_grad...]
    reduce_sum x11 -> x0, other arithmetic: 38.1 us -> none  [the longest x1 8.2 us: local(): jnp.sum(first_normalized_gradient * first_unit_variance_rows, axis=0)]
    all_to_all x0 -> x3, waiting for transfers between devices: none -> 35 us  [quarter_trade(): lax.all_to_all(parts, 'dp', 0, 0, axis_index_groups=[[0, 2, 4, 6], [1, 3,...]
  transfers between devices with their start and end apart: 4 -> 32, of which waited for: 4 -> 14; matrix products, arithmetic and copies ran while one was open for 5% -> 5% of each run, Pallas kernels for 0% -> 37%
where the time goes in v1:
time: 292 us; the launch traced here: 291 us
  Pallas kernels  129 us (44%)
  waiting for transfers between devices  88.8 us (30%)
  starting transfers between devices  30.6 us (10%)
  local copies, waits for them, and re-layouts  17.2 us (6%)
  between operations  14.6 us (5%)
  other arithmetic  11.3 us (4%)
    pallas_call x2, Pallas kernels, attend_back(): pl.pallas_call(ignoring(len(wait), functools.partial(attend_back_kernel,...  40.5 us
    all_to_all x3, waiting for transfers between devices, quarter_trade(): lax.all_to_all(parts, 'dp', 0, 0, axis_index_groups=[[0, 2, 4, 6], [1, 3,...  35 us
    ppermute x3, waiting for transfers between devices, half_swap(): lax.ppermute(value, 'dp', [(i, i ^ 1) for i in range(lax.axis_size('dp'))])  30.8 us
    pallas_call x2, Pallas kernels, feed(): pl.pallas_call(ignoring(len(wait), functools.partial(feed_kernel, first,...  26.9 us
    ppermute x10, waiting for transfers between devices, chip_swap(): return lax.ppermute(value, 'mp', CHIP_SWAP)  18.7 us
    pallas_call x2, Pallas kernels, attend(): pl.pallas_call(ignoring(len(wait), attend_kernel), grid_spec=pltpu.Prefet...  16.9 us
    all_to_all x3, starting transfers between devices, quarter_trade(): lax.all_to_all(parts, 'dp', 0, 0, axis_index_groups=[[0, 2, 4, 6], [1, 3,...  14.6 us
    unnamed x104, local copies, waits for them, and re-layouts  13.9 us
  transfers between devices with their start and end apart: 32, of which 14 were waited for; matrix products, arithmetic and copies ran while one was open for 5% of the time, Pallas kernels for 37%

profile of v1, /device:TPU:0, one launch (start us, length us, event | category | flops | bytes accessed | tf_op | source)
XLA Modules:
  0.0 291.2 jit_solution(12958438087243493890)
XLA Ops:
  7.7 2.6 collective-permute-start.6
  11.7 2.1 prepare.1
  13.8 1.2 copy-done
  15.0 1.0 copy-done.5
  15.9 0.9 copy-done.12
  16.8 0.7 copy-done.14
  17.6 5.4 %project.2 = (bf16[1024,768]{1,0:T(8,128)(2,1)}, bf16[192,1024]{1,0:T(8,128)(2,1)S(1)}, bf16[192,1024]{1,0:T(8,128)(2,1)S(1)}, bf16[192,1024]{1,0:T(8,128)(2,1)S(1)}) custom-call(s32[2]{0:T(128)S(1)} %pad_add_fusion.c_ref, bf16[2048,768]{1,0:T(8,128)(2,1)} %x_ref.1, s32[2,2048]{1,0:T(2,128)S(1)} %copy-done.14, bf16[384,128]{1,0:T(8,128)(2,1)S(1)} %copy-done.12, ...), custom_call_target="tpu_custom_call" | custom-call | flops 905969664 | bytes 5210112 | tf_op jit(solution)/shard_map/project/pallas_call | solution.py:151
  23.4 8.5 %attend.2 = (bf16[192,512]{1,0:T(8,128)(2,1)S(1)}, bf16[192,512]{1,0:T(8,128)(2,1)S(1)}, f32[192,1024]{1,0:T(8,128)}, f32[8,1024]{1,0:T(8,128)}) custom-call(s32[2]{0:T(128)S(1)} %pad_add_fusion.c_ref, bf16[192,1024]{1,0:T(8,128)(2,1)S(1)} %get-tuple-element.81.refs_0_.refs_3_, bf16[192,1024]{1,0:T(8,128)(2,1)S(1)} %get-tuple-element.82.refs_1_.refs_4_, ...), custom_call_target="tpu_custom_call" | custom-call | flops 1610612736 | bytes 2359296 | tf_op jit(solution)/shard_map/attend/pallas_call | solution.py:256
  32.5 0.9 collective-permute-done.refs_0_.refs_3_
  33.3 0.9 collective-permute-start.5
  34.3 5.4 %project.3 = (bf16[1024,768]{1,0:T(8,128)(2,1)}, bf16[192,1024]{1,0:T(8,128)(2,1)S(1)}, bf16[192,1024]{1,0:T(8,128)(2,1)S(1)}, bf16[192,1024]{1,0:T(8,128)(2,1)S(1)}) custom-call(s32[2]{0:T(128)S(1)} %pad_add_fusion.c_ref, bf16[192,512]{1,0:T(8,128)(2,1)S(1)} %get-tuple-element.85.refs_0_.refs_2_, ...), custom_call_target="tpu_custom_call" | custom-call | flops 905969664 | bytes 5210112 | tf_op jit(solution)/shard_map/project/pallas_call | solution.py:151
  39.8 8.5 %attend.3 = (bf16[192,512]{1,0:T(8,128)(2,1)S(1)}, bf16[192,512]{1,0:T(8,128)(2,1)S(1)}, f32[192,1024]{1,0:T(8,128)}, f32[8,1024]{1,0:T(8,128)}) custom-call(s32[2]{0:T(128)S(1)} %pad_add_fusion.c_ref, bf16[192,512]{1,0:T(8,128)(2,1)S(1)} %collective-permute-done.refs_0_.refs_3_, bf16[192,512]{1,0:T(8,128)(2,1)S(1)} %collective-permute-done.1.refs_1_.refs_4_, ...), custom_call_target="tpu_custom_call" | custom-call | flops 1610612736 | bytes 2359296 | tf_op jit(solution)/shard_map/attend/pallas_call | solution.py:256
  48.3 4.2 %norm_two.2 = (f32[512,768]{1,0:T(8,128)}, bf16[512,768]{1,0:T(8,128)(2,1)S(1)}) custom-call(s32[2]{0:T(128)S(1)} %pad_add_fusion.c_ref, bf16[192,512]{1,0:T(8,128)(2,1)S(1)} %get-tuple-element.90.refs_0_.refs_2_, bf16[2048,768]{1,0:T(8,128)(2,1)} %x_ref.1, bf16[192,512]{1,0:T(8,128)(2,1)S(1)} %get-tuple-element.85.refs_0_.refs_2_, ...), custom_call_target="tpu_custom_call" | custom-call | flops 603979776 | bytes 4718592 | tf_op jit(solution)/shard_map/norm_two/pallas_call | solution.py:313
  53.0 1.0 collective-permute-start.4
  54.0 1.1 collective-permute-done.3.refs_0_.refs_3_
  55.1 4.8 %collective-permute-done.4.refs_1_.refs_4_ = bf16[192,512]{1,0:T(8,128)(2,1)S(1)} collective-permute-done((bf16[192,512]{1,0:T(8,128)(2,1)S(1)}, bf16[192,512]{1,0:T(8,128)(2,1)S(1)}, u32[]{:S(2)}, u32[]{:S(2)}) %collective-permute-start.4) | collective-permute-done | bytes 196640 | tf_op jit(solution)/shard_map/ppermute | solution.py:754
  59.9 13.8 %feed.2 = (bf16[512,768]{1,0:T(8,128)(2,1)}, bf16[512,768]{1,0:T(8,128)(2,1)}, bf16[512,768]{1,0:T(8,128)(2,1)S(1)}, bf16[512,768]{1,0:T(8,128)(2,1)S(1)}, f32[8...) custom-call(s32[2]{0:T(128)S(1)} %pad_add_fusion.c_ref, ...), custom_call_target="tpu_custom_call" | custom-call | flops 7247757312 | bytes 13369344 | tf_op jit(solution)/shard_map/feed/pallas_call | solution.py:433
  73.7 1.0 collective-permute-start.9
  74.7 6.3 %collective-permute-done.9.refs_5_ = bf16[192,512]{1,0:T(8,128)(2,1)S(1)} collective-permute-done((bf16[192,512]{1,0:T(8,128)(2,1)S(1)}, bf16[192,512]{1,0:T(8,128)(2,1)S(1)}, u32[]{:S(2)}, u32[]{:S(2)}) %collective-permute-start.9) | collective-permute-done | bytes 196640 | tf_op jit(solution)/shard_map/ppermute | solution.py:754
  81.0 4.2 %norm_two.3 = (f32[512,768]{1,0:T(8,128)}, bf16[512,768]{1,0:T(8,128)(2,1)S(1)}) custom-call(s32[2]{0:T(128)S(1)} %pad_add_fusion.c_ref, bf16[512,768]{1,0:T(8,128)(2,1)S(1)} %get-tuple-element.92.refs_0_, bf16[2048,768]{1,0:T(8,128)(2,1)} %x_ref.1, bf16[192,512]{1,0:T(8,128)(2,1)S(1)} %get-tuple-element.90.refs_0_.refs_2_, ...), custom_call_target="tpu_custom_call" | custom-call | flops 603979776 | bytes 4718592 | tf_op jit(solution)/shard_map/norm_two/pallas_call | solution.py:313
  85.4 1.0 collective-permute-start.16
  86.4 1.1 collective-permute-done.11.refs_2_
  87.5 13.1 %feed.3 = (bf16[512,768]{1,0:T(8,128)(2,1)}, bf16[512,768]{1,0:T(8,128)(2,1)}, bf16[512,768]{1,0:T(8,128)(2,1)S(1)}, bf16[512,768]{1,0:T(8,128)(2,1)S(1)}, f32[8...) custom-call(s32[2]{0:T(128)S(1)} %pad_add_fusion.c_ref, ...), custom_call_target="tpu_custom_call" | custom-call | flops 7247757312 | bytes 13369344 | tf_op jit(solution)/shard_map/feed/pallas_call | solution.py:433
  100.8 4.6 %collective-permute-done.16.refs_2_ = bf16[512,768]{1,0:T(8,128)(2,1)S(1)} collective-permute-done((bf16[512,768]{1,0:T(8,128)(2,1)S(1)}, bf16[512,768]{1,0:T(8,128)(2,1)S(1)}, u32[]{:S(2)}, u32[]{:S(2)}) %collective-permute-start.16) | collective-permute-done | bytes 786464 | tf_op jit(solution)/shard_map/ppermute | solution.py:754
  105.5 4.2 %norm_two_back.2 = (f32[512,768]{1,0:T(8,128)}, bf16[512,768]{1,0:T(8,128)(2,1)S(1)}, f32[8,768]{1,0:T(8,128)}) custom-call(s32[2]{0:T(128)S(1)} %pad_add_fusion.c_ref, bf16[512,768]{1,0:T(8,128)(2,1)S(1)} %get-tuple-element.104.refs_0_, bf16[512,768]{1,0:T(8,128)(2,1)S(1)} %add_convert_fusion.6.refs_0_.refs_1_, ...), custom_call_target="tpu_custom_call" | custom-call | flops 7864320 | bytes 6291456 | tf_op jit(solution)/shard_map/norm_two_back/pallas_call | solution.py:499
  109.7 1.6 collective-permute-start.19
  111.8 1.1 add_convert_fusion.2.refs_0_.refs_1_
  112.9 0.9 collective-permute-start.20
  113.9 19.7 %attend_back.2 = (bf16[512,768]{1,0:T(8,128)(2,1)}, bf16[512,768]{1,0:T(8,128)(2,1)S(1)}, f32[576,768]{1,0:T(8,128)}, f32[192,768]{1,0:T(8,128)}, f32[8,576]{1,0...) custom-call(s32[2]{0:T(128)S(1)} %pad_add_fusion.c_ref, bf16[512,768]{1,0:T(8,128)(2,1)} %add_convert_fusion.2.refs_0_.refs_1_, ...), custom_call_target="tpu_custom_call" | custom-call | flops 7046430720 | bytes 9437184 | tf_op jit(solution)/shard_map/attend_back/pallas_call | solution.py:698
  133.5 4.6 %collective-permute-done.19.refs_2_ = bf16[4,192,768]{2,1,0:T(8,128)(2,1)S(1)} collective-permute-done((bf16[4,192,768]{2,1,0:T(8,128)(2,1)S(1)}, bf16[4,192,768]{2,1,0:T(8,128)(2,1)S(1)}, u32[]{:S(2)}, u32[]{:S(2)}) %collective-permute-start.19) | collective-permute-done | bytes 1179680 | tf_op jit(solution)/shard_map/ppermute | solution.py:879
  138.1 1.8 add_parts.2.refs_0_
  139.9 6.0 %all-to-all-start.2 = ((bf16[4,192,768]{2,1,0:T(8,128)(2,1)}), bf16[4,192,768]{2,1,0:T(8,128)(2,1)S(1)}, u32[]{:S(2)}, u32[]{:S(2)}) async-start(bf16[4,192,768]{2,1,0:T(8,128)(2,1)} %add_parts.2.refs_0_), calls=%async_computation.2 | async-start | bytes 2359296 | tf_op jit(solution)/shard_map/all_to_all | solution.py:883
  145.9 4.7 %norm_two_back.3 = (f32[512,768]{1,0:T(8,128)}, bf16[512,768]{1,0:T(8,128)(2,1)}, f32[8,768]{1,0:T(8,128)}) custom-call(s32[2]{0:T(128)S(1)} %pad_add_fusion.c_ref, bf16[4,192,768]{2,1,0:T(8,128)(2,1)} %add_parts.2.refs_0_, bf16[512,768]{1,0:T(8,128)(2,1)} %add_convert_fusion.2.refs_0_.refs_1_, bf16[512,768]{1,0:T(8,128)(2,1)} %collective-permute-done.20.refs_2_, ...), custom_call_target="tpu_custom_call" | custom-call | flops 7864320 | bytes 6291456 | tf_op jit(solution)/shard_map/norm_two_back/pallas_call | solution.py:499
  151.3 2.4 broadcast_select_fusion.1.refs_1_
  153.7 1.0 collective-permute-start.14
  154.8 1.1 copy-done.31
  155.9 1.5 copy-done.35
  157.4 1.1 copy-done.37
  158.4 1.0 copy-done.39
  159.4 20.9 %attend_back.3 = (bf16[512,768]{1,0:T(8,128)(2,1)S(1)}, bf16[512,768]{1,0:T(8,128)(2,1)S(1)}, f32[8,768]{1,0:T(8,128)}, bf16[4,96,768]{2,1,0:T(8,128)(2,1)}, bf16[4,96,768]{2,1,0:T(8,128)(2,1)}) custom-call(s32[2]{0:T(128)S(1)} %pad_add_fusion.c_ref, bf16[512,768]{1,0:T(8,128)(2,1)} %collective-permute-done.18.refs_0_, ...), custom_call_target="tpu_custom_call" | custom-call | flops 7046430720 | bytes 9437184 | tf_op jit(solution)/shard_map/attend_back/pallas_call | solution.py:698
  180.3 0.9 copy-done.10
  181.1 0.9 copy-done.22
  182.0 0.9 copy-done.44
  182.9 1.1 copy-done.3
  184.0 1.4 sum_parts.3
  186.0 18.0 %collective-permute-done.26.refs_1_ = bf16[4,96,768]{2,1,0:T(8,128)(2,1)S(1)} collective-permute-done((bf16[4,96,768]{2,1,0:T(8,128)(2,1)}, bf16[4,96,768]{2,1,0:T(8,128)(2,1)S(1)}, u32[]{:S(2)}, u32[]{:S(2)}) %collective-permute-start.26) | collective-permute-done | bytes 589856 | tf_op jit(solution)/shard_map/ppermute | solution.py:879
  204.0 1.5 add_parts.3
  205.5 5.1 %all-to-all-start = ((bf16[4,96,768]{2,1,0:T(8,128)(2,1)}), bf16[4,96,768]{2,1,0:T(8,128)(2,1)S(1)}, u32[]{:S(2)}, u32[]{:S(2)}) async-start(bf16[4,96,768]{2,1,0:T(8,128)(2,1)} %add_parts.3), calls=%async_computation | async-start | bytes 1179648 | tf_op jit(solution)/shard_map/all_to_all | solution.py:883
  210.6 1.2 collective-permute-done.23
  211.9 1.0 collective-permute-start.24
  212.9 2.8 collective-permute-done.24
  215.8 20.9 %all-to-all-done.refs_0_ = bf16[4,96,768]{2,1,0:T(8,128)(2,1)S(1)} async-done(((bf16[4,96,768]{2,1,0:T(8,128)(2,1)}), bf16[4,96,768]{2,1,0:T(8,128)(2,1)S(1)}, u32[]{:S(2)}, u32[]{:S(2)}) %all-to-all-start) | async-done | bytes 589856 | tf_op jit(solution)/shard_map/all_to_all | solution.py:883
  236.7 1.5 sum_parts.2
  238.2 3.5 %all-to-all-start.1 = ((bf16[4,112,768]{2,1,0:T(8,128)(2,1)}), bf16[4,112,768]{2,1,0:T(8,128)(2,1)S(1)}, u32[]{:S(2)}, u32[]{:S(2)}) async-start(bf16[4,112,768]{2,1,0:T(8,128)(2,1)} %sum_parts.2), calls=%async_computation.1 | async-start | bytes 1376256 | tf_op jit(solution)/shard_map/all_to_all | solution.py:883
  241.7 2.7 broadcast_select_fusion.2
  244.4 0.9 collective-permute-start.25
  245.3 14.1 %all-to-all-done.1.mine_ref = bf16[4,112,768]{2,1,0:T(8,128)(2,1)S(1)} async-done(((bf16[4,112,768]{2,1,0:T(8,128)(2,1)}), bf16[4,112,768]{2,1,0:T(8,128)(2,1)S(1)}, u32[]{:S(2)}, u32[]{:S(2)}) %all-to-all-start.1) | async-done | bytes 688160 | tf_op jit(solution)/shard_map/all_to_all | solution.py:883
  259.4 0.7 collective-permute-start.27
  260.1 4.1 %add_convert_fusion.3 = bf16[512,768]{1,0:T(8,128)(2,1)} fusion(bf16[512,768]{1,0:T(8,128)(2,1)} %copy-done.44, f32[512,768]{1,0:T(8,128)} %get-tuple-element.93.refs_3_, f32[512,768]{1,0:T(8,128)} %get-tuple-element.94.refs_3_, f32[768]{0:T(1024)S(1)} %copy-done.46, pred[]{:T(512)S(6)} %ge.3, bf16[512,768]{1,0:T(8,128)(2,1)} %collective-permute-done.12, ...), kind=kLoop, calls=%fused_computation.3 | loop fusion | flops 6291456 | bytes 7867393 | tf_op jit(solution)/shard_map/convert_element_type | solution.py:998
  264.2 3.4 %norm_one_back.1 = bf16[512,768]{1,0:T(8,128)(2,1)} custom-call(s32[1]{0:T(128)} %bitcast.6.m_ref, bf16[512,768]{1,0:T(8,128)(2,1)S(1)} %get-tuple-element.153.mine_ref, bf16[512,768]{1,0:T(8,128)(2,1)S(1)} %collective-permute-done.25.theirs_ref, bf16[2048,768]{1,0:T(8,128)(2,1)} %x_ref.1, f32[512,768]{1,0:T(8,128)} %get-tuple-element.133.rg0_ref, ...), custom_call_target="tpu_custom_call" | custom-call | flops 7864320 | bytes 6291456 | tf_op jit(solution)/shard_map/norm_one_back/pallas_call | solution.py:727
  267.7 8.2 %collective-permute-done.27.theirs_ref = bf16[4,112,768]{2,1,0:T(8,128)(2,1)S(1)} collective-permute-done((bf16[4,112,768]{2,1,0:T(8,128)(2,1)S(1)}, bf16[4,112,768]{2,1,0:T(8,128)(2,1)S(1)}, u32[]{:S(2)}, u32[]{:S(2)}) %collective-permute-start.27) | collective-permute-done | bytes 688160 | tf_op jit(solution)/shard_map/ppermute | solution.py:879
  275.9 2.1 place_parts.1
  280.2 1.7 copy-done.2
  281.9 2.5 place_all.1
  (148 shorter events, 8.2 us)
Async XLA Ops:
  7.2 27.1 %collective-permute-start.2 = (bf16[192,768]{1,0:T(8,128)(2,1)}, bf16[192,768]{1,0:T(8,128)(2,1)S(1)}, u32[]{:S(2)}, u32[]{:S(2)}) collective-permute-start(bf16[192,768]{1,0:T(8,128)(2,1)} %refs_12_.1), channel_id=1, source_target_pairs={{0,1},{1,0},{2,3},{3,2},{4,5},{5,4},{6,7},{7,6},{8,9},{9,8},{10,11... | collective-permute-start | bytes 884744 | tf_op jit(solution)/shard_map/ppermute | solution.py:750
  7.7 24.6 %collective-permute-start.6 = (bf16[192,768]{1,0:T(8,128)(2,1)}, bf16[192,768]{1,0:T(8,128)(2,1)S(1)}, u32[]{:S(2)}, u32[]{:S(2)}) collective-permute-start(bf16[192,768]{1,0:T(8,128)(2,1)} %refs_12_.1), channel_id=1, source_target_pairs={{0,2},{1,3},{2,0},{3,1},{4,6},{5,7},{6,4},{7,5},{8,10},{9,11},{10,... | collective-permute-start | bytes 884744 | tf_op jit(solution)/shard_map/ppermute | solution.py:754
  17.6 5.5 %copy-start.17 = (s32[2048]{0:T(1024)S(1)}, s32[2048]{0:T(1024)}, u32[]{:S(2)}) copy-start(s32[2048]{0:T(1024)} %param.18) | copy-start | bytes 24580
  23.3 90.5 %copy-start.8 = (s32[2048,128]{1,0:T(8,128)}, s32[2048,128]{1,0:T(8,128)S(1)}, u32[]{:S(2)}) copy-start(s32[2048,128]{1,0:T(8,128)S(1)} %broadcast_in_dim.12.refs_5_.refs_7_.refs_10_.refs_11_) | copy-start | bytes 3145732
  23.3 9.1 %copy-start.47 = (f32[768]{0:T(1024)S(1)}, f32[768]{0:T(1024)}, u32[]{:S(2)}) copy-start(f32[768]{0:T(1024)} %param.27) | copy-start | bytes 9220
  23.4 9.1 %copy-start.48 = (f32[768]{0:T(1024)S(1)}, f32[768]{0:T(1024)}, u32[]{:S(2)}) copy-start(f32[768]{0:T(1024)} %param.26) | copy-start | bytes 9220
  23.4 9.1 %copy-start.49 = (f32[768]{0:T(1024)S(1)}, f32[768]{0:T(1024)}, u32[]{:S(2)}) copy-start(f32[768]{0:T(1024)} %param.28) | copy-start | bytes 9220
  23.4 10.9 %copy-start.1 = (bf16[768,3,192]{0,2,1:T(8,128)(2,1)S(1)}, bf16[768,3,192]{0,2,1:T(8,128)(2,1)}, u32[]{:S(2)}) copy-start(bf16[768,3,192]{0,2,1:T(8,128)(2,1)} %param.22) | copy-start | bytes 2654212
  23.4 10.9 %copy-start.6 = (f32[576,128]{1,0:T(8,128)S(1)}, f32[576,128]{1,0:T(8,128)}, u32[]{:S(2)}) copy-start(f32[576,128]{1,0:T(8,128)} %get-tuple-element.80.refs_4_.refs_6_) | copy-start | bytes 884740
  23.4 10.9 %copy-start.15 = (s32[2,2048]{1,0:T(2,128)S(1)}, s32[2,2048]{1,0:T(2,128)}, u32[]{:S(2)}) copy-start(s32[2,2048]{1,0:T(2,128)} %refs_15_.1) | copy-start | bytes 49156
  31.9 1.4 collective-permute-start
  32.1 7.7 %collective-permute-start.1 = (bf16[192,512]{1,0:T(8,128)(2,1)S(1)}, bf16[192,512]{1,0:T(8,128)(2,1)S(1)}, u32[]{:S(2)}, u32[]{:S(2)}) collective-permute-start(bf16[192,512]{1,0:T(8,128)(2,1)S(1)} %get-tuple-element.85.refs_0_.refs_2_), channel_id=1, source_target_pairs={{0,2},{1,3},{2,0},{3,1},{4,6},{5,7},{6,4},{7,5},{8,10},{9,11},{10,... | collective-permute-start | bytes 589832 | tf_op jit(solution)/shard_map/ppermute | solution.py:754
  32.3 15.9 %collective-permute-start.7 = (bf16[192,768]{1,0:T(8,128)(2,1)S(1)}, bf16[192,768]{1,0:T(8,128)(2,1)S(1)}, u32[]{:S(2)}, u32[]{:S(2)}) collective-permute-start(bf16[192,768]{1,0:T(8,128)(2,1)S(1)} %collective-permute-done.6.refs_8_), channel_id=1, source_target_pairs={{0,1},{1,0},{2,3},{3,2},{4,5},{5,4},{6,7},{7,6},{8,9},{9,8},{10,11... | collective-permute-start | bytes 884744 | tf_op jit(solution)/shard_map/ppermute | solution.py:750
  33.3 14.9 %collective-permute-start.5 = (bf16[192,512]{1,0:T(8,128)(2,1)S(1)}, bf16[192,512]{1,0:T(8,128)(2,1)S(1)}, u32[]{:S(2)}, u32[]{:S(2)}) collective-permute-start(bf16[192,512]{1,0:T(8,128)(2,1)S(1)} %collective-permute-done.refs_0_.refs_3_), channel_id=1, source_target_pairs={{0,2},{1,3},{2,0},{3,1},{4,6},{5,7},{6,4},{7,5},{8,10},{9,11},{10,... | collective-permute-start | bytes 589832 | tf_op jit(solution)/shard_map/ppermute | solution.py:754
  39.7 8.6 %copy-start.24 = (bf16[192,1024]{1,0:T(8,128)(2,1)}, bf16[192,1024]{1,0:T(8,128)(2,1)S(1)}, u32[]{:S(2)}) copy-start(bf16[192,1024]{1,0:T(8,128)(2,1)S(1)} %get-tuple-element.86.refs_2_.refs_4_) | copy-start | bytes 1179652
  39.7 8.6 %copy-start.26 = (bf16[192,1024]{1,0:T(8,128)(2,1)}, bf16[192,1024]{1,0:T(8,128)(2,1)S(1)}, u32[]{:S(2)}) copy-start(bf16[192,1024]{1,0:T(8,128)(2,1)S(1)} %get-tuple-element.87.refs_3_.refs_5_) | copy-start | bytes 1179652
  39.7 8.6 %copy-start.28 = (bf16[192,1024]{1,0:T(8,128)(2,1)}, bf16[192,1024]{1,0:T(8,128)(2,1)S(1)}, u32[]{:S(2)}) copy-start(bf16[192,1024]{1,0:T(8,128)(2,1)S(1)} %get-tuple-element.88.refs_4_.refs_6_) | copy-start | bytes 1179652
  39.8 8.5 %copy-start.4 = (bf16[192,768]{1,0:T(8,128)(2,1)S(1)}, bf16[192,768]{1,0:T(8,128)(2,1)}, u32[]{:S(2)}) copy-start(bf16[192,768]{1,0:T(8,128)(2,1)} %refs_12_.1) | copy-start | bytes 884740
  48.3 5.7 %copy-start.50 = (f32[768]{0:T(1024)S(1)}, f32[768]{0:T(1024)}, u32[]{:S(2)}) copy-start(f32[768]{0:T(1024)} %param.30) | copy-start | bytes 9220
  48.3 11.6 %copy-start.20 = (bf16[768,768]{1,0:T(8,128)(2,1)S(1)}, bf16[768,768]{1,0:T(8,128)(2,1)}, u32[]{:S(2)}) copy-start(bf16[768,768]{1,0:T(8,128)(2,1)} %refs_4_.5) | copy-start | bytes 3538948
  48.3 11.6 %copy-start.21 = (bf16[768,768]{1,0:T(8,128)(2,1)S(1)}, bf16[768,768]{1,0:T(8,128)(2,1)}, u32[]{:S(2)}) copy-start(bf16[768,768]{1,0:T(8,128)(2,1)} %refs_6_.5) | copy-start | bytes 3538948
  52.5 7.4 %collective-permute-start.8 = (bf16[512,768]{1,0:T(8,128)(2,1)S(1)}, bf16[512,768]{1,0:T(8,128)(2,1)S(1)}, u32[]{:S(2)}, u32[]{:S(2)}) collective-permute-start(bf16[512,768]{1,0:T(8,128)(2,1)S(1)} %get-tuple-element.91.refs_2_), channel_id=1, source_target_pairs={{0,1},{1,0},{2,3},{3,2},{4,5},{5,4},{6,7},{7,6},{8,9},{9,8},{10,11... | collective-permute-start | bytes 2359304 | tf_op jit(solution)/shard_map/ppermute | solution.py:750
  52.6 2.5 collective-permute-start.3
  53.0 6.9 %collective-permute-start.4 = (bf16[192,512]{1,0:T(8,128)(2,1)S(1)}, bf16[192,512]{1,0:T(8,128)(2,1)S(1)}, u32[]{:S(2)}, u32[]{:S(2)}) collective-permute-start(bf16[192,512]{1,0:T(8,128)(2,1)S(1)} %get-tuple-element.90.refs_0_.refs_2_), channel_id=1, source_target_pairs={{0,2},{1,3},{2,0},{3,1},{4,6},{5,7},{6,4},{7,5},{8,10},{9,11},{10,... | collective-permute-start | bytes 589832 | tf_op jit(solution)/shard_map/ppermute | solution.py:754
  73.7 11.6 %collective-permute-start.10 = (bf16[512,768]{1,0:T(8,128)(2,1)S(1)}, bf16[512,768]{1,0:T(8,128)(2,1)S(1)}, u32[]{:S(2)}, u32[]{:S(2)}) collective-permute-start(bf16[512,768]{1,0:T(8,128)(2,1)S(1)} %get-tuple-element.95), channel_id=1, source_target_pairs={{0,1},{1,0},{2,3},{3,2},{4,5},{5,4},{6,7},{7,6},{8,9},{9,8},{10,11... | collective-permute-start | bytes 2359304 | tf_op jit(solution)/shard_map/ppermute | solution.py:750
  73.7 7.3 %collective-permute-start.9 = (bf16[192,512]{1,0:T(8,128)(2,1)S(1)}, bf16[192,512]{1,0:T(8,128)(2,1)S(1)}, u32[]{:S(2)}, u32[]{:S(2)}) collective-permute-start(bf16[192,512]{1,0:T(8,128)(2,1)S(1)} %collective-permute-done.3.refs_0_.refs_3_), channel_id=1, source_target_pairs={{0,2},{1,3},{2,0},{3,1},{4,6},{5,7},{6,4},{7,5},{8,10},{9,11},{10,... | collective-permute-start | bytes 589832 | tf_op jit(solution)/shard_map/ppermute | solution.py:754
  81.0 6.5 %copy-start.34 = (f32[768,768]{1,0:T(8,128)S(1)}, f32[768,768]{1,0:T(8,128)}, u32[]{:S(2)}) copy-start(f32[768,768]{1,0:T(8,128)} %get-tuple-element.99.refs_9_) | copy-start | bytes 7077892
  81.0 6.5 %copy-start.41 = (f32[8,768]{1,0:T(8,128)S(1)}, f32[8,768]{1,0:T(8,128)}, u32[]{:S(2)}) copy-start(f32[8,768]{1,0:T(8,128)} %get-tuple-element.97.refs_7_) | copy-start | bytes 73732
  85.2 2.3 collective-permute-start.11
  85.4 20.0 %collective-permute-start.16 = (bf16[512,768]{1,0:T(8,128)(2,1)S(1)}, bf16[512,768]{1,0:T(8,128)(2,1)S(1)}, u32[]{:S(2)}, u32[]{:S(2)}) collective-permute-start(bf16[512,768]{1,0:T(8,128)(2,1)S(1)} %add_convert_fusion.6.refs_0_.refs_1_), channel_id=1, source_target_pairs={{0,2},{1,3},{2,0},{3,1},{4,6},{5,7},{6,4},{7,5},{8,10},{9,11},{10,... | collective-permute-start | bytes 2359304 | tf_op jit(solution)/shard_map/ppermute | solution.py:754
  100.6 11.2 %collective-permute-start.15 = (bf16[512,768]{1,0:T(8,128)(2,1)S(1)}, bf16[512,768]{1,0:T(8,128)(2,1)S(1)}, u32[]{:S(2)}, u32[]{:S(2)}) collective-permute-start(bf16[512,768]{1,0:T(8,128)(2,1)S(1)} %get-tuple-element.105), channel_id=1, source_target_pairs={{0,1},{1,0},{2,3},{3,2},{4,5},{5,4},{6,7},{7,6},{8,9},{9,8},{10,11... | collective-permute-start | bytes 2359304 | tf_op jit(solution)/shard_map/ppermute | solution.py:750
  105.5 4.2 %copy-start.51 = (bf16[4,192,768]{2,1,0:T(8,128)(2,1)S(1)}, bf16[4,192,768]{2,1,0:T(8,128)(2,1)}, u32[]{:S(2)}) copy-start(bf16[4,192,768]{2,1,0:T(8,128)(2,1)} %get-tuple-element.113) | copy-start | bytes 3538948
  105.5 8.3 %copy-start.32 = (f32[192,1024]{1,0:T(8,128)S(1)}, f32[192,1024]{1,0:T(8,128)}, u32[]{:S(2)}) copy-start(f32[192,1024]{1,0:T(8,128)} %get-tuple-element.107.refs_6_) | copy-start | bytes 2359300
  109.6 4.2 %copy-start.13 = (bf16[384,128]{1,0:T(8,128)(2,1)S(1)}, bf16[384,128]{1,0:T(8,128)(2,1)}, u32[]{:S(2)}) copy-start(bf16[384,128]{1,0:T(8,128)(2,1)} %get-tuple-element.79.refs_2_.refs_4_.refs_13_.refs_14_) | copy-start | bytes 294916
  109.6 4.2 %copy-start.19 = (bf16[1024,768]{1,0:T(8,128)(2,1)S(1)}, bf16[1024,768]{1,0:T(8,128)(2,1)}, u32[]{:S(2)}) copy-start(bf16[1024,768]{1,0:T(8,128)(2,1)} %get-tuple-element.109.refs_15_) | copy-start | bytes 4718596
  109.6 4.2 %copy-start.38 = (f32[8,1024]{1,0:T(8,128)S(1)}, f32[8,1024]{1,0:T(8,128)}, u32[]{:S(2)}) copy-start(f32[8,1024]{1,0:T(8,128)} %get-tuple-element.108.refs_7_) | copy-start | bytes 98308
  109.6 4.2 %collective-permute-start.17 = (bf16[512,768]{1,0:T(8,128)(2,1)S(1)}, bf16[512,768]{1,0:T(8,128)(2,1)S(1)}, u32[]{:S(2)}, u32[]{:S(2)}) collective-permute-start(bf16[512,768]{1,0:T(8,128)(2,1)S(1)} %get-tuple-element.106.refs_1_), channel_id=1, source_target_pairs={{0,1},{1,0},{2,3},{3,2},{4,5},{5,4},{6,7},{7,6},{8,9},{9,8},{10,11... | collective-permute-start | bytes 2359304 | tf_op jit(solution)/shard_map/ppermute | solution.py:750
  109.7 28.4 %collective-permute-start.19 = (bf16[4,192,768]{2,1,0:T(8,128)(2,1)S(1)}, bf16[4,192,768]{2,1,0:T(8,128)(2,1)S(1)}, u32[]{:S(2)}, u32[]{:S(2)}) collective-permute-start(bf16[4,192,768]{2,1,0:T(8,128)(2,1)S(1)} %copy-done.51), channel_id=1, source_target_pairs={{0,4},{4,0},{8,12},{12,8},{16,20},{20,16},{24,28},{28,24},{1,5},{5... | collective-permute-start | bytes 3538952 | tf_op jit(solution)/shard_map/ppermute | solution.py:879
  111.3 39.9 %collective-permute-start.13 = (bf16[512,768]{1,0:T(8,128)(2,1)}, bf16[512,768]{1,0:T(8,128)(2,1)}, u32[]{:S(2)}, u32[]{:S(2)}) collective-permute-start(bf16[512,768]{1,0:T(8,128)(2,1)} %get-tuple-element.103), channel_id=1, source_target_pairs={{0,1},{1,0},{2,3},{3,2},{4,5},{5,4},{6,7},{7,6},{8,9},{9,8},{10,11... | collective-permute-start | bytes 2359304 | tf_op jit(solution)/shard_map/ppermute | solution.py:750
  111.5 39.8 %collective-permute-start.12 = (bf16[512,768]{1,0:T(8,128)(2,1)}, bf16[512,768]{1,0:T(8,128)(2,1)}, u32[]{:S(2)}, u32[]{:S(2)}) collective-permute-start(bf16[512,768]{1,0:T(8,128)(2,1)} %get-tuple-element.101), channel_id=1, source_target_pairs={{0,1},{1,0},{2,3},{3,2},{4,5},{5,4},{6,7},{7,6},{8,9},{9,8},{10,11... | collective-permute-start | bytes 2359304 | tf_op jit(solution)/shard_map/ppermute | solution.py:750
  112.9 33.0 %collective-permute-start.20 = (bf16[512,768]{1,0:T(8,128)(2,1)}, bf16[512,768]{1,0:T(8,128)(2,1)}, u32[]{:S(2)}, u32[]{:S(2)}) collective-permute-start(bf16[512,768]{1,0:T(8,128)(2,1)} %add_convert_fusion.2.refs_0_.refs_1_), channel_id=1, source_target_pairs={{0,2},{1,3},{2,0},{3,1},{4,6},{5,7},{6,4},{7,5},{8,10},{9,11},{10,... | collective-permute-start | bytes 2359304 | tf_op jit(solution)/shard_map/ppermute | solution.py:754
  113.8 24.2 %copy-start.7 = (bf16[4,192,768]{2,1,0:T(8,128)(2,1)S(1)}, bf16[4,192,768]{2,1,0:T(8,128)(2,1)}, u32[]{:S(2)}) copy-start(bf16[4,192,768]{2,1,0:T(8,128)(2,1)} %get-tuple-element.112.refs_1_) | copy-start | bytes 3538948
  139.9 6.0 %copy-start.16 = (f32[8,768]{1,0:T(8,128)S(1)}, f32[8,768]{1,0:T(8,128)}, u32[]{:S(2)}) copy-start(f32[8,768]{1,0:T(8,128)} %get-tuple-element.114.refs_6_) | copy-start | bytes 73732
  139.9 43.0 %all-to-all-start.2 = ((bf16[4,192,768]{2,1,0:T(8,128)(2,1)}), bf16[4,192,768]{2,1,0:T(8,128)(2,1)S(1)}, u32[]{:S(2)}, u32[]{:S(2)}) async-start(bf16[4,192,768]{2,1,0:T(8,128)(2,1)} %add_parts.2.refs_0_), calls=%async_computation.2 | async-start | bytes 2359296 | tf_op jit(solution)/shard_map/all_to_all | solution.py:883
  145.9 134.3 %all-gather.2.cloned.1.call-start = ((), (), s32[]{:S(2)}) async-start(), calls=%async_computation.3 | async-start | bytes 2654208 | tf_op jit(solution)/shard_map/all_gather | solution.py:982
  150.6 4.0 %collective-permute-start.21 = (bf16[512,768]{1,0:T(8,128)(2,1)}, bf16[512,768]{1,0:T(8,128)(2,1)}, u32[]{:S(2)}, u32[]{:S(2)}) collective-permute-start(bf16[512,768]{1,0:T(8,128)(2,1)} %get-tuple-element.115.refs_2_), channel_id=1, source_target_pairs={{0,1},{1,0},{2,3},{3,2},{4,5},{5,4},{6,7},{7,6},{8,9},{9,8},{10,11... | collective-permute-start | bytes 2359304 | tf_op jit(solution)/shard_map/ppermute | solution.py:750
  150.7 3.9 %collective-permute-start.18 = (bf16[512,768]{1,0:T(8,128)(2,1)}, bf16[512,768]{1,0:T(8,128)(2,1)}, u32[]{:S(2)}, u32[]{:S(2)}) collective-permute-start(bf16[512,768]{1,0:T(8,128)(2,1)} %get-tuple-element.110), channel_id=1, source_target_pairs={{0,1},{1,0},{2,3},{3,2},{4,5},{5,4},{6,7},{7,6},{8,9},{9,8},{10,11... | collective-permute-start | bytes 2359304 | tf_op jit(solution)/shard_map/ppermute | solution.py:750
  151.2 3.4 %copy-start.18 = (bf16[1024,768]{1,0:T(8,128)(2,1)S(1)}, bf16[1024,768]{1,0:T(8,128)(2,1)}, u32[]{:S(2)}) copy-start(bf16[1024,768]{1,0:T(8,128)(2,1)} %get-tuple-element.118.refs_16_) | copy-start | bytes 4718596
  151.2 3.4 %copy-start.25 = (bf16[192,1024]{1,0:T(8,128)(2,1)S(1)}, bf16[192,1024]{1,0:T(8,128)(2,1)}, u32[]{:S(2)}) copy-start(bf16[192,1024]{1,0:T(8,128)(2,1)} %copy-done.24) | copy-start | bytes 1179652
  151.2 3.4 %copy-start.27 = (bf16[192,1024]{1,0:T(8,128)(2,1)S(1)}, bf16[192,1024]{1,0:T(8,128)(2,1)}, u32[]{:S(2)}) copy-start(bf16[192,1024]{1,0:T(8,128)(2,1)} %copy-done.26) | copy-start | bytes 1179652
  151.2 3.4 %copy-start.29 = (bf16[192,1024]{1,0:T(8,128)(2,1)S(1)}, bf16[192,1024]{1,0:T(8,128)(2,1)}, u32[]{:S(2)}) copy-start(bf16[192,1024]{1,0:T(8,128)(2,1)} %copy-done.28) | copy-start | bytes 1179652
  153.7 28.3 %collective-permute-start.14 = (bf16[512,768]{1,0:T(8,128)(2,1)S(1)}, bf16[512,768]{1,0:T(8,128)(2,1)S(1)}, u32[]{:S(2)}, u32[]{:S(2)}) collective-permute-start(bf16[512,768]{1,0:T(8,128)(2,1)S(1)} %broadcast_select_fusion.1.refs_1_), channel_id=1, source_target_pairs={{0,2},{1,3},{2,0},{3,1},{4,6},{5,7},{6,4},{7,5},{8,10},{9,11},{10,... | collective-permute-start | bytes 2359304 | tf_op jit(solution)/shard_map/ppermute | solution.py:754
  185.4 25.2 %copy-start.45 = (f32[8,768]{1,0:T(8,128)S(1)}, f32[8,768]{1,0:T(8,128)}, u32[]{:S(2)}) copy-start(f32[8,768]{1,0:T(8,128)} %get-tuple-element.131) | copy-start | bytes 73732
  185.4 27.5 %copy-start.23 = (bf16[512,768]{1,0:T(8,128)(2,1)S(1)}, bf16[512,768]{1,0:T(8,128)(2,1)}, u32[]{:S(2)}) copy-start(bf16[512,768]{1,0:T(8,128)(2,1)} %copy-done.22) | copy-start | bytes 2359300
  185.4 18.6 %collective-permute-start.26 = (bf16[4,96,768]{2,1,0:T(8,128)(2,1)}, bf16[4,96,768]{2,1,0:T(8,128)(2,1)S(1)}, u32[]{:S(2)}, u32[]{:S(2)}) collective-permute-start(bf16[4,96,768]{2,1,0:T(8,128)(2,1)} %get-tuple-element.136), channel_id=1, source_target_pairs={{0,4},{4,0},{8,12},{12,8},{16,20},{20,16},{24,28},{28,24},{1,5},{5... | collective-permute-start | bytes 1769480 | tf_op jit(solution)/shard_map/ppermute | solution.py:879
  205.5 31.2 %all-to-all-start = ((bf16[4,96,768]{2,1,0:T(8,128)(2,1)}), bf16[4,96,768]{2,1,0:T(8,128)(2,1)S(1)}, u32[]{:S(2)}, u32[]{:S(2)}) async-start(bf16[4,96,768]{2,1,0:T(8,128)(2,1)} %add_parts.3), calls=%async_computation | async-start | bytes 1179648 | tf_op jit(solution)/shard_map/all_to_all | solution.py:883
  210.6 31.1 %copy-start.11 = (bf16[512,768]{1,0:T(8,128)(2,1)S(1)}, bf16[512,768]{1,0:T(8,128)(2,1)}, u32[]{:S(2)}) copy-start(bf16[512,768]{1,0:T(8,128)(2,1)} %copy-done.10) | copy-start | bytes 2359300
  210.6 1.2 collective-permute-start.23
  211.9 3.8 %collective-permute-start.24 = (f32[8,768]{1,0:T(8,128)S(1)}, f32[8,768]{1,0:T(8,128)S(1)}, u32[]{:S(2)}, u32[]{:S(2)}) collective-permute-start(f32[8,768]{1,0:T(8,128)S(1)} %select_add_fusion.1), channel_id=1, source_target_pairs={{0,2},{1,3},{2,0},{3,1},{4,6},{5,7},{6,4},{7,5},{8,10},{9,11},{10,... | collective-permute-start | bytes 73736 | tf_op jit(solution)/shard_map/ppermute | solution.py:754
  212.9 28.8 %collective-permute-start.22 = (bf16[512,768]{1,0:T(8,128)(2,1)S(1)}, bf16[512,768]{1,0:T(8,128)(2,1)}, u32[]{:S(2)}, u32[]{:S(2)}) collective-permute-start(bf16[512,768]{1,0:T(8,128)(2,1)S(1)} %copy-done.23), channel_id=1, source_target_pairs={{0,1},{1,0},{2,3},{3,2},{4,5},{5,4},{6,7},{7,6},{8,9},{9,8},{10,11... | collective-permute-start | bytes 2359304 | tf_op jit(solution)/shard_map/ppermute | solution.py:750
  238.2 21.2 %all-to-all-start.1 = ((bf16[4,112,768]{2,1,0:T(8,128)(2,1)}), bf16[4,112,768]{2,1,0:T(8,128)(2,1)S(1)}, u32[]{:S(2)}, u32[]{:S(2)}) async-start(bf16[4,112,768]{2,1,0:T(8,128)(2,1)} %sum_parts.2), calls=%async_computation.1 | async-start | bytes 1376256 | tf_op jit(solution)/shard_map/all_to_all | solution.py:883
  241.7 18.4 %copy-start.46 = (f32[768]{0:T(1024)S(1)}, f32[768]{0:T(1024)}, u32[]{:S(2)}) copy-start(f32[768]{0:T(1024)} %param.32) | copy-start | bytes 9220
  244.4 19.8 %collective-permute-start.25 = (bf16[512,768]{1,0:T(8,128)(2,1)}, bf16[512,768]{1,0:T(8,128)(2,1)S(1)}, u32[]{:S(2)}, u32[]{:S(2)}) collective-permute-start(bf16[512,768]{1,0:T(8,128)(2,1)} %get-tuple-element.132), channel_id=1, source_target_pairs={{0,2},{1,3},{2,0},{3,1},{4,6},{5,7},{6,4},{7,5},{8,10},{9,11},{10,... | collective-permute-start | bytes 2359304 | tf_op jit(solution)/shard_map/ppermute | solution.py:754
  259.4 16.4 %collective-permute-start.27 = (bf16[4,112,768]{2,1,0:T(8,128)(2,1)S(1)}, bf16[4,112,768]{2,1,0:T(8,128)(2,1)S(1)}, u32[]{:S(2)}, u32[]{:S(2)}) collective-permute-start(bf16[4,112,768]{2,1,0:T(8,128)(2,1)S(1)} %all-to-all-done.1.mine_ref), channel_id=1, source_target_pairs={{0,4},{4,0},{8,12},{12,8},{16,20},{20,16},{24,28},{28,24},{1,5},{5... | collective-permute-start | bytes 2064392 | tf_op jit(solution)/shard_map/ppermute | solution.py:879
  (20 other events, 36.7 us)
Sparse Core Ops, SparseCore 0:
  185.5 67.3 all-gather.1

commit v2 on v1

--- a/solution.py
+++ b/solution.py
@@ -13,6 +13,7 @@
 HALF = HD // 2
 RB = 256
 KB = 256
+FB = 512
 
 masked_score = -1e30
 epsilon = 1e-06
@@ -55,7 +56,7 @@
 
 
 def cost(flops, nbytes, trans=0):
-    return pl.CostEstimate(flops=int(flops), bytes_accessed=int(nbytes), transcendentals=int(trans))
+    return pl.CostEstimate(flops=int(flops) // 4, bytes_accessed=int(nbytes) // 4, transcendentals=int(trans) // 4)
 
 
 def standardize(values):
@@ -145,9 +146,9 @@
     d = patches.shape[1]
     wide = wt.shape[0]
     width = wide // 3
-    steps = LEN // RB
+    steps = LEN // FB
     whole = lambda *shape: pl.BlockSpec(shape, lambda i, c: (0,) * len(shape), pipeline_mode=pl.Buffered(1))
-    tall = pl.BlockSpec((width, RB), lambda i, c: (0, i))
+    tall = pl.BlockSpec((width, FB), lambda i, c: (0, i))
     return pl.pallas_call(
         ignoring(len(wait), proj_kernel),
         grid_spec=pltpu.PrefetchScalarGridSpec(
@@ -155,21 +156,21 @@
             grid=(steps,),
             in_specs=[ANY] * len(wait)
             + [
-                pl.BlockSpec((RB, d), lambda i, c: (seq * steps + i, 0)),
-                pl.BlockSpec((2, RB), lambda i, c: (0, seq * steps + i)),
+                pl.BlockSpec((FB, d), lambda i, c: (seq * steps + i, 0)),
+                pl.BlockSpec((2, FB), lambda i, c: (0, seq * steps + i)),
                 whole(*tab.shape),
                 whole(*wt.shape),
                 whole(*bias_cols.shape),
                 whole(1, d),
                 whole(1, d),
             ],
-            out_specs=[pl.BlockSpec((RB, d), lambda i, c: (i, 0)), tall, tall, tall],
+            out_specs=[pl.BlockSpec((FB, d), lambda i, c: (i, 0)), tall, tall, tall],
         ),
         out_shape=[hbm((LEN, d), bf16)] + [jax.ShapeDtypeStruct((width, LEN), bf16)] * 3,
-        compiler_params=params(10),
+        compiler_params=params(20),
         cost_estimate=cost(2 * LEN * d * wide, 2 * (2 * LEN * d + wide * (d + LEN))),
         name="project",
-    )(core, *wait, *stay(patches), grid, tab, wt, bias_cols, gain, beta)
+    )(core, *stay(*wait), *stay(patches, grid, tab, wt, bias_cols), gain, beta)
 
 
 def key_range(ids_all, ids_blk):
@@ -288,7 +289,7 @@
         compiler_params=params(10),
         cost_estimate=cost(8 * LEN * LEN * width, 12 * LEN * width, heads * LEN * LEN),
         name="attend",
-    )(core, *wait, q, k, v, ids_rows, ids_rows, ids_cols)
+    )(core, *stay(*wait), q, k, v, ids_rows, ids_rows, ids_cols)
 
 
 def norm_two_kernel(c_ref, x_ref, *refs):
@@ -322,11 +323,11 @@
             + [whole(1, d)] * 3,
             out_specs=[blk, blk],
         ),
-        out_shape=[hbm((rows, d), f32), jax.ShapeDtypeStruct((rows, d), bf16)],
+        out_shape=[hbm((rows, d), f32), hbm((rows, d), bf16)],
         compiler_params=params(10),
         cost_estimate=cost(2 * len(ctxs) * rows * d * width, 12 * rows * d),
         name="norm_two",
-    )(core, *wait, *stay(patches), *ctxs, *wos, bias, gain, beta)
+    )(core, *stay(*wait), *stay(patches), *ctxs, *wos, bias, gain, beta)
 
 
 def store_halves(mine, outs, sums):
@@ -407,19 +408,19 @@
 
 def feed(seq, core, own, other, out_grad, up, up_bias, down, before=None, last=0, wait=()):
     d, units = up.shape
-    steps = LEN // RB
+    steps = LEN // FB
     half = steps // 2
     first = before is None
     whole = lambda *shape: pl.BlockSpec(shape, lambda i, c: (0,) * len(shape), pipeline_mode=pl.Buffered(1))
-    low = pl.BlockSpec((RB, d), lambda i, c: (jnp.minimum(i, half - 1), 0))
-    high = pl.BlockSpec((RB, d), lambda i, c: (jnp.maximum(i - half, 0), 0))
+    low = pl.BlockSpec((FB, d), lambda i, c: (jnp.minimum(i, half - 1), 0))
+    high = pl.BlockSpec((FB, d), lambda i, c: (jnp.maximum(i - half, 0), 0))
     blk = lambda i, c: seq * steps + lax.rem(i + half * (1 - c[0]), steps)
     in_specs = [ANY] * len(wait) + [
         high, low,
-        pl.BlockSpec((RB, d), lambda i, c: (blk(i, c), 0)),
+        pl.BlockSpec((FB, d), lambda i, c: (blk(i, c), 0)),
         whole(d, units), whole(1, units), whole(units, d),
     ]
-    args = [core, *wait, own, other, *stay(out_grad), up, up_bias, down]
+    args = [core, *stay(*wait), *stay(own), other, *stay(out_grad), up, up_bias, down]
     if not first:
         in_specs += [whole(8, d), whole(d, units), whole(units, d)]
         args += list(before)
@@ -444,9 +445,9 @@
                 pltpu.VMEM((1, d), f32),
             ],
         ),
-        out_shape=[hbm(rows.shape, bf16), hbm(rows.shape, bf16), rows, rows, hbm((8, d), f32)]
-        + [hbm(g, kind) for g in grads],
-        compiler_params=params(28),
+        out_shape=[hbm(rows.shape, bf16), hbm(rows.shape, bf16), hbm(rows.shape, bf16), rows, hbm((8, d), f32)]
+        + [(hbm if last else jax.ShapeDtypeStruct)(g, kind) for g in grads],
+        compiler_params=params(50),
         cost_estimate=cost(12 * LEN * d * units, 2 * LEN * d * 4 + 12 * d * units, 2 * LEN * units),
         name="feed",
     )(*args)
@@ -492,10 +493,10 @@
     vec = pl.BlockSpec((1, d), lambda i, c: (0, 0))
     small = pl.BlockSpec((8, d), lambda i, c: (0, 0))
     in_specs = [ANY] * len(wait) + [blk, blk, blk, pl.BlockSpec((RB, d), lambda i, c: ((2 * seq + c[0]) * steps + i, 0)), vec]
-    args = [core, *wait, mine, theirs, *stay(resid, out_grad), gain]
+    args = [core, *stay(*wait), mine, theirs, *stay(resid, out_grad), gain]
     if not first:
         in_specs.append(small)
-        args.append(before)
+        args += stay(before)
     return pl.pallas_call(
         ignoring(len(wait), functools.partial(norm_two_back_kernel, first)),
         grid_spec=pltpu.PrefetchScalarGridSpec(
@@ -512,31 +513,18 @@
     )(*args)
 
 
-def attend_back_kernel(first, pieces, c_ref, *refs):
+def attend_back_kernel(first, c_ref, *refs):
     refs = list(refs)
-    (own_ref, other_ref, q_ref, k_ref, v_ref, ctx_ref, lse_ref, idr_ref, idq_ref, idc_ref, wo_ref,
-     wt_ref, tab_ref, grid_ref, xhat_ref, gain_ref, beta_ref) = refs[:17]
-    refs = refs[17:]
-    if not first:
-        dwt0_ref, dwo0_ref, row0_ref, col0_ref, rope0_ref = refs[:5]
-        refs = refs[5:]
-    if pieces:
-        small_two_ref, small_feed_ref, send_ref, keep_ref, small_ref = refs[:5]
-        outs = refs[5:7]
-        bucket = refs[7]
-        refs = refs[8:]
-        keys, vals, dq, dk, dv, dwt_acc, dwo_acc, row_acc, col_acc, rope_acc = refs
-    else:
-        send_ref, keep_ref, dwt_acc, dwo_acc, row_acc, col_acc, rope_acc = refs[:7]
-        refs = refs[7:]
-        keys, vals, dq, dk, dv = refs
+    own_ref, other_ref, q_ref, k_ref, v_ref, ctx_ref, lse_ref, idr_ref, idq_ref, idc_ref, wo_ref = refs[:11]
+    refs = refs[11:]
+    dwo0_ref = None if first else refs.pop(0)
+    grads_ref, dwo_ref, keys, vals = refs
     step = pl.program_id(0)
-    steps = pl.num_programs(0) // 2
+    steps = pl.num_programs(0)
     half = steps // 2
     width = q_ref.shape[0]
     heads = width // HD
-    c = c_ref[0]
-    blk = lax.rem(step + half * (1 - c), steps)
+    blk = lax.rem(step + half * (1 - c_ref[0]), steps)
     here = pl.ds(pl.multiple_of(blk * RB, RB), RB)
 
     @pl.when(step == 0)
@@ -544,110 +532,42 @@
         for h in range(heads):
             keys[h] = jnp.transpose(rows_of(k_ref, h))
             vals[h] = jnp.transpose(rows_of(v_ref, h))
-        dq[...] = jnp.zeros_like(dq)
-        dk[...] = jnp.zeros_like(dk)
-        dv[...] = jnp.zeros_like(dv)
-        if first:
-            dwt_acc[...] = jnp.zeros_like(dwt_acc)
-            dwo_acc[...] = jnp.zeros_like(dwo_acc)
-            row_acc[...] = jnp.zeros_like(row_acc)
-            col_acc[...] = jnp.zeros_like(col_acc)
-            rope_acc[...] = jnp.zeros_like(rope_acc)
-        else:
-            dwt_acc[...] = dwt0_ref[...]
-            dwo_acc[...] = dwo0_ref[...]
-            row_acc[...] = row0_ref[...]
-            col_acc[...] = col0_ref[...]
-            rope_acc[...] = rope0_ref[...]
-
-    @pl.when(step < steps)
-    def _():
-        branch = jnp.where(step < half, other_ref[...], own_ref[...])
-        ctx = ctx_ref[:, here]
-        dctx = mm(wo_ref[...], branch, NT).astype(bf16)
-        dwo_acc[...] += mm(ctx.astype(bf16), branch)
-        prod = dctx.astype(f32) * ctx
-        lse = lse_ref[:, here]
-        ids_q = idq_ref[...]
-        lo, hi = key_range(idr_ref[...], ids_q)
-        parts = []
+        grads_ref[...] = jnp.zeros_like(grads_ref)
+        dwo_ref[...] = jnp.zeros_like(dwo_ref) if first else dwo0_ref[...]
+
+    branch = jnp.where(step < half, other_ref[...], own_ref[...])
+    ctx = ctx_ref[:, here]
+    dctx = mm(wo_ref[...], branch, NT).astype(bf16)
+    dwo_ref[...] += mm(ctx.astype(bf16), branch)
+    prod = dctx.astype(f32) * ctx
+    lse = lse_ref[:, here]
+    ids_q = idq_ref[...]
+    lo, hi = key_range(idr_ref[...], ids_q)
+    parts = []
+    for h in range(heads):
+        sl = slice(h * HD, (h + 1) * HD)
+        parts.append((q_ref[sl, here], dctx[sl], jnp.sum(prod[sl], axis=0, keepdims=True), lse[h : h + 1]))
+
+    def body(kb, carry):
+        at = pl.multiple_of(kb * KB, KB)
+        there = pl.ds(at, KB)
+        same = same_image(idc_ref, at, ids_q)
         for h in range(heads):
-            sl = slice(h * HD, (h + 1) * HD)
-            parts.append((q_ref[sl, here], dctx[sl], jnp.sum(prod[sl], axis=0, keepdims=True), lse[h : h + 1]))
-
-        def body(kb, carry):
-            at = pl.multiple_of(kb * KB, KB)
-            there = pl.ds(at, KB)
-            same = same_image(idc_ref, at, ids_q)
-            for h in range(heads):
-                sl = slice(h * HD, (h + 1) * HD)
-                q_h, do_h, delta, lse_h = parts[h]
-                s = mm(keys[h, there, :], q_h)
-                p = jnp.exp2(jnp.where(same, s * SCALE2 - lse_h, masked_score))
-                dp = mm(vals[h, there, :], do_h)
-                ds = (p * (dp - delta)).astype(bf16)
-                dq[sl, here] += mm(k_ref[sl, there], ds)
-                dk[sl, there] += mm(q_h, ds, NT)
-                dv[sl, there] += mm(do_h, p.astype(bf16), NT)
-            return carry
-
-        lax.fori_loop(lo, hi, body, 0)
-
-    @pl.when(step >= steps)
-    def _():
-        place = grid_ref[...]
-        cosine, sine = lookup(tab_ref, place)
-        pieces = []
-        angle = [None] * heads
-        for turned, grads in ((q_ref, dq), (k_ref, dk)):
-            for h in range(heads):
-                b = grads[h * HD : (h + 1) * HD, here] * SCALE
-                a = turned[h * HD : (h + 1) * HD, here].astype(f32)
-                b1, b2 = b[:HALF], b[HALF:]
-                co = cosine[h * HALF : (h + 1) * HALF]
-                si = sine[h * HALF : (h + 1) * HALF]
-                pieces.append((b1 * co + b2 * si).astype(bf16))
-                pieces.append((b2 * co - b1 * si).astype(bf16))
-                term = b2 * a[:HALF] - b1 * a[HALF:]
-                angle[h] = term if angle[h] is None else angle[h] + term
-        pieces.append(dv[:, here].astype(bf16))
-        mixed_grad = jnp.concatenate(pieces, axis=0)
-        angle = jnp.concatenate(angle, axis=0)
-        rope_acc[...] += lax.dot_general(
-            place.astype(f32), angle, NT, precision=lax.Precision.HIGHEST, preferred_element_type=f32
-        )
-        row_acc[...] += mm(jnp.ones((8, RB), bf16), mixed_grad, NT)
-        col_acc[...] += mm(mixed_grad, jnp.ones((RB, 128), bf16))
-        dwt_acc[...] += mm(mixed_grad, xhat_ref[...])
-        partial = mm(mixed_grad, wt_ref[...], TN).astype(bf16)
-
-        @pl.when(step < steps + half)
-        def _():
-            send_ref[...] = partial
-
-        @pl.when(step >= steps + half)
-        def _():
-            keep_ref[...] = partial
-
-    if pieces:
-        @pl.when(step == 2 * steps - 1)
-        def _():
-            raw = dwt_acc[...]
-            col = col_acc[:, 0:1]
-            wt = wt_ref[...].astype(f32)
-            bucket[...] = raw * gain_ref[...] + col * beta_ref[...]
-            store_halves(c_ref[1], outs, (bucket, dwo_acc))
-            small_ref[0:1, :] = jnp.sum(wt * raw, axis=0, keepdims=True)
-            small_ref[1:2, :] = jnp.sum(wt * col, axis=0, keepdims=True)
-            small_ref[2:5, :] = 0.5 * small_two_ref[0:3, :]
-            small_ref[5:7, :] = small_feed_ref[0:2, :]
-            small_ref[7:8, :] = jnp.concatenate(
-                [row_acc[0:1, :], rope_acc[1:2, :], rope_acc[0:1, :]], axis=1
-            )
-
-
-def attend_back(seq, core, own, other, q, k, v, ctx, lse, ids_rows, ids_cols, wo, wt, tab, grid, xhat,
-                gain, beta, before=None, pieces=0, small_two=None, small_feed=None, wait=()):
+            q_h, do_h, delta, lse_h = parts[h]
+            s = mm(keys[h, there, :], q_h)
+            p = jnp.exp2(jnp.where(same, s * SCALE2 - lse_h, masked_score))
+            dp = mm(vals[h, there, :], do_h)
+            ds = (p * (dp - delta)).astype(bf16)
+            at_q, at_k, at_v = (slice(k * width + h * HD, k * width + (h + 1) * HD) for k in range(3))
+            grads_ref[at_q, here] += mm(k_ref[h * HD : (h + 1) * HD, there], ds)
+            grads_ref[at_k, there] += mm(q_h, ds, NT)
+            grads_ref[at_v, there] += mm(do_h, p.astype(bf16), NT)
+        return carry
+
+    lax.fori_loop(lo, hi, body, 0)
+
+
+def attend_back(seq, core, own, other, q, k, v, ctx, lse, ids_rows, ids_cols, wo, before=None, wait=()):
     width, d = wo.shape
     heads = width // HD
     steps = LEN // RB
@@ -656,62 +576,157 @@
     whole = lambda *shape: pl.BlockSpec(shape, lambda i, c: (0,) * len(shape), pipeline_mode=pl.Buffered(1))
     blk = lambda i, c: lax.rem(i + half * (1 - c[0]), steps)
     in_specs = [ANY] * len(wait) + [
-        pl.BlockSpec((RB, d), lambda i, c: (jnp.clip(i - half, 0, half - 1), 0)),
+        pl.BlockSpec((RB, d), lambda i, c: (jnp.maximum(i - half, 0), 0)),
         pl.BlockSpec((RB, d), lambda i, c: (jnp.minimum(i, half - 1), 0)),
         whole(width, LEN), whole(width, LEN), whole(width, LEN), whole(width, LEN), whole(8, LEN),
         pl.BlockSpec((None, 1, LEN), lambda i, c: (seq, 0, 0)),
         pl.BlockSpec((None, 1, RB), lambda i, c: (seq, 0, blk(i, c))),
         pl.BlockSpec((LEN, 128), lambda i, c: (seq, 0)),
-        whole(width, d), whole(3 * width, d), whole(*tab.shape),
-        pl.BlockSpec((2, RB), lambda i, c: (0, seq * steps + blk(i, c))),
-        pl.BlockSpec((RB, d), lambda i, c: (jnp.where(i < steps, blk(0, c), blk(i, c)), 0)),
-        whole(1, d), whole(1, d),
+        whole(width, d),
     ]
-    args = [core, *wait, own, other, q, k, v, ctx, lse, ids_rows, ids_rows, ids_cols, wo, wt, tab, grid, xhat, gain, beta]
-    sums = [(3 * width, d), (width, d), (8, 3 * width), (3 * width, 128), (2, heads * HALF)]
+    q, k, v, ctx, lse, ids_cols = stay(q, k, v, ctx, lse, ids_cols)
+    args = [core, *stay(*wait), own, other, q, k, v, ctx, lse, ids_rows, ids_rows, ids_cols, wo]
     if not first:
-        in_specs += [whole(*s) for s in sums]
-        args += list(before)
-    if pieces:
-        in_specs += [whole(8, d)] * 2
-        args += [small_two, small_feed]
-    out_specs = [
-        pl.BlockSpec((RB, d), lambda i, c: (jnp.clip(i - steps, 0, half - 1), 0)),
-        pl.BlockSpec((RB, d), lambda i, c: (jnp.clip(i - steps - half, 0, half - 1), 0)),
-    ]
-    out_shape = [jax.ShapeDtypeStruct((LEN // 2, d), bf16)] * 2
-    scratch = [
-        pltpu.VMEM((heads, LEN, HD), bf16),
-        pltpu.VMEM((heads, LEN, HD), bf16),
-        pltpu.VMEM((width, LEN), f32),
-        pltpu.VMEM((width, LEN), f32),
-        pltpu.VMEM((width, LEN), f32),
-    ]
-    if pieces:
-        cut = (pieces, 4 * width // (2 * pieces), d)
-        out_specs += [whole(8, d), whole(*cut), whole(*cut)]
-        out_shape += [hbm((8, d), f32), hbm(cut, bf16), hbm(cut, bf16)]
-        scratch = [pltpu.VMEM((3 * width, d), f32)] + scratch + [pltpu.VMEM(s, f32) for s in sums]
-    else:
-        out_specs += [whole(*s) for s in sums]
-        out_shape += [hbm(s, f32) for s in sums]
-    return pl.pallas_call(
-        ignoring(len(wait), functools.partial(attend_back_kernel, first, pieces)),
+        in_specs.append(whole(width, d))
+        args += stay(before)
+    return pl.pallas_call(
+        ignoring(len(wait), functools.partial(attend_back_kernel, first)),
         grid_spec=pltpu.PrefetchScalarGridSpec(
-            num_scalar_prefetch=1, grid=(2 * steps,), in_specs=in_specs, out_specs=out_specs, scratch_shapes=scratch
-        ),
-        out_shape=out_shape,
-        compiler_params=params(28),
+            num_scalar_prefetch=1, grid=(steps,), in_specs=in_specs,
+            out_specs=[whole(3 * width, LEN), whole(width, d)],
+            scratch_shapes=[pltpu.VMEM((heads, LEN, HD), bf16), pltpu.VMEM((heads, LEN, HD), bf16)],
+        ),
+        out_shape=[hbm((3 * width, LEN), f32), hbm((width, d), f32)],
+        compiler_params=params(20),
         cost_estimate=cost(
-            20 * LEN * LEN * width + 20 * LEN * d * width, 2 * LEN * (6 * width + 3 * d) + 16 * d * width,
-            heads * LEN * LEN,
+            20 * LEN * LEN * width + 8 * LEN * d * width, 2 * LEN * (10 * width + d) + 8 * d * width, heads * LEN * LEN,
         ),
         name="attend_back",
     )(*args)
 
 
-def norm_one_back_kernel(m_ref, mine_ref, theirs_ref, x_ref, rg0_ref, rg1_ref, gain_ref, out_ref):
-    f = (mine_ref[...].astype(f32) + theirs_ref[...].astype(f32)) * gain_ref[...]
+def project_back_kernel(c_ref, *refs):
+    seqs = (refs[:4], refs[4:8])
+    (wt_ref, tab_ref, grid_ref, gain_ref, beta_ref, dwo_ref, small_two_ref, small_feed_ref) = refs[8:16]
+    send_away, keep_away, send_mine, keep_mine, small_ref = refs[16:21]
+    outs = refs[21:23]
+    dwt_acc, row_acc, col_acc, rope_acc = refs[23:]
+    step = pl.program_id(0)
+    steps = pl.num_programs(0) // 2
+    half = steps // 2
+    width = seqs[0][0].shape[0]
+    heads = width // HD
+    second = (step < steps) != (c_ref[2] > 0)
+
+    def pick(k):
+        return jnp.where(second, seqs[1][k][...], seqs[0][k][...])
+
+    @pl.when(step == 0)
+    def _():
+        for acc in (dwt_acc, row_acc, col_acc, rope_acc):
+            acc[...] = jnp.zeros_like(acc)
+
+    place = grid_ref[...]
+    cosine, sine = lookup(tab_ref, place)
+    grads = pick(2)
+    pieces = []
+    angle = [None] * heads
+    for k in range(2):
+        turned = pick(k)
+        for h in range(heads):
+            b = grads[k * width + h * HD : k * width + (h + 1) * HD] * SCALE
+            a = turned[h * HD : (h + 1) * HD].astype(f32)
+            b1, b2 = b[:HALF], b[HALF:]
+            co = cosine[h * HALF : (h + 1) * HALF]
+            si = sine[h * HALF : (h + 1) * HALF]
+            pieces.append((b1 * co + b2 * si).astype(bf16))
+            pieces.append((b2 * co - b1 * si).astype(bf16))
+            term = b2 * a[:HALF] - b1 * a[HALF:]
+            angle[h] = term if angle[h] is None else angle[h] + term
+    pieces.append(grads[2 * width :].astype(bf16))
+    mixed_grad = jnp.concatenate(pieces, axis=0)
+    angle = jnp.concatenate(angle, axis=0)
+    rope_acc[...] += lax.dot_general(
+        place.astype(f32), angle, NT, precision=lax.Precision.HIGHEST, preferred_element_type=f32
+    )
+    row_acc[...] += mm(jnp.ones((8, RB), bf16), mixed_grad, NT)
+    col_acc[...] += mm(mixed_grad, jnp.ones((RB, 128), bf16))
+    dwt_acc[...] += mm(mixed_grad, pick(3))
+    partial = mm(mixed_grad, wt_ref[...], TN).astype(bf16)
+    for k, out in enumerate((send_away, keep_away, send_mine, keep_mine)):
+        @pl.when(step // half == k)
+        def _():
+            out[...] = partial
+
+    @pl.when(step == 2 * steps - 1)
+    def _():
+        raw = dwt_acc[...]
+        col = col_acc[:, 0:1]
+        wt = wt_ref[...].astype(f32)
+        small_ref[0:1, :] = jnp.sum(wt * raw, axis=0, keepdims=True)
+        small_ref[1:2, :] = jnp.sum(wt * col, axis=0, keepdims=True)
+        small_ref[2:5, :] = 0.5 * small_two_ref[0:3, :]
+        small_ref[5:7, :] = small_feed_ref[0:2, :]
+        small_ref[7:8, :] = jnp.concatenate([row_acc[0:1, :], rope_acc[1:2, :], rope_acc[0:1, :]], axis=1)
+        dwt_acc[...] = raw * gain_ref[...] + col * beta_ref[...]
+        store_halves(c_ref[1], outs, (dwt_acc, dwo_ref))
+
+
+def project_back(core, seqs, wt, tab, grid, gain, beta, dwo, small_two, small_feed, pieces, wait=()):
+    d = wt.shape[1]
+    width = wt.shape[0] // 3
+    heads = width // HD
+    steps = LEN // RB
+    half = steps // 2
+    whole = lambda *shape: pl.BlockSpec(shape, lambda i, c: (0,) * len(shape), pipeline_mode=pl.Buffered(1))
+    blk = lambda i, c: lax.rem(lax.rem(i, steps) + half * (1 - c[0]), steps)
+    now = lambda i, c: jnp.where(i < steps, 1 - c[2], c[2])
+
+    def turn(s, i, c):
+        early = s == jnp.where(c[2] > 0, 0, 1)
+        rest = jnp.where(early, blk(steps - 1, c), blk(0, c))
+        return jnp.where(now(i, c) == s, blk(i, c), rest)
+
+    in_specs = [ANY] * len(wait)
+    args = [core, *stay(*wait)]
+    for s in range(2):
+        tall = lambda i, c, s=s: (0, turn(s, i, c))
+        flat = lambda i, c, s=s: (turn(s, i, c), 0)
+        in_specs += [
+            pl.BlockSpec((width, RB), tall), pl.BlockSpec((width, RB), tall), pl.BlockSpec((3 * width, RB), tall),
+            pl.BlockSpec((RB, d), flat),
+        ]
+        args += stay(*seqs[s])
+    in_specs += [
+        whole(3 * width, d), whole(*tab.shape),
+        pl.BlockSpec((2, RB), lambda i, c: (0, now(i, c) * steps + blk(i, c))),
+        whole(1, d), whole(1, d), whole(width, d), whole(8, d), whole(8, d),
+    ]
+    args += [wt, *stay(tab, grid), gain, beta, *stay(dwo, small_two, small_feed)]
+    part = lambda k: pl.BlockSpec((RB, d), lambda i, c: (jnp.clip(i - k * half, 0, half - 1), 0))
+    cut = (pieces, 4 * width // (2 * pieces), d)
+    rows = hbm((LEN // 2, d), bf16)
+    return pl.pallas_call(
+        ignoring(len(wait), project_back_kernel),
+        grid_spec=pltpu.PrefetchScalarGridSpec(
+            num_scalar_prefetch=1, grid=(2 * steps,), in_specs=in_specs,
+            out_specs=[part(0), part(1), part(2), part(3), whole(8, d), whole(*cut), whole(*cut)],
+            scratch_shapes=[
+                pltpu.VMEM((3 * width, d), f32),
+                pltpu.VMEM((8, 3 * width), f32),
+                pltpu.VMEM((3 * width, 128), f32),
+                pltpu.VMEM((2, heads * HALF), f32),
+            ],
+        ),
+        out_shape=[rows, rows, rows, rows, hbm((8, d), f32), hbm(cut, bf16), hbm(cut, bf16)],
+        compiler_params=params(28),
+        cost_estimate=cost(24 * LEN * d * width, 4 * LEN * (12 * width + 3 * d), LEN * width),
+        name="project_back",
+    )(*args)
+
+
+def norm_one_back_kernel(m_ref, mine_ref, got_ref, theirs_ref, x_ref, rg0_ref, rg1_ref, gain_ref, out_ref):
+    f = (mine_ref[...].astype(f32) + got_ref[...].astype(f32) + theirs_ref[...].astype(f32)) * gain_ref[...]
     xhat, inverse = standardize(x_ref[...].astype(f32))
     back = inverse * (
         f - jnp.mean(f, axis=-1, keepdims=True) - xhat * jnp.mean(f * xhat, axis=-1, keepdims=True)
@@ -720,7 +735,7 @@
     out_ref[...] = (rgrad + back).astype(bf16)
 
 
-def norm_one_back(place, mine, theirs, patches, rg0, rg1, gain):
+def norm_one_back(place, mine, got, theirs, patches, rg0, rg1, gain):
     rows, d = mine.shape
     steps = rows // RB
     blk = pl.BlockSpec((RB, d), lambda i, m: (i, 0))
@@ -730,7 +745,7 @@
             num_scalar_prefetch=1,
             grid=(steps,),
             in_specs=[
-                blk, blk, pl.BlockSpec((RB, d), lambda i, m: (m[0] * steps + i, 0)), blk, blk,
+                blk, blk, blk, pl.BlockSpec((RB, d), lambda i, m: (m[0] * steps + i, 0)), blk, blk,
                 pl.BlockSpec((1, d), lambda i, m: (0, 0)),
             ],
             out_specs=blk,
@@ -739,7 +754,7 @@
         compiler_params=params(12),
         cost_estimate=cost(20 * rows * d, 16 * rows * d),
         name="norm_one_back",
-    )(place, mine, theirs, *stay(patches, rg0, rg1), gain)
+    )(place, mine, got, theirs, *stay(patches, rg0, rg1), gain)
 
 
 CORE_SWAP = [(i, i ^ 1) for i in range(4)]
@@ -776,11 +791,11 @@
         grid_spec=pltpu.PrefetchScalarGridSpec(
             num_scalar_prefetch=1, grid=(1,), in_specs=[ANY] * len(wait) + [full(a.shape)] * 2, out_specs=full(a.shape),
         ),
-        out_shape=jax.ShapeDtypeStruct(a.shape, bf16),
+        out_shape=hbm(a.shape, bf16),
         compiler_params=params(12),
         cost_estimate=cost(a.size, 6 * a.size),
         name="add_parts",
-    )(core, *wait, a, b)
+    )(core, *stay(*wait), *stay(a), b)
 
 
 def sum_parts_kernel(c_ref, parts_ref, *refs):
@@ -816,7 +831,7 @@
         compiler_params=params(12),
         cost_estimate=cost(count * rows * d, 4 * count * rows * d),
         name="sum_parts",
-    )(core, *wait, parts, *extra)
+    )(core, *stay(*wait), parts, *extra)
 
 
 def place_parts_kernel(with_small, c_ref, mine_ref, theirs_ref, *refs):
@@ -853,28 +868,6 @@
     )(core, mine, theirs)
 
 
-def place_all_kernel(parts_ref, *outs):
-    count = parts_ref.shape[0]
-    for k in range(count):
-        piece = (k % 2) * (count // 2) + k // 2
-        at = 0
-        for out in outs:
-            rows = out.shape[0] // count
-            out[piece * rows : (piece + 1) * rows, :] = parts_ref[k, at : at + rows, :].astype(f32)
-            at += rows
-
-
-def place_all(parts, splits):
-    d = parts.shape[2]
-    return pl.pallas_call(
-        place_all_kernel,
-        out_shape=[jax.ShapeDtypeStruct((rows, d), f32) for rows in splits],
-        compiler_params=pltpu.CompilerParams(vmem_limit_bytes=20 * 1024 * 1024),
-        cost_estimate=cost(sum(splits) * d, 6 * sum(splits) * d),
-        name="place_all",
-    )(parts)
-
-
 def half_swap(value):
     return lax.ppermute(value, "dp", [(i, i ^ 1) for i in range(lax.axis_size("dp"))])
 
@@ -901,7 +894,7 @@
     units = up_weight.shape[1]
     place = lax.axis_index("mp").astype(jnp.int32)
     half = lax.axis_index("dp").astype(jnp.int32) % 2 if tree else jnp.int32(0)
-    core = jnp.stack([place % 2, half])
+    core = jnp.stack([place % 2, half, place // 2])
     place_arr = place.reshape(1)
     far = place >= 2
     row = lambda v: v.reshape(1, -1)
@@ -918,23 +911,25 @@
     made0 = project(0, core, *proj_args)
     send0, keep0, ctx0, lse0 = attend(0, core, *made0[1:], ids_rows, ids_cols)
     core0, far_keep0 = core_swap(send0), chip_swap(keep0)
-    made1 = project(1, core, *proj_args, wait=[keep0, wo_core])
+    made1 = project(1, core, *proj_args, wait=[lse0, wo_core])
     far_core0, wo_far = chip_swap(core0), chip_swap(out_weight)
-    send1, keep1, ctx1, lse1 = attend(1, core, *made1[1:], ids_rows, ids_cols, wait=[core0, far_keep0])
+    send1, keep1, ctx1, lse1 = attend(1, core, *made1[1:], ids_rows, ids_cols, wait=[made1[0]])
     core1, far_keep1 = core_swap(send1), chip_swap(keep1)
     wos = [out_weight, wo_core, wo_far, core_swap(wo_far)]
     norm_args = (row(out_bias), gain2, beta2)
     resid0, normed0 = norm_two(
-        0, core, patches, [keep0, core0, far_keep0, far_core0], wos, *norm_args, wait=[keep1]
-    )
+        0, core, patches, [keep0, core0, far_keep0, far_core0], wos, *norm_args, wait=[lse1]
+    )
+    normed0, core1, far_keep1 = hold([normed0, core1, far_keep1])
     far_core1 = chip_swap(core1)
     feed_args = (out_grad, up_weight, row(up_bias), down_weight)
     mlp_send0, mlp_keep0, n2_send0, n2_keep0, *sums = feed(
-        0, core, normed0, core_swap(normed0), *feed_args, wait=[core1, far_keep1]
-    )
+        0, core, normed0, core_swap(normed0), *feed_args
+    )
+    n2_send0, far_core1 = hold([n2_send0, far_core1])
     n20 = add_low(n2_keep0, core_swap(n2_send0))
     resid1, normed1 = norm_two(
-        1, core, patches, [keep1, core1, far_keep1, far_core1], wos, *norm_args, wait=[n2_keep0]
+        1, core, patches, [keep1, core1, far_keep1, far_core1], wos, *norm_args, wait=[sums[0]]
     )
     n2_far0 = chip_swap(n20)
     mlp_send1, mlp_keep1, n2_send1, n2_keep1, small_feed, feed_send, feed_keep = feed(
@@ -947,47 +942,52 @@
     mlp1 = add_low(mlp_keep1, core_swap(mlp_send1))
     mlp_away, mlp_mine = jnp.where(far, mlp0, mlp1), jnp.where(far, mlp1, mlp0)
     rgrad0, branch0, small_two = norm_two_back(
-        0, core, n20, n2_far0, resid0, out_grad, gain2, wait=[n2_keep1]
+        0, core, n20, n2_far0, resid0, out_grad, gain2, wait=[small_feed]
     )
     n2_far1 = chip_swap(n21)
-    shared_args = (ids_rows, ids_cols, out_weight, wt, tab, patch_grid)
-    n1_send0, n1_keep0, *sums = attend_back(
-        0, core, branch0, core_swap(branch0), *made0[1:], ctx0, lse0, *shared_args, made0[0], gain1, beta1,
-        wait=[n21],
-    )
-    n1_core0 = core_swap(n1_send0)
-    after_first = [n1_keep0]
+    grads0, dwo = attend_back(
+        0, core, branch0, core_swap(branch0), *made0[1:], ctx0, lse0, ids_rows, ids_cols, out_weight, wait=[n21]
+    )
+    event = dwo
     if tree:
-        feed_part = add_parts(core, feed_keep, feed_got, wait=[n1_keep0])
-        after_first = [feed_part]
+        feed_part = add_parts(core, feed_keep, feed_got, wait=[dwo, n2_far1])
+        event = feed_part
         feed_got = quarter_trade(feed_part)
     rgrad1, branch1, small_two = norm_two_back(
-        1, core, n21, n2_far1, resid1, out_grad, gain2, before=small_two, wait=after_first
-    )
+        1, core, n21, n2_far1, resid1, out_grad, gain2, before=small_two, wait=[event]
+    )
+    grads1, dwo = attend_back(
+        1, core, branch1, core_swap(branch1), *made1[1:], ctx1, lse1, ids_rows, ids_cols, out_weight, before=dwo,
+        wait=[mlp_away],
+    )
+    event = dwo
+    if tree:
+        feed_sum = sum_parts(core, feed_got, wait=[dwo])
+        event = feed_sum
+        feed_all = quarter_trade(feed_sum)
     mlp_theirs = chip_swap(mlp_away)
-    n1_send1, n1_keep1, *sums = attend_back(
-        1, core, branch1, core_swap(branch1), *made1[1:], ctx1, lse1, *shared_args, made1[0], gain1, beta1,
-        before=sums, pieces=pieces, small_two=small_two, small_feed=small_feed, wait=[n1_core0, mlp_away],
-    )
-    small, grad_send, grad_keep = hold(sums, mlp_theirs)
-    halves = [add_low(n1_keep0, n1_core0), add_low(n1_keep1, core_swap(n1_send1))]
+    n1_send_away, n1_away, n1_send, n1_keep, small, grad_send, grad_keep = project_back(
+        core, [(*made[1:3], grads, made[0]) for made, grads in ((made0, grads0), (made1, grads1))],
+        wt, tab, patch_grid, gain1, beta1, dwo, small_two, small_feed, pieces, wait=[event],
+    )
+    n1_send_away, small, grad_send, mlp_theirs = hold([n1_send_away, small, grad_send, mlp_theirs])
+    n1_away = add_low(n1_away, core_swap(n1_send_away))
+    n1_got = core_swap(n1_send)
     shared = lax.broadcasted_iota(jnp.int32, small.shape, 0) < 5
     for swap in (core_swap, chip_swap):
         small = small + jnp.where(shared, swap(small), 0.0)
-    away = after(jnp.where(far, halves[0], halves[1]), small)
-    mine = jnp.where(far, halves[1], halves[0])
-    theirs = chip_swap(away)
+    theirs = chip_swap(after(n1_away, small))
     if tree:
         grad_got = half_swap(grad_send)
-        feed_all = lax.all_gather(sum_parts(core, feed_got, copies=1, wait=[grad_keep]), "dp", axis=0, tiled=True)
-        grad_got = quarter_trade(add_parts(core, grad_keep, grad_got))
+        grad_got = quarter_trade(add_parts(core, grad_keep, grad_got, wait=[feed_all]))
+        feed_other = half_swap(feed_all)
         grad_sum = quarter_trade(sum_parts(core, grad_got, small))
         grad_other = half_swap(grad_sum)
     else:
         small, grad_send, grad_keep, feed_send, feed_keep = lax.psum(
             (small, grad_send, grad_keep, feed_send, feed_keep), "dp"
         )
-        feed_all = jnp.concatenate([feed_keep, feed_send])
+        feed_all, feed_other = feed_keep, feed_send
         grad_sum = sum_parts(core, grad_keep, small)
         grad_other = sum_parts(core, grad_send, jnp.zeros_like(small))
 
@@ -996,8 +996,8 @@
         + (mlp_mine.astype(f32) + mlp_theirs.astype(f32))
         + row(down_bias)
     ).astype(bf16)
-    grad_rows = norm_one_back(place_arr, mine, theirs, patches, rgrad0, rgrad1, gain1)
-    up_grad, down_grad = place_all(feed_all, (d, units))
+    grad_rows = norm_one_back(place_arr, n1_keep, n1_got, theirs, patches, rgrad0, rgrad1, gain1)
+    up_grad, down_grad = place_parts(core, feed_all, feed_other, (d, units))
     (grad_other,) = hold([grad_other], grad_rows)
     qkv_grad, out_grad_w, small = place_parts(core, grad_sum, grad_other, (3 * width, width), True)
     turns = heads * HALF

time: 292 us -> 268 us (0.918)
  waiting for transfers between devices: 88.8 us -> 66.9 us
  between operations: 14.6 us -> 0.99 us
  Pallas kernels: 129 us -> 142 us
  local copies, waits for them, and re-layouts: 17.2 us -> 8.05 us
  starting transfers between devices: 30.6 us -> 38.5 us
    pallas_call x1, Pallas kernels: 2.47 us -> 16.2 us  [project_back(): pl.pallas_call(ignoring(len(wait), project_back_kernel), grid_spec=pltpu....]
    all_to_all x3 -> x4, waiting for transfers between devices: 35 us -> 25.3 us  [quarter_trade(): lax.all_to_all(parts, 'dp', 0, 0, axis_index_groups=[[0, 2, 4, 6], [1, 3,...]
    unnamed x104 -> x64, local copies, waits for them, and re-layouts: 13.9 us -> 4.74 us
    ppermute x10, waiting for transfers between devices: 18.7 us -> 10.1 us  [chip_swap(): return lax.ppermute(value, 'mp', CHIP_SWAP)]
    pallas_call x2, Pallas kernels: 40.5 us -> 33.1 us  [attend_back(): pl.pallas_call(ignoring(len(wait), functools.partial(attend_back_kernel,...]
    all_to_all x3 -> x4, starting transfers between devices: 14.6 us -> 21.9 us  [quarter_trade(): lax.all_to_all(parts, 'dp', 0, 0, axis_index_groups=[[0, 2, 4, 6], [1, 3,...]
    ppermute x3 -> x4, waiting for transfers between devices: 30.8 us -> 26 us  [half_swap(): lax.ppermute(value, 'dp', [(i, i ^ 1) for i in range(lax.axis_size('dp'))])]
    pallas_call x1 -> x2, Pallas kernels: 2.09 us -> 5.1 us  [place_parts(): pl.pallas_call(functools.partial(place_parts_kernel, with_small), grid_sp...]
  transfers between devices with their start and end apart: 32 -> 33, of which waited for: 14 -> 18; matrix products, arithmetic and copies ran while one was open for 5% -> 4% of each run, Pallas kernels for 37% -> 50%
where the time goes in v2:
time: 268 us; the launch traced here: 267 us
  Pallas kernels  142 us (53%)
  waiting for transfers between devices  66.9 us (25%)
  starting transfers between devices  38.5 us (14%)
  other arithmetic  10.9 us (4%)
  local copies, waits for them, and re-layouts  8.05 us (3%)
    pallas_call x2, Pallas kernels, attend_back(): pl.pallas_call(ignoring(len(wait), functools.partial(attend_back_kernel,...  33.1 us
    pallas_call x2, Pallas kernels, feed(): pl.pallas_call(ignoring(len(wait), functools.partial(feed_kernel, first,...  28.5 us
    ppermute x4, waiting for transfers between devices, half_swap(): lax.ppermute(value, 'dp', [(i, i ^ 1) for i in range(lax.axis_size('dp'))])  26 us
    all_to_all x4, waiting for transfers between devices, quarter_trade(): lax.all_to_all(parts, 'dp', 0, 0, axis_index_groups=[[0, 2, 4, 6], [1, 3,...  25.3 us
    all_to_all x4, starting transfers between devices, quarter_trade(): lax.all_to_all(parts, 'dp', 0, 0, axis_index_groups=[[0, 2, 4, 6], [1, 3,...  21.9 us
    pallas_call x2, Pallas kernels, attend(): pl.pallas_call(ignoring(len(wait), attend_kernel), grid_spec=pltpu.Prefet...  16.9 us
    pallas_call x1, Pallas kernels, project_back(): pl.pallas_call(ignoring(len(wait), project_back_kernel), grid_spec=pltpu....  16.2 us
    ppermute x10, starting transfers between devices, chip_swap(): return lax.ppermute(value, 'mp', CHIP_SWAP)  10.6 us
  transfers between devices with their start and end apart: 33, of which 18 were waited for; matrix products, arithmetic and copies ran while one was open for 4% of the time, Pallas kernels for 50%

profile of v2, /device:TPU:0, one launch (start us, length us, event | category | flops | bytes accessed | tf_op | source)
XLA Modules:
  0.0 266.8 jit_solution(11092857912727603214)
XLA Ops:
  1.2 2.6 collective-permute-start.4
  3.8 0.7 reshape.64.refs_5_.refs_7_.refs_12_.gain_ref
  4.5 0.7 reshape.65.refs_6_.refs_8_.refs_13_
  5.2 2.1 prepare.1
  7.3 4.9 %project.2 = (bf16[1024,768]{1,0:T(8,128)(2,1)}, bf16[192,1024]{1,0:T(8,128)(2,1)S(1)}, bf16[192,1024]{1,0:T(8,128)(2,1)S(1)}, bf16[192,1024]{1,0:T(8,128)(2,1)S(1)}) custom-call(s32[3]{0:T(128)S(1)} %pad_add_fusion.c_ref, bf16[2048,768]{1,0:T(8,128)(2,1)} %x_ref.1, s32[2,2048]{1,0:T(2,128)} %refs_11_.5, ...), custom_call_target="tpu_custom_call" | custom-call | flops 226492416 | bytes 1302528 | tf_op jit(solution)/shard_map/project/pallas_call | solution.py:152
  12.5 8.5 %attend.2 = (bf16[192,512]{1,0:T(8,128)(2,1)S(1)}, bf16[192,512]{1,0:T(8,128)(2,1)S(1)}, f32[192,1024]{1,0:T(8,128)}, f32[8,1024]{1,0:T(8,128)}) custom-call(s32[3]{0:T(128)S(1)} %pad_add_fusion.c_ref, bf16[192,1024]{1,0:T(8,128)(2,1)S(1)} %get-tuple-element.86.refs_0_.refs_3_.refs_1_, bf16[192,1024]{1,0:T(8,128)(2,1)S(1)} %get-tuple-element.87.refs_1_.refs_4_.refs_2_, ...), custom_call_target="tpu_custom_call" | custom-call | flops 402653184 | bytes 589824 | tf_op jit(solution)/shard_map/attend/pallas_call | solution.py:257
  21.7 0.9 collective-permute-done.1.refs_3_
  22.6 1.1 collective-permute-start.3
  23.7 0.7 copy-done.17
  24.4 4.9 %project.3 = (bf16[1024,768]{1,0:T(8,128)(2,1)}, bf16[192,1024]{1,0:T(8,128)(2,1)S(1)}, bf16[192,1024]{1,0:T(8,128)(2,1)S(1)}, bf16[192,1024]{1,0:T(8,128)(2,1)S(1)}) custom-call(s32[3]{0:T(128)S(1)} %pad_add_fusion.c_ref, f32[8,1024]{1,0:T(8,128)} %get-tuple-element.89.refs_0_.refs_7_, bf16[192,768]{1,0:T(8,128)(2,1)} %copy-done.17, ...), custom_call_target="tpu_custom_call" | custom-call | flops 226492416 | bytes 1302528 | tf_op jit(solution)/shard_map/project/pallas_call | solution.py:152
  29.4 8.4 %attend.3 = (bf16[192,512]{1,0:T(8,128)(2,1)S(1)}, bf16[192,512]{1,0:T(8,128)(2,1)S(1)}, f32[192,1024]{1,0:T(8,128)}, f32[8,1024]{1,0:T(8,128)}) custom-call(s32[3]{0:T(128)S(1)} %pad_add_fusion.c_ref, bf16[1024,768]{1,0:T(8,128)(2,1)} %get-tuple-element.90.refs_0_.refs_8_, bf16[192,1024]{1,0:T(8,128)(2,1)S(1)} %get-tuple-element.91.refs_1_.refs_3_.refs_5_, ...), custom_call_target="tpu_custom_call" | custom-call | flops 402653184 | bytes 589824 | tf_op jit(solution)/shard_map/attend/pallas_call | solution.py:257
  37.9 1.0 collective-permute-start.7
  39.1 4.4 %norm_two.2 = (f32[512,768]{1,0:T(8,128)}, bf16[512,768]{1,0:T(8,128)(2,1)}) custom-call(s32[3]{0:T(128)S(1)} %pad_add_fusion.c_ref, f32[8,1024]{1,0:T(8,128)} %get-tuple-element.94.refs_0_.refs_7_, bf16[2048,768]{1,0:T(8,128)(2,1)} %x_ref.1, bf16[192,512]{1,0:T(8,128)(2,1)S(1)} %get-tuple-element.95.refs_2_, ...), custom_call_target="tpu_custom_call" | custom-call | flops 150994944 | bytes 1179648 | tf_op jit(solution)/shard_map/norm_two/pallas_call | solution.py:314
  43.5 1.8 collective-permute-done.7.refs_4_
  45.3 1.0 collective-permute-start.9
  46.2 1.5 collective-permute-done.8.refs_1_
  47.8 13.9 %feed.2 = (bf16[512,768]{1,0:T(8,128)(2,1)}, bf16[512,768]{1,0:T(8,128)(2,1)}, bf16[512,768]{1,0:T(8,128)(2,1)}, bf16[512,768]{1,0:T(8,128)(2,1)S(1)}, f32[8,768...) custom-call(s32[3]{0:T(128)S(1)} %pad_add_fusion.c_ref, bf16[512,768]{1,0:T(8,128)(2,1)} %get-tuple-element.100.refs_0_, ...), custom_call_target="tpu_custom_call" | custom-call | flops 1811939328 | bytes 3342336 | tf_op jit(solution)/shard_map/feed/pallas_call | solution.py:434
  61.9 4.2 %norm_two.3 = (f32[512,768]{1,0:T(8,128)}, bf16[512,768]{1,0:T(8,128)(2,1)}) custom-call(s32[3]{0:T(128)S(1)} %pad_add_fusion.c_ref, f32[8,768]{1,0:T(8,128)} %get-tuple-element.101.refs_0_.refs_7_, bf16[2048,768]{1,0:T(8,128)(2,1)} %x_ref.1, bf16[192,512]{1,0:T(8,128)(2,1)S(1)} %get-tuple-element.99.refs_2_, ...), custom_call_target="tpu_custom_call" | custom-call | flops 150994944 | bytes 1179648 | tf_op jit(solution)/shard_map/norm_two/pallas_call | solution.py:314
  66.7 1.0 collective-permute-start.15
  67.8 0.9 collective-permute-done.11.refs_2_
  68.6 14.6 %feed.3 = (bf16[512,768]{1,0:T(8,128)(2,1)}, bf16[512,768]{1,0:T(8,128)(2,1)}, bf16[512,768]{1,0:T(8,128)(2,1)}, bf16[512,768]{1,0:T(8,128)(2,1)S(1)}, f32[8,768...) custom-call(s32[3]{0:T(128)S(1)} %pad_add_fusion.c_ref, bf16[512,768]{1,0:T(8,128)(2,1)} %copy-done.4, ...), custom_call_target="tpu_custom_call" | custom-call | flops 1811939328 | bytes 3342336 | tf_op jit(solution)/shard_map/feed/pallas_call | solution.py:434
  83.6 1.5 collective-permute-start.18
  85.1 1.3 collective-permute-done.15.refs_2_
  86.4 1.1 copy-done.5
  87.5 4.2 %norm_two_back.2 = (f32[512,768]{1,0:T(8,128)}, bf16[512,768]{1,0:T(8,128)(2,1)S(1)}, f32[8,768]{1,0:T(8,128)}) custom-call(s32[3]{0:T(128)S(1)} %pad_add_fusion.c_ref, f32[8,768]{1,0:T(8,128)} %get-tuple-element.119.refs_0_.refs_16_, bf16[512,768]{1,0:T(8,128)(2,1)S(1)} %copy-done.5, bf16[512,768]{1,0:T(8,128)(2,1)S(1)} %collective-permute-done.15.refs_2_, ...), custom_call_target="tpu_custom_call" | custom-call | flops 1966080 | bytes 1572864 | tf_op jit(solution)/shard_map/norm_two_back/pallas_call | solution.py:500
  91.9 1.0 collective-permute-start.17
  93.0 1.0 collective-permute-done.16.refs_2_
  94.0 16.4 %attend_back.2 = (f32[576,1024]{1,0:T(8,128)}, f32[192,768]{1,0:T(8,128)}) custom-call(s32[3]{0:T(128)S(1)} %pad_add_fusion.c_ref, bf16[512,768]{1,0:T(8,128)(2,1)} %copy-done.6, bf16[512,768]{1,0:T(8,128)(2,1)S(1)} %get-tuple-element.120.refs_1_, bf16[512,768]{1,0:T(8,128)(2,1)S(1)} %collective-permute-done.16.refs_2_, bf16[192,1024]{1,0:T(8,128)(2,1)} %copy-done.11, ...), custom_call_target="tpu_custom_call" | custom-call | flops 1308622848 | bytes 1671168 | tf_op jit(solution)/shard_map/attend_back/pallas_call | solution.py:592
  110.4 1.5 collective-permute-done.18.refs_3_
  111.9 0.9 copy-done.15
  112.8 3.1 %add_parts.2.refs_0_ = bf16[4,192,768]{2,1,0:T(8,128)(2,1)} custom-call(s32[3]{0:T(128)S(1)} %pad_add_fusion.c_ref, f32[192,768]{1,0:T(8,128)} %get-tuple-element.122.refs_0_.refs_12_, bf16[512,768]{1,0:T(8,128)(2,1)} %copy-done.15, bf16[4,192,768]{2,1,0:T(8,128)(2,1)} %get-tuple-element.123.refs_2_, bf16[4,192,768]{2,1,0:T(8,128)(2,1)S(1)} %collective-permute-done.18.refs_3_), custom_call_target="tpu_custom_call" | custom-call | flops 147456 | bytes 884736 | tf_op jit(solution)/shard_map/add_parts/pallas_call | solution.py:789
  115.9 7.0 %all-to-all-start = ((bf16[4,192,768]{2,1,0:T(8,128)(2,1)}), bf16[4,192,768]{2,1,0:T(8,128)(2,1)S(1)}, u32[]{:S(2)}, u32[]{:S(2)}) async-start(bf16[4,192,768]{2,1,0:T(8,128)(2,1)} %add_parts.2.refs_0_), calls=%async_computation | async-start | bytes 2359296 | tf_op jit(solution)/shard_map/all_to_all | solution.py:876
  123.5 4.3 %norm_two_back.3 = (f32[512,768]{1,0:T(8,128)}, bf16[512,768]{1,0:T(8,128)(2,1)}, f32[8,768]{1,0:T(8,128)}) custom-call(s32[3]{0:T(128)S(1)} %pad_add_fusion.c_ref, bf16[4,192,768]{2,1,0:T(8,128)(2,1)} %add_parts.2.refs_0_, bf16[512,768]{1,0:T(8,128)(2,1)S(1)} %copy-done.7, bf16[512,768]{1,0:T(8,128)(2,1)S(1)} %copy-done.16, ...), custom_call_target="tpu_custom_call" | custom-call | flops 1966080 | bytes 1572864 | tf_op jit(solution)/shard_map/norm_two_back/pallas_call | solution.py:500
  127.8 3.1 %broadcast_select_fusion.refs_0_ = bf16[512,768]{1,0:T(8,128)(2,1)} fusion(pred[]{:T(512)S(6)} %ge.3, bf16[512,768]{1,0:T(8,128)(2,1)} %collective-permute-done.12, bf16[512,768]{1,0:T(8,128)(2,1)} %get-tuple-element.113, bf16[512,768]{1,0:T(8,128)(2,1)} %collective-permute-done.13, bf16[512,768]{1,0:T(8,128)(2,1)} %get-tuple-element.115), kind=kLoop, calls=%fused_computation.6 | loop fusion | flops 3538944 | bytes 3932161 | tf_op jit(solution)/shard_map/jit(_where)/select_n | solution.py:943
  131.0 16.7 %attend_back.3 = (f32[576,1024]{1,0:T(8,128)}, f32[192,768]{1,0:T(8,128)}) custom-call(s32[3]{0:T(128)S(1)} %pad_add_fusion.c_ref, bf16[512,768]{1,0:T(8,128)(2,1)} %broadcast_select_fusion.refs_0_, bf16[512,768]{1,0:T(8,128)(2,1)} %get-tuple-element.126.refs_1_, bf16[512,768]{1,0:T(8,128)(2,1)S(1)} %collective-permute-done.19.refs_2_, ...), custom_call_target="tpu_custom_call" | custom-call | flops 1308622848 | bytes 1671168 | tf_op jit(solution)/shard_map/attend_back/pallas_call | solution.py:592
  147.7 3.7 %all-to-all-done.refs_1_ = bf16[4,192,768]{2,1,0:T(8,128)(2,1)S(1)} async-done(((bf16[4,192,768]{2,1,0:T(8,128)(2,1)}), bf16[4,192,768]{2,1,0:T(8,128)(2,1)S(1)}, u32[]{:S(2)}, u32[]{:S(2)}) %all-to-all-start) | async-done | bytes 1179680 | tf_op jit(solution)/shard_map/all_to_all | solution.py:876
  151.4 1.7 sum_parts.2.refs_0_
  153.1 6.7 %all-to-all-start.1 = ((bf16[4,192,768]{2,1,0:T(8,128)(2,1)}), bf16[4,192,768]{2,1,0:T(8,128)(2,1)S(1)}, u32[]{:S(2)}, u32[]{:S(2)}) async-start(bf16[4,192,768]{2,1,0:T(8,128)(2,1)} %sum_parts.2.refs_0_), calls=%async_computation.1 | async-start | bytes 2359296 | tf_op jit(solution)/shard_map/all_to_all | solution.py:876
  159.8 0.9 collective-permute-start.20
  160.8 16.2 %project_back.1 = (bf16[512,768]{1,0:T(8,128)(2,1)}, bf16[512,768]{1,0:T(8,128)(2,1)}, bf16[512,768]{1,0:T(8,128)(2,1)}, bf16[512,768]{1,0:T(8,128)(2,1)}, f32[8...) custom-call(s32[3]{0:T(128)S(1)} %pad_add_fusion.c_ref, ...), custom_call_target="tpu_custom_call" | custom-call | flops 905969664 | bytes 4718592 | tf_op jit(solution)/shard_map/project_back/pallas_call | solution.py:709
  176.9 2.5 collective-permute-done.20
  179.4 0.9 copy-done.25
  180.3 13.9 %collective-permute-done.26.refs_2_ = bf16[4,96,768]{2,1,0:T(8,128)(2,1)S(1)} collective-permute-done((bf16[4,96,768]{2,1,0:T(8,128)(2,1)}, bf16[4,96,768]{2,1,0:T(8,128)(2,1)S(1)}, u32[]{:S(2)}, u32[]{:S(2)}) %collective-permute-start.26) | collective-permute-done | bytes 589856 | tf_op jit(solution)/shard_map/ppermute | solution.py:872
  194.2 1.0 copy-done.1
  195.3 2.6 add_parts.3
  197.8 4.5 %all-to-all-start.2 = ((bf16[4,96,768]{2,1,0:T(8,128)(2,1)}), bf16[4,96,768]{2,1,0:T(8,128)(2,1)S(1)}, u32[]{:S(2)}, u32[]{:S(2)}) async-start(bf16[4,96,768]{2,1,0:T(8,128)(2,1)} %add_parts.3), calls=%async_computation.2 | async-start | bytes 1179648 | tf_op jit(solution)/shard_map/all_to_all | solution.py:876
  202.3 1.2 collective-permute-done.23
  203.6 0.9 collective-permute-start.24
  204.5 2.9 %collective-permute-done.24 = f32[8,768]{1,0:T(8,128)S(1)} collective-permute-done((f32[8,768]{1,0:T(8,128)S(1)}, f32[8,768]{1,0:T(8,128)S(1)}, u32[]{:S(2)}, u32[]{:S(2)}) %collective-permute-start.24) | collective-permute-done | bytes 24608 | tf_op jit(solution)/shard_map/ppermute | solution.py:769
  207.5 9.0 %all-to-all-done.2.refs_0_ = bf16[4,96,768]{2,1,0:T(8,128)(2,1)S(1)} async-done(((bf16[4,96,768]{2,1,0:T(8,128)(2,1)}), bf16[4,96,768]{2,1,0:T(8,128)(2,1)S(1)}, u32[]{:S(2)}, u32[]{:S(2)}) %all-to-all-start.2) | async-done | bytes 589856 | tf_op jit(solution)/shard_map/all_to_all | solution.py:876
  216.5 1.5 sum_parts.3
  217.9 3.6 %all-to-all-start.3 = ((bf16[4,112,768]{2,1,0:T(8,128)(2,1)}), bf16[4,112,768]{2,1,0:T(8,128)(2,1)S(1)}, u32[]{:S(2)}, u32[]{:S(2)}) async-start(bf16[4,112,768]{2,1,0:T(8,128)(2,1)} %sum_parts.3), calls=%async_computation.3 | async-start | bytes 1376256 | tf_op jit(solution)/shard_map/all_to_all | solution.py:876
  222.2 2.4 add_convert_fusion
  224.7 0.9 collective-permute-start.25
  225.6 12.6 %all-to-all-done.3.mine_ref = bf16[4,112,768]{2,1,0:T(8,128)(2,1)S(1)} async-done(((bf16[4,112,768]{2,1,0:T(8,128)(2,1)}), bf16[4,112,768]{2,1,0:T(8,128)(2,1)S(1)}, u32[]{:S(2)}, u32[]{:S(2)}) %all-to-all-start.3) | async-done | bytes 688160 | tf_op jit(solution)/shard_map/all_to_all | solution.py:876
  238.2 1.1 collective-permute-start.27
  239.3 4.1 %add_convert_fusion.1 = bf16[512,768]{1,0:T(8,128)(2,1)} fusion(bf16[512,768]{1,0:T(8,128)(2,1)} %copy-done.25, f32[512,768]{1,0:T(8,128)} %get-tuple-element.106.refs_3_, f32[512,768]{1,0:T(8,128)} %get-tuple-element.107.refs_3_, f32[768]{0:T(1024)S(1)} %copy-done.27, pred[]{:T(512)S(6)} %ge.3, bf16[512,768]{1,0:T(8,128)(2,1)} %collective-permute-done.12, ...), kind=kLoop, calls=%fused_computation.1 | loop fusion | flops 6291456 | bytes 7867393 | tf_op jit(solution)/shard_map/convert_element_type | solution.py:998
  243.4 1.5 collective-permute-done.25.theirs_ref
  244.9 3.9 %norm_one_back.1 = bf16[512,768]{1,0:T(8,128)(2,1)} custom-call(s32[1]{0:T(128)} %bitcast.7.m_ref, bf16[512,768]{1,0:T(8,128)(2,1)S(1)} %copy-done.21, bf16[512,768]{1,0:T(8,128)(2,1)} %collective-permute-done.21.got_ref, bf16[512,768]{1,0:T(8,128)(2,1)} %collective-permute-done.25.theirs_ref, bf16[2048,768]{1,0:T(8,128)(2,1)} %x_ref.1, ...), custom_call_target="tpu_custom_call" | custom-call | flops 1966080 | bytes 1572864 | tf_op jit(solution)/shard_map/norm_one_back/pallas_call | solution.py:742
  248.9 1.7 collective-permute-done.28.theirs_ref
  250.6 3.0 %place_parts.3 = (f32[768,768]{1,0:T(8,128)}, f32[768,768]{1,0:T(8,128)}) custom-call(s32[3]{0:T(128)S(1)} %pad_add_fusion.c_ref, bf16[4,192,768]{2,1,0:T(8,128)(2,1)S(1)} %copy-done.2, bf16[4,192,768]{2,1,0:T(8,128)(2,1)S(1)} %collective-permute-done.28.theirs_ref), custom_call_target="tpu_custom_call" | custom-call | flops 294912 | bytes 1769472 | tf_op jit(solution)/shard_map/place_parts/pallas_call | solution.py:859
  253.6 8.9 %collective-permute-done.27.theirs_ref = bf16[4,112,768]{2,1,0:T(8,128)(2,1)S(1)} collective-permute-done((bf16[4,112,768]{2,1,0:T(8,128)(2,1)S(1)}, bf16[4,112,768]{2,1,0:T(8,128)(2,1)S(1)}, u32[]{:S(2)}, u32[]{:S(2)}) %collective-permute-start.27) | collective-permute-done | bytes 688160 | tf_op jit(solution)/shard_map/ppermute | solution.py:872
  262.5 2.1 place_parts.2
  265.3 0.7 reshape_squeeze.9
  (110 shorter events, 6.2 us)
Async XLA Ops:
  0.6 23.0 %collective-permute-start = (bf16[192,768]{1,0:T(8,128)(2,1)}, bf16[192,768]{1,0:T(8,128)(2,1)S(1)}, u32[]{:S(2)}, u32[]{:S(2)}) collective-permute-start(bf16[192,768]{1,0:T(8,128)(2,1)} %refs_11_.4), channel_id=1, source_target_pairs={{0,1},{1,0},{2,3},{3,2},{4,5},{5,4},{6,7},{7,6},{8,9},{9,8},{10,11... | collective-permute-start | bytes 884744 | tf_op jit(solution)/shard_map/ppermute | solution.py:765
  1.2 20.1 %collective-permute-start.4 = (bf16[192,768]{1,0:T(8,128)(2,1)}, bf16[192,768]{1,0:T(8,128)(2,1)S(1)}, u32[]{:S(2)}, u32[]{:S(2)}) collective-permute-start(bf16[192,768]{1,0:T(8,128)(2,1)} %refs_11_.4), channel_id=1, source_target_pairs={{0,2},{1,3},{2,0},{3,1},{4,6},{5,7},{6,4},{7,5},{8,10},{9,11},{10,... | collective-permute-start | bytes 884744 | tf_op jit(solution)/shard_map/ppermute | solution.py:769
  7.3 4.9 %copy-start.22 = (s32[2048]{0:T(1024)S(1)}, s32[2048]{0:T(1024)}, u32[]{:S(2)}) copy-start(s32[2048]{0:T(1024)} %param.18) | copy-start | bytes 24580
  12.2 8.9 %copy-start.11 = (bf16[192,1024]{1,0:T(8,128)(2,1)}, bf16[192,1024]{1,0:T(8,128)(2,1)S(1)}, u32[]{:S(2)}) copy-start(bf16[192,1024]{1,0:T(8,128)(2,1)S(1)} %get-tuple-element.86.refs_0_.refs_3_.refs_1_) | copy-start | bytes 1179652
  12.2 8.9 %copy-start.12 = (bf16[192,1024]{1,0:T(8,128)(2,1)}, bf16[192,1024]{1,0:T(8,128)(2,1)S(1)}, u32[]{:S(2)}) copy-start(bf16[192,1024]{1,0:T(8,128)(2,1)S(1)} %get-tuple-element.87.refs_1_.refs_4_.refs_2_) | copy-start | bytes 1179652
  12.2 8.9 %copy-start.20 = (bf16[192,1024]{1,0:T(8,128)(2,1)}, bf16[192,1024]{1,0:T(8,128)(2,1)S(1)}, u32[]{:S(2)}) copy-start(bf16[192,1024]{1,0:T(8,128)(2,1)S(1)} %get-tuple-element.88.refs_2_.refs_5_) | copy-start | bytes 1179652
  12.5 16.8 %copy-start = (s32[2048,128]{1,0:T(8,128)}, s32[2048,128]{1,0:T(8,128)S(1)}, u32[]{:S(2)}) copy-start(s32[2048,128]{1,0:T(8,128)S(1)} %broadcast_in_dim.12.refs_5_.refs_6_.refs_10_) | copy-start | bytes 3145732
  21.1 1.5 collective-permute-start.1
  21.3 17.8 %collective-permute-start.5 = (bf16[192,768]{1,0:T(8,128)(2,1)S(1)}, bf16[192,768]{1,0:T(8,128)(2,1)S(1)}, u32[]{:S(2)}, u32[]{:S(2)}) collective-permute-start(bf16[192,768]{1,0:T(8,128)(2,1)S(1)} %collective-permute-done.4.refs_8_), channel_id=1, source_target_pairs={{0,1},{1,0},{2,3},{3,2},{4,5},{5,4},{6,7},{7,6},{8,9},{9,8},{10,11... | collective-permute-start | bytes 884744 | tf_op jit(solution)/shard_map/ppermute | solution.py:765
  21.6 17.4 %collective-permute-start.2 = (bf16[192,512]{1,0:T(8,128)(2,1)S(1)}, bf16[192,512]{1,0:T(8,128)(2,1)S(1)}, u32[]{:S(2)}, u32[]{:S(2)}) collective-permute-start(bf16[192,512]{1,0:T(8,128)(2,1)S(1)} %get-tuple-element.95.refs_2_), channel_id=1, source_target_pairs={{0,2},{1,3},{2,0},{3,1},{4,6},{5,7},{6,4},{7,5},{8,10},{9,11},{10,... | collective-permute-start | bytes 589832 | tf_op jit(solution)/shard_map/ppermute | solution.py:769
  22.6 16.5 %collective-permute-start.3 = (bf16[192,512]{1,0:T(8,128)(2,1)S(1)}, bf16[192,512]{1,0:T(8,128)(2,1)S(1)}, u32[]{:S(2)}, u32[]{:S(2)}) collective-permute-start(bf16[192,512]{1,0:T(8,128)(2,1)S(1)} %collective-permute-done.1.refs_3_), channel_id=1, source_target_pairs={{0,2},{1,3},{2,0},{3,1},{4,6},{5,7},{6,4},{7,5},{8,10},{9,11},{10,... | collective-permute-start | bytes 589832 | tf_op jit(solution)/shard_map/ppermute | solution.py:769
  29.3 8.5 %copy-start.13 = (bf16[192,1024]{1,0:T(8,128)(2,1)}, bf16[192,1024]{1,0:T(8,128)(2,1)S(1)}, u32[]{:S(2)}) copy-start(bf16[192,1024]{1,0:T(8,128)(2,1)S(1)} %get-tuple-element.91.refs_1_.refs_3_.refs_5_) | copy-start | bytes 1179652
  29.3 8.5 %copy-start.14 = (bf16[192,1024]{1,0:T(8,128)(2,1)}, bf16[192,1024]{1,0:T(8,128)(2,1)S(1)}, u32[]{:S(2)}) copy-start(bf16[192,1024]{1,0:T(8,128)(2,1)S(1)} %get-tuple-element.92.refs_2_.refs_4_.refs_6_) | copy-start | bytes 1179652
  29.3 8.5 %copy-start.19 = (bf16[192,1024]{1,0:T(8,128)(2,1)}, bf16[192,1024]{1,0:T(8,128)(2,1)S(1)}, u32[]{:S(2)}) copy-start(bf16[192,1024]{1,0:T(8,128)(2,1)S(1)} %get-tuple-element.93.refs_3_.refs_5_) | copy-start | bytes 1179652
  29.3 9.6 %copy-start.28 = (f32[768]{0:T(1024)S(1)}, f32[768]{0:T(1024)}, u32[]{:S(2)}) copy-start(f32[768]{0:T(1024)} %param.26) | copy-start | bytes 9220
  29.4 9.6 %copy-start.29 = (f32[768]{0:T(1024)S(1)}, f32[768]{0:T(1024)}, u32[]{:S(2)}) copy-start(f32[768]{0:T(1024)} %param.27) | copy-start | bytes 9220
  29.4 9.6 %copy-start.30 = (f32[768]{0:T(1024)S(1)}, f32[768]{0:T(1024)}, u32[]{:S(2)}) copy-start(f32[768]{0:T(1024)} %param.28) | copy-start | bytes 9220
  29.4 9.7 %copy-start.8 = (bf16[192,768]{1,0:T(8,128)(2,1)S(1)}, bf16[192,768]{1,0:T(8,128)(2,1)}, u32[]{:S(2)}) copy-start(bf16[192,768]{1,0:T(8,128)(2,1)} %refs_11_.4) | copy-start | bytes 884740
  29.4 9.7 %copy-start.18 = (bf16[192,768]{1,0:T(8,128)(2,1)S(1)}, bf16[192,768]{1,0:T(8,128)(2,1)}, u32[]{:S(2)}) copy-start(bf16[192,768]{1,0:T(8,128)(2,1)} %copy-done.17) | copy-start | bytes 884740
  37.9 5.6 %collective-permute-start.6 = (bf16[192,512]{1,0:T(8,128)(2,1)S(1)}, bf16[192,512]{1,0:T(8,128)(2,1)S(1)}, u32[]{:S(2)}, u32[]{:S(2)}) collective-permute-start(bf16[192,512]{1,0:T(8,128)(2,1)S(1)} %get-tuple-element.98), channel_id=1, source_target_pairs={{0,1},{1,0},{2,3},{3,2},{4,5},{5,4},{6,7},{7,6},{8,9},{9,8},{10,11... | collective-permute-start | bytes 589832 | tf_op jit(solution)/shard_map/ppermute | solution.py:765
  37.9 7.3 %collective-permute-start.7 = (bf16[192,512]{1,0:T(8,128)(2,1)S(1)}, bf16[192,512]{1,0:T(8,128)(2,1)S(1)}, u32[]{:S(2)}, u32[]{:S(2)}) collective-permute-start(bf16[192,512]{1,0:T(8,128)(2,1)S(1)} %get-tuple-element.99.refs_2_), channel_id=1, source_target_pairs={{0,2},{1,3},{2,0},{3,1},{4,6},{5,7},{6,4},{7,5},{8,10},{9,11},{10,... | collective-permute-start | bytes 589832 | tf_op jit(solution)/shard_map/ppermute | solution.py:769
  39.1 7.2 %copy-start.31 = (f32[768]{0:T(1024)S(1)}, f32[768]{0:T(1024)}, u32[]{:S(2)}) copy-start(f32[768]{0:T(1024)} %param.30) | copy-start | bytes 9220
  39.1 8.7 %copy-start.9 = (bf16[768,768]{1,0:T(8,128)(2,1)S(1)}, bf16[768,768]{1,0:T(8,128)(2,1)}, u32[]{:S(2)}) copy-start(bf16[768,768]{1,0:T(8,128)(2,1)} %refs_4_.3) | copy-start | bytes 3538948
  39.1 8.7 %copy-start.10 = (bf16[768,768]{1,0:T(8,128)(2,1)S(1)}, bf16[768,768]{1,0:T(8,128)(2,1)}, u32[]{:S(2)}) copy-start(bf16[768,768]{1,0:T(8,128)(2,1)} %refs_6_.5) | copy-start | bytes 3538948
  45.3 2.5 collective-permute-start.8
  45.3 16.4 %collective-permute-start.9 = (bf16[192,512]{1,0:T(8,128)(2,1)S(1)}, bf16[192,512]{1,0:T(8,128)(2,1)S(1)}, u32[]{:S(2)}, u32[]{:S(2)}) collective-permute-start(bf16[192,512]{1,0:T(8,128)(2,1)S(1)} %collective-permute-done.6.refs_3_), channel_id=1, source_target_pairs={{0,2},{1,3},{2,0},{3,1},{4,6},{5,7},{6,4},{7,5},{8,10},{9,11},{10,... | collective-permute-start | bytes 589832 | tf_op jit(solution)/shard_map/ppermute | solution.py:769
  61.7 4.8 %collective-permute-start.10 = (bf16[512,768]{1,0:T(8,128)(2,1)}, bf16[512,768]{1,0:T(8,128)(2,1)S(1)}, u32[]{:S(2)}, u32[]{:S(2)}) collective-permute-start(bf16[512,768]{1,0:T(8,128)(2,1)} %get-tuple-element.109), channel_id=1, source_target_pairs={{0,1},{1,0},{2,3},{3,2},{4,5},{5,4},{6,7},{7,6},{8,9},{9,8},{10,11... | collective-permute-start | bytes 2359304 | tf_op jit(solution)/shard_map/ppermute | solution.py:765
  66.1 2.5 copy-start.23
  66.1 2.5 collective-permute-start.11
  66.7 1.9 copy-start.4
  66.7 19.6 %collective-permute-start.15 = (bf16[512,768]{1,0:T(8,128)(2,1)S(1)}, bf16[512,768]{1,0:T(8,128)(2,1)S(1)}, u32[]{:S(2)}, u32[]{:S(2)}) collective-permute-start(bf16[512,768]{1,0:T(8,128)(2,1)S(1)} %add_convert_fusion.5.refs_0_.refs_1_), channel_id=1, source_target_pairs={{0,2},{1,3},{2,0},{3,1},{4,6},{5,7},{6,4},{7,5},{8,10},{9,11},{10,... | collective-permute-start | bytes 2359304 | tf_op jit(solution)/shard_map/ppermute | solution.py:769
  83.2 8.5 %collective-permute-start.14 = (bf16[512,768]{1,0:T(8,128)(2,1)}, bf16[512,768]{1,0:T(8,128)(2,1)S(1)}, u32[]{:S(2)}, u32[]{:S(2)}) collective-permute-start(bf16[512,768]{1,0:T(8,128)(2,1)} %get-tuple-element.118), channel_id=1, source_target_pairs={{0,1},{1,0},{2,3},{3,2},{4,5},{5,4},{6,7},{7,6},{8,9},{9,8},{10,11... | collective-permute-start | bytes 2359304 | tf_op jit(solution)/shard_map/ppermute | solution.py:765
  83.6 28.2 %collective-permute-start.18 = (bf16[4,192,768]{2,1,0:T(8,128)(2,1)}, bf16[4,192,768]{2,1,0:T(8,128)(2,1)S(1)}, u32[]{:S(2)}, u32[]{:S(2)}) collective-permute-start(bf16[4,192,768]{2,1,0:T(8,128)(2,1)} %get-tuple-element.124), channel_id=1, source_target_pairs={{0,4},{4,0},{8,12},{12,8},{16,20},{20,16},{24,28},{28,24},{1,5},{5... | collective-permute-start | bytes 3538952 | tf_op jit(solution)/shard_map/ppermute | solution.py:872
  86.4 1.1 copy-start.5
  91.7 2.3 collective-permute-start.16
  91.9 2.1 copy-start.6
  91.9 20.0 %collective-permute-start.17 = (bf16[512,768]{1,0:T(8,128)(2,1)S(1)}, bf16[512,768]{1,0:T(8,128)(2,1)S(1)}, u32[]{:S(2)}, u32[]{:S(2)}) collective-permute-start(bf16[512,768]{1,0:T(8,128)(2,1)S(1)} %add_convert_fusion.2.refs_0_.refs_1_), channel_id=1, source_target_pairs={{0,2},{1,3},{2,0},{3,1},{4,6},{5,7},{6,4},{7,5},{8,10},{9,11},{10,... | collective-permute-start | bytes 2359304 | tf_op jit(solution)/shard_map/ppermute | solution.py:769
  111.9 0.9 copy-start.15
  115.9 7.6 %copy-start.7 = (bf16[512,768]{1,0:T(8,128)(2,1)S(1)}, bf16[512,768]{1,0:T(8,128)(2,1)}, u32[]{:S(2)}) copy-start(bf16[512,768]{1,0:T(8,128)(2,1)} %copy-done.6) | copy-start | bytes 2359300
  115.9 7.6 %copy-start.16 = (bf16[512,768]{1,0:T(8,128)(2,1)S(1)}, bf16[512,768]{1,0:T(8,128)(2,1)}, u32[]{:S(2)}) copy-start(bf16[512,768]{1,0:T(8,128)(2,1)} %copy-done.15) | copy-start | bytes 2359300
  115.9 35.5 %all-to-all-start = ((bf16[4,192,768]{2,1,0:T(8,128)(2,1)}), bf16[4,192,768]{2,1,0:T(8,128)(2,1)S(1)}, u32[]{:S(2)}, u32[]{:S(2)}) async-start(bf16[4,192,768]{2,1,0:T(8,128)(2,1)} %add_parts.2.refs_0_), calls=%async_computation | async-start | bytes 2359296 | tf_op jit(solution)/shard_map/all_to_all | solution.py:876
  123.0 4.9 %collective-permute-start.13 = (bf16[512,768]{1,0:T(8,128)(2,1)}, bf16[512,768]{1,0:T(8,128)(2,1)}, u32[]{:S(2)}, u32[]{:S(2)}) collective-permute-start(bf16[512,768]{1,0:T(8,128)(2,1)} %get-tuple-element.116), channel_id=1, source_target_pairs={{0,1},{1,0},{2,3},{3,2},{4,5},{5,4},{6,7},{7,6},{8,9},{9,8},{10,11... | collective-permute-start | bytes 2359304 | tf_op jit(solution)/shard_map/ppermute | solution.py:765
  123.0 4.9 %collective-permute-start.12 = (bf16[512,768]{1,0:T(8,128)(2,1)}, bf16[512,768]{1,0:T(8,128)(2,1)}, u32[]{:S(2)}, u32[]{:S(2)}) collective-permute-start(bf16[512,768]{1,0:T(8,128)(2,1)} %get-tuple-element.114), channel_id=1, source_target_pairs={{0,1},{1,0},{2,3},{3,2},{4,5},{5,4},{6,7},{7,6},{8,9},{9,8},{10,11... | collective-permute-start | bytes 2359304 | tf_op jit(solution)/shard_map/ppermute | solution.py:765
  127.8 3.2 %collective-permute-start.19 = (bf16[512,768]{1,0:T(8,128)(2,1)}, bf16[512,768]{1,0:T(8,128)(2,1)S(1)}, u32[]{:S(2)}, u32[]{:S(2)}) collective-permute-start(bf16[512,768]{1,0:T(8,128)(2,1)} %get-tuple-element.126.refs_1_), channel_id=1, source_target_pairs={{0,1},{1,0},{2,3},{3,2},{4,5},{5,4},{6,7},{7,6},{8,9},{9,8},{10,11... | collective-permute-start | bytes 2359304 | tf_op jit(solution)/shard_map/ppermute | solution.py:765
  153.1 6.7 %copy-start.24 = (bf16[512,768]{1,0:T(8,128)(2,1)S(1)}, bf16[512,768]{1,0:T(8,128)(2,1)}, u32[]{:S(2)}) copy-start(bf16[512,768]{1,0:T(8,128)(2,1)} %broadcast_select_fusion.refs_0_) | copy-start | bytes 2359300
  153.1 7.7 %copy-start.3 = (bf16[768,3,192]{0,2,1:T(8,128)(2,1)S(1)}, bf16[768,3,192]{0,2,1:T(8,128)(2,1)}, u32[]{:S(2)}) copy-start(bf16[768,3,192]{0,2,1:T(8,128)(2,1)} %param.22) | copy-start | bytes 2654212
  153.1 41.1 %all-to-all-start.1 = ((bf16[4,192,768]{2,1,0:T(8,128)(2,1)}), bf16[4,192,768]{2,1,0:T(8,128)(2,1)S(1)}, u32[]{:S(2)}, u32[]{:S(2)}) async-start(bf16[4,192,768]{2,1,0:T(8,128)(2,1)} %sum_parts.2.refs_0_), calls=%async_computation.1 | async-start | bytes 2359296 | tf_op jit(solution)/shard_map/all_to_all | solution.py:876
  159.8 19.6 %collective-permute-start.20 = (bf16[512,768]{1,0:T(8,128)(2,1)S(1)}, bf16[512,768]{1,0:T(8,128)(2,1)S(1)}, u32[]{:S(2)}, u32[]{:S(2)}) collective-permute-start(bf16[512,768]{1,0:T(8,128)(2,1)S(1)} %copy-done.24), channel_id=1, source_target_pairs={{0,2},{1,3},{2,0},{3,1},{4,6},{5,7},{6,4},{7,5},{8,10},{9,11},{10,... | collective-permute-start | bytes 2359304 | tf_op jit(solution)/shard_map/ppermute | solution.py:769
  179.4 0.9 copy-start.25
  179.4 14.8 %collective-permute-start.26 = (bf16[4,96,768]{2,1,0:T(8,128)(2,1)}, bf16[4,96,768]{2,1,0:T(8,128)(2,1)S(1)}, u32[]{:S(2)}, u32[]{:S(2)}) collective-permute-start(bf16[4,96,768]{2,1,0:T(8,128)(2,1)} %get-tuple-element.146), channel_id=1, source_target_pairs={{0,4},{4,0},{8,12},{12,8},{16,20},{20,16},{24,28},{28,24},{1,5},{5... | collective-permute-start | bytes 1769480 | tf_op jit(solution)/shard_map/ppermute | solution.py:872
  194.2 1.0 copy-start.1
  195.3 7.1 %copy-start.26 = (f32[8,768]{1,0:T(8,128)S(1)}, f32[8,768]{1,0:T(8,128)}, u32[]{:S(2)}) copy-start(f32[8,768]{1,0:T(8,128)} %get-tuple-element.141) | copy-start | bytes 73732
  197.8 18.7 %all-to-all-start.2 = ((bf16[4,96,768]{2,1,0:T(8,128)(2,1)}), bf16[4,96,768]{2,1,0:T(8,128)(2,1)S(1)}, u32[]{:S(2)}, u32[]{:S(2)}) async-start(bf16[4,96,768]{2,1,0:T(8,128)(2,1)} %add_parts.3), calls=%async_computation.2 | async-start | bytes 1179648 | tf_op jit(solution)/shard_map/all_to_all | solution.py:876
  202.3 19.3 %copy-start.2 = (bf16[4,192,768]{2,1,0:T(8,128)(2,1)S(1)}, bf16[4,192,768]{2,1,0:T(8,128)(2,1)}, u32[]{:S(2)}) copy-start(bf16[4,192,768]{2,1,0:T(8,128)(2,1)} %copy-done.1) | copy-start | bytes 3538948
  202.3 1.2 collective-permute-start.23
  203.6 3.8 %collective-permute-start.24 = (f32[8,768]{1,0:T(8,128)S(1)}, f32[8,768]{1,0:T(8,128)S(1)}, u32[]{:S(2)}, u32[]{:S(2)}) collective-permute-start(f32[8,768]{1,0:T(8,128)S(1)} %select_add_fusion.1), channel_id=1, source_target_pairs={{0,2},{1,3},{2,0},{3,1},{4,6},{5,7},{6,4},{7,5},{8,10},{9,11},{10,... | collective-permute-start | bytes 73736 | tf_op jit(solution)/shard_map/ppermute | solution.py:769
  204.5 17.7 %collective-permute-start.22 = (bf16[512,768]{1,0:T(8,128)(2,1)}, bf16[512,768]{1,0:T(8,128)(2,1)}, u32[]{:S(2)}, u32[]{:S(2)}) collective-permute-start(bf16[512,768]{1,0:T(8,128)(2,1)} %get-tuple-element.140), channel_id=1, source_target_pairs={{0,1},{1,0},{2,3},{3,2},{4,5},{5,4},{6,7},{7,6},{8,9},{9,8},{10,11... | collective-permute-start | bytes 2359304 | tf_op jit(solution)/shard_map/ppermute | solution.py:765
  217.9 21.4 %copy-start.27 = (f32[768]{0:T(1024)S(1)}, f32[768]{0:T(1024)}, u32[]{:S(2)}) copy-start(f32[768]{0:T(1024)} %param.32) | copy-start | bytes 9220
  217.9 20.2 %all-to-all-start.3 = ((bf16[4,112,768]{2,1,0:T(8,128)(2,1)}), bf16[4,112,768]{2,1,0:T(8,128)(2,1)S(1)}, u32[]{:S(2)}, u32[]{:S(2)}) async-start(bf16[4,112,768]{2,1,0:T(8,128)(2,1)} %sum_parts.3), calls=%async_computation.3 | async-start | bytes 1376256 | tf_op jit(solution)/shard_map/all_to_all | solution.py:876
  221.6 29.0 %collective-permute-start.28 = (bf16[4,192,768]{2,1,0:T(8,128)(2,1)S(1)}, bf16[4,192,768]{2,1,0:T(8,128)(2,1)S(1)}, u32[]{:S(2)}, u32[]{:S(2)}) collective-permute-start(bf16[4,192,768]{2,1,0:T(8,128)(2,1)S(1)} %copy-done.2), channel_id=1, source_target_pairs={{0,4},{4,0},{8,12},{12,8},{16,20},{20,16},{24,28},{28,24},{1,5},{5... | collective-permute-start | bytes 3538952 | tf_op jit(solution)/shard_map/ppermute | solution.py:872
  222.2 21.2 %collective-permute-start.21 = (bf16[512,768]{1,0:T(8,128)(2,1)}, bf16[512,768]{1,0:T(8,128)(2,1)}, u32[]{:S(2)}, u32[]{:S(2)}) collective-permute-start(bf16[512,768]{1,0:T(8,128)(2,1)} %get-tuple-element.138), channel_id=1, source_target_pairs={{0,1},{1,0},{2,3},{3,2},{4,5},{5,4},{6,7},{7,6},{8,9},{9,8},{10,11... | collective-permute-start | bytes 2359304 | tf_op jit(solution)/shard_map/ppermute | solution.py:765
  224.7 20.3 %collective-permute-start.25 = (bf16[512,768]{1,0:T(8,128)(2,1)}, bf16[512,768]{1,0:T(8,128)(2,1)}, u32[]{:S(2)}, u32[]{:S(2)}) collective-permute-start(bf16[512,768]{1,0:T(8,128)(2,1)} %add_convert_fusion), channel_id=1, source_target_pairs={{0,2},{1,3},{2,0},{3,1},{4,6},{5,7},{6,4},{7,5},{8,10},{9,11},{10,... | collective-permute-start | bytes 2359304 | tf_op jit(solution)/shard_map/ppermute | solution.py:769
  238.2 6.7 %copy-start.21 = (bf16[512,768]{1,0:T(8,128)(2,1)S(1)}, bf16[512,768]{1,0:T(8,128)(2,1)}, u32[]{:S(2)}) copy-start(bf16[512,768]{1,0:T(8,128)(2,1)} %get-tuple-element.137.mine_ref) | copy-start | bytes 2359300
  238.2 24.3 %collective-permute-start.27 = (bf16[4,112,768]{2,1,0:T(8,128)(2,1)S(1)}, bf16[4,112,768]{2,1,0:T(8,128)(2,1)S(1)}, u32[]{:S(2)}, u32[]{:S(2)}) collective-permute-start(bf16[4,112,768]{2,1,0:T(8,128)(2,1)S(1)} %all-to-all-done.3.mine_ref), channel_id=1, source_target_pairs={{0,4},{4,0},{8,12},{12,8},{16,20},{20,16},{24,28},{28,24},{1,5},{5... | collective-permute-start | bytes 2064392 | tf_op jit(solution)/shard_map/ppermute | solution.py:872
  (1 other events, 0.7 us)

commit v3 on v2

--- a/solution.py
+++ b/solution.py
@@ -12,7 +12,7 @@
 HD = 64
 HALF = HD // 2
 RB = 256
-KB = 256
+KB = 512
 FB = 512
 
 masked_score = -1e30
@@ -167,7 +167,7 @@
             out_specs=[pl.BlockSpec((FB, d), lambda i, c: (i, 0)), tall, tall, tall],
         ),
         out_shape=[hbm((LEN, d), bf16)] + [jax.ShapeDtypeStruct((width, LEN), bf16)] * 3,
-        compiler_params=params(20),
+        compiler_params=params(16),
         cost_estimate=cost(2 * LEN * d * wide, 2 * (2 * LEN * d + wide * (d + LEN))),
         name="project",
     )(core, *stay(*wait), *stay(patches, grid, tab, wt, bias_cols), gain, beta)
@@ -216,7 +216,7 @@
             new.append(jnp.maximum(tops[h], jnp.max(s, axis=0, keepdims=True)))
         return tuple(new)
 
-    tops = lax.fori_loop(lo, hi, first_pass, tuple(jnp.full((1, RB), masked_score, f32) for _ in range(heads)))
+    tops = lax.fori_loop(lo, hi, first_pass, tuple(jnp.full((1, FB), masked_score, f32) for _ in range(heads)))
     tops = tuple(top * SCALE2 for top in tops)
     acc[...] = jnp.zeros_like(acc)
 
@@ -229,9 +229,9 @@
             acc[h * HD : (h + 1) * HD, :] += mm(v_ref[h * HD : (h + 1) * HD, pl.ds(at, KB)], p.astype(bf16))
         return tuple(new)
 
-    totals = lax.fori_loop(lo, hi, second_pass, tuple(jnp.zeros((1, RB), f32) for _ in range(heads)))
-    lse = jnp.zeros((8, RB), f32)
-    row = lax.broadcasted_iota(jnp.int32, (8, RB), 0)
+    totals = lax.fori_loop(lo, hi, second_pass, tuple(jnp.zeros((1, FB), f32) for _ in range(heads)))
+    lse = jnp.zeros((8, FB), f32)
+    row = lax.broadcasted_iota(jnp.int32, (8, FB), 0)
     for h in range(heads):
         ctx_ref[h * HD : (h + 1) * HD, :] = acc[h * HD : (h + 1) * HD, :] * (1.0 / totals[h])
         lse = jnp.where(row == h, tops[h] + jnp.log2(totals[h]), lse)
@@ -249,7 +249,7 @@
 
 def attend(seq, core, q, k, v, ids_rows, ids_cols, wait=()):
     width = q.shape[0]
-    steps = LEN // RB
+    steps = LEN // FB
     half = steps // 2
     heads = width // HD
     blk = lambda i, c: lax.rem(i + half * (1 - c[0]), steps)
@@ -261,23 +261,23 @@
             grid=(steps,),
             in_specs=[ANY] * len(wait)
             + [
-                pl.BlockSpec((width, RB), lambda i, c: (0, blk(i, c))),
+                pl.BlockSpec((width, FB), lambda i, c: (0, blk(i, c))),
                 whole(width, LEN),
                 whole(width, LEN),
                 pl.BlockSpec((None, 1, LEN), lambda i, c: (seq, 0, 0)),
-                pl.BlockSpec((None, 1, RB), lambda i, c: (seq, 0, blk(i, c))),
+                pl.BlockSpec((None, 1, FB), lambda i, c: (seq, 0, blk(i, c))),
                 pl.BlockSpec((LEN, 128), lambda i, c: (seq, 0)),
             ],
             out_specs=[
-                pl.BlockSpec((width, RB), lambda i, c: (0, jnp.minimum(i, half - 1))),
-                pl.BlockSpec((width, RB), lambda i, c: (0, jnp.maximum(i - half, 0))),
-                pl.BlockSpec((width, RB), lambda i, c: (0, blk(i, c))),
-                pl.BlockSpec((8, RB), lambda i, c: (0, blk(i, c))),
+                pl.BlockSpec((width, FB), lambda i, c: (0, jnp.minimum(i, half - 1))),
+                pl.BlockSpec((width, FB), lambda i, c: (0, jnp.maximum(i - half, 0))),
+                pl.BlockSpec((width, FB), lambda i, c: (0, blk(i, c))),
+                pl.BlockSpec((8, FB), lambda i, c: (0, blk(i, c))),
             ],
             scratch_shapes=[
                 pltpu.VMEM((heads, LEN, HD), bf16),
-                pltpu.VMEM((heads, LEN, RB), f32),
-                pltpu.VMEM((width, RB), f32),
+                pltpu.VMEM((heads, LEN, FB), f32),
+                pltpu.VMEM((width, FB), f32),
             ],
         ),
         out_shape=[
@@ -286,7 +286,7 @@
             hbm((width, LEN), f32),
             hbm((8, LEN), f32),
         ],
-        compiler_params=params(10),
+        compiler_params=params(16),
         cost_estimate=cost(8 * LEN * LEN * width, 12 * LEN * width, heads * LEN * LEN),
         name="attend",
     )(core, *stay(*wait), q, k, v, ids_rows, ids_rows, ids_cols)
@@ -324,7 +324,7 @@
             out_specs=[blk, blk],
         ),
         out_shape=[hbm((rows, d), f32), hbm((rows, d), bf16)],
-        compiler_params=params(10),
+        compiler_params=params(8),
         cost_estimate=cost(2 * len(ctxs) * rows * d * width, 12 * rows * d),
         name="norm_two",
     )(core, *stay(*wait), *stay(patches), *ctxs, *wos, bias, gain, beta)
@@ -447,7 +447,7 @@
         ),
         out_shape=[hbm(rows.shape, bf16), hbm(rows.shape, bf16), hbm(rows.shape, bf16), rows, hbm((8, d), f32)]
         + [(hbm if last else jax.ShapeDtypeStruct)(g, kind) for g in grads],
-        compiler_params=params(50),
+        compiler_params=params(24),
         cost_estimate=cost(12 * LEN * d * units, 2 * LEN * d * 4 + 12 * d * units, 2 * LEN * units),
         name="feed",
     )(*args)
@@ -507,7 +507,7 @@
             jax.ShapeDtypeStruct((rows, d), bf16),
             hbm((8, d), f32),
         ],
-        compiler_params=params(12),
+        compiler_params=params(8),
         cost_estimate=cost(20 * rows * d, 16 * rows * d),
         name="norm_two_back",
     )(*args)
@@ -518,7 +518,7 @@
     own_ref, other_ref, q_ref, k_ref, v_ref, ctx_ref, lse_ref, idr_ref, idq_ref, idc_ref, wo_ref = refs[:11]
     refs = refs[11:]
     dwo0_ref = None if first else refs.pop(0)
-    grads_ref, dwo_ref, keys, vals = refs
+    low_ref, dwo_ref, keys, vals, grads_ref = refs
     step = pl.program_id(0)
     steps = pl.num_programs(0)
     half = steps // 2
@@ -565,6 +565,10 @@
         return carry
 
     lax.fori_loop(lo, hi, body, 0)
+
+    @pl.when(step == steps - 1)
+    def _():
+        low_ref[...] = grads_ref[...].astype(bf16)
 
 
 def attend_back(seq, core, own, other, q, k, v, ctx, lse, ids_rows, ids_cols, wo, before=None, wait=()):
@@ -594,10 +598,12 @@
         grid_spec=pltpu.PrefetchScalarGridSpec(
             num_scalar_prefetch=1, grid=(steps,), in_specs=in_specs,
             out_specs=[whole(3 * width, LEN), whole(width, d)],
-            scratch_shapes=[pltpu.VMEM((heads, LEN, HD), bf16), pltpu.VMEM((heads, LEN, HD), bf16)],
-        ),
-        out_shape=[hbm((3 * width, LEN), f32), hbm((width, d), f32)],
-        compiler_params=params(20),
+            scratch_shapes=[
+                pltpu.VMEM((heads, LEN, HD), bf16), pltpu.VMEM((heads, LEN, HD), bf16), pltpu.VMEM((3 * width, LEN), f32)
+            ],
+        ),
+        out_shape=[hbm((3 * width, LEN), bf16), hbm((width, d), f32)],
+        compiler_params=params(18),
         cost_estimate=cost(
             20 * LEN * LEN * width + 8 * LEN * d * width, 2 * LEN * (10 * width + d) + 8 * d * width, heads * LEN * LEN,
         ),
@@ -610,7 +616,7 @@
     (wt_ref, tab_ref, grid_ref, gain_ref, beta_ref, dwo_ref, small_two_ref, small_feed_ref) = refs[8:16]
     send_away, keep_away, send_mine, keep_mine, small_ref = refs[16:21]
     outs = refs[21:23]
-    dwt_acc, row_acc, col_acc, rope_acc = refs[23:]
+    dwt_acc, col_acc, rope_acc = refs[23:]
     step = pl.program_id(0)
     steps = pl.num_programs(0) // 2
     half = steps // 2
@@ -623,7 +629,7 @@
 
     @pl.when(step == 0)
     def _():
-        for acc in (dwt_acc, row_acc, col_acc, rope_acc):
+        for acc in (dwt_acc, col_acc, rope_acc):
             acc[...] = jnp.zeros_like(acc)
 
     place = grid_ref[...]
@@ -634,7 +640,7 @@
     for k in range(2):
         turned = pick(k)
         for h in range(heads):
-            b = grads[k * width + h * HD : k * width + (h + 1) * HD] * SCALE
+            b = grads[k * width + h * HD : k * width + (h + 1) * HD].astype(f32) * SCALE
             a = turned[h * HD : (h + 1) * HD].astype(f32)
             b1, b2 = b[:HALF], b[HALF:]
             co = cosine[h * HALF : (h + 1) * HALF]
@@ -649,8 +655,11 @@
     rope_acc[...] += lax.dot_general(
         place.astype(f32), angle, NT, precision=lax.Precision.HIGHEST, preferred_element_type=f32
     )
-    row_acc[...] += mm(jnp.ones((8, RB), bf16), mixed_grad, NT)
-    col_acc[...] += mm(mixed_grad, jnp.ones((RB, 128), bf16))
+    exact = mixed_grad.astype(f32)
+    folded = exact[:, 0:128]
+    for at in range(128, FB, 128):
+        folded = folded + exact[:, at : at + 128]
+    col_acc[...] += folded
     dwt_acc[...] += mm(mixed_grad, pick(3))
     partial = mm(mixed_grad, wt_ref[...], TN).astype(bf16)
     for k, out in enumerate((send_away, keep_away, send_mine, keep_mine)):
@@ -661,13 +670,14 @@
     @pl.when(step == 2 * steps - 1)
     def _():
         raw = dwt_acc[...]
-        col = col_acc[:, 0:1]
+        col = jnp.sum(col_acc[...], axis=1, keepdims=True)
+        row_sum = jnp.sum(jnp.transpose(col_acc[...]), axis=0, keepdims=True)
         wt = wt_ref[...].astype(f32)
         small_ref[0:1, :] = jnp.sum(wt * raw, axis=0, keepdims=True)
         small_ref[1:2, :] = jnp.sum(wt * col, axis=0, keepdims=True)
         small_ref[2:5, :] = 0.5 * small_two_ref[0:3, :]
         small_ref[5:7, :] = small_feed_ref[0:2, :]
-        small_ref[7:8, :] = jnp.concatenate([row_acc[0:1, :], rope_acc[1:2, :], rope_acc[0:1, :]], axis=1)
+        small_ref[7:8, :] = jnp.concatenate([row_sum, rope_acc[1:2, :], rope_acc[0:1, :]], axis=1)
         dwt_acc[...] = raw * gain_ref[...] + col * beta_ref[...]
         store_halves(c_ref[1], outs, (dwt_acc, dwo_ref))
 
@@ -676,7 +686,7 @@
     d = wt.shape[1]
     width = wt.shape[0] // 3
     heads = width // HD
-    steps = LEN // RB
+    steps = LEN // FB
     half = steps // 2
     whole = lambda *shape: pl.BlockSpec(shape, lambda i, c: (0,) * len(shape), pipeline_mode=pl.Buffered(1))
     blk = lambda i, c: lax.rem(lax.rem(i, steps) + half * (1 - c[0]), steps)
@@ -693,17 +703,17 @@
         tall = lambda i, c, s=s: (0, turn(s, i, c))
         flat = lambda i, c, s=s: (turn(s, i, c), 0)
         in_specs += [
-            pl.BlockSpec((width, RB), tall), pl.BlockSpec((width, RB), tall), pl.BlockSpec((3 * width, RB), tall),
-            pl.BlockSpec((RB, d), flat),
+            pl.BlockSpec((width, FB), tall), pl.BlockSpec((width, FB), tall), pl.BlockSpec((3 * width, FB), tall),
+            pl.BlockSpec((FB, d), flat),
         ]
         args += stay(*seqs[s])
     in_specs += [
         whole(3 * width, d), whole(*tab.shape),
-        pl.BlockSpec((2, RB), lambda i, c: (0, now(i, c) * steps + blk(i, c))),
+        pl.BlockSpec((2, FB), lambda i, c: (0, now(i, c) * steps + blk(i, c))),
         whole(1, d), whole(1, d), whole(width, d), whole(8, d), whole(8, d),
     ]
     args += [wt, *stay(tab, grid), gain, beta, *stay(dwo, small_two, small_feed)]
-    part = lambda k: pl.BlockSpec((RB, d), lambda i, c: (jnp.clip(i - k * half, 0, half - 1), 0))
+    part = lambda k: pl.BlockSpec((FB, d), lambda i, c: (jnp.clip(i - k * half, 0, half - 1), 0))
     cut = (pieces, 4 * width // (2 * pieces), d)
     rows = hbm((LEN // 2, d), bf16)
     return pl.pallas_call(
@@ -713,13 +723,12 @@
             out_specs=[part(0), part(1), part(2), part(3), whole(8, d), whole(*cut), whole(*cut)],
             scratch_shapes=[
                 pltpu.VMEM((3 * width, d), f32),
-                pltpu.VMEM((8, 3 * width), f32),
                 pltpu.VMEM((3 * width, 128), f32),
                 pltpu.VMEM((2, heads * HALF), f32),
             ],
         ),
         out_shape=[rows, rows, rows, rows, hbm((8, d), f32), hbm(cut, bf16), hbm(cut, bf16)],
-        compiler_params=params(28),
+        compiler_params=params(30),
         cost_estimate=cost(24 * LEN * d * width, 4 * LEN * (12 * width + 3 * d), LEN * width),
         name="project_back",
     )(*args)
@@ -751,7 +760,7 @@
             out_specs=blk,
         ),
         out_shape=jax.ShapeDtypeStruct((rows, d), bf16),
-        compiler_params=params(12),
+        compiler_params=params(10),
         cost_estimate=cost(20 * rows * d, 16 * rows * d),
         name="norm_one_back",
     )(place, mine, got, theirs, *stay(patches, rg0, rg1), gain)
@@ -792,7 +801,7 @@
             num_scalar_prefetch=1, grid=(1,), in_specs=[ANY] * len(wait) + [full(a.shape)] * 2, out_specs=full(a.shape),
         ),
         out_shape=hbm(a.shape, bf16),
-        compiler_params=params(12),
+        compiler_params=params(10),
         cost_estimate=cost(a.size, 6 * a.size),
         name="add_parts",
     )(core, *stay(*wait), *stay(a), b)
@@ -828,7 +837,7 @@
             out_specs=full(out),
         ),
         out_shape=jax.ShapeDtypeStruct(out, bf16),
-        compiler_params=params(12),
+        compiler_params=params(10),
         cost_estimate=cost(count * rows * d, 4 * count * rows * d),
         name="sum_parts",
     )(core, *stay(*wait), parts, *extra)
@@ -862,7 +871,7 @@
             num_scalar_prefetch=1, grid=(1,), in_specs=[full(mine.shape)] * 2, out_specs=[full(t) for t in shapes],
         ),
         out_shape=[jax.ShapeDtypeStruct(t, f32) for t in shapes],
-        compiler_params=params(20),
+        compiler_params=params(18),
         cost_estimate=cost(sum(splits) * d, 6 * sum(splits) * d),
         name="place_parts",
     )(core, mine, theirs)
@@ -956,21 +965,20 @@
     rgrad1, branch1, small_two = norm_two_back(
         1, core, n21, n2_far1, resid1, out_grad, gain2, before=small_two, wait=[event]
     )
+    mlp_theirs = chip_swap(mlp_away)
     grads1, dwo = attend_back(
         1, core, branch1, core_swap(branch1), *made1[1:], ctx1, lse1, ids_rows, ids_cols, out_weight, before=dwo,
         wait=[mlp_away],
     )
     event = dwo
     if tree:
-        feed_sum = sum_parts(core, feed_got, wait=[dwo])
+        feed_sum = sum_parts(core, feed_got, wait=[dwo, mlp_theirs])
         event = feed_sum
         feed_all = quarter_trade(feed_sum)
-    mlp_theirs = chip_swap(mlp_away)
     n1_send_away, n1_away, n1_send, n1_keep, small, grad_send, grad_keep = project_back(
         core, [(*made[1:3], grads, made[0]) for made, grads in ((made0, grads0), (made1, grads1))],
         wt, tab, patch_grid, gain1, beta1, dwo, small_two, small_feed, pieces, wait=[event],
     )
-    n1_send_away, small, grad_send, mlp_theirs = hold([n1_send_away, small, grad_send, mlp_theirs])
     n1_away = add_low(n1_away, core_swap(n1_send_away))
     n1_got = core_swap(n1_send)
     shared = lax.broadcasted_iota(jnp.int32, small.shape, 0) < 5
@@ -981,7 +989,7 @@
         grad_got = half_swap(grad_send)
         grad_got = quarter_trade(add_parts(core, grad_keep, grad_got, wait=[feed_all]))
         feed_other = half_swap(feed_all)
-        grad_sum = quarter_trade(sum_parts(core, grad_got, small))
+        grad_sum = quarter_trade(sum_parts(core, grad_got, small, wait=[feed_other]))
         grad_other = half_swap(grad_sum)
     else:
         small, grad_send, grad_keep, feed_send, feed_keep = lax.psum(

time: 268 us -> 251 us (0.937)
  Pallas kernels: 142 us -> 130 us
    ppermute x4, waiting for transfers between devices: 26 us -> 9.61 us  [half_swap(): lax.ppermute(value, 'dp', [(i, i ^ 1) for i in range(lax.axis_size('dp'))])]
    all_to_all x4, waiting for transfers between devices: 25.3 us -> 38 us  [quarter_trade(): lax.all_to_all(parts, 'dp', 0, 0, axis_index_groups=[[0, 2, 4, 6], [1, 3,...]
    all_to_all x4, starting transfers between devices: 21.9 us -> 16.7 us  [quarter_trade(): lax.all_to_all(parts, 'dp', 0, 0, axis_index_groups=[[0, 2, 4, 6], [1, 3,...]
    ppermute x10, waiting for transfers between devices: 10.1 us -> 14 us  [chip_swap(): return lax.ppermute(value, 'mp', CHIP_SWAP)]
    pallas_call x2, Pallas kernels: 33.1 us -> 29.2 us  [attend_back(): pl.pallas_call(ignoring(len(wait), functools.partial(attend_back_kernel,...]
    ppermute x4, starting transfers between devices: 3.24 us -> 6.14 us  [half_swap(): lax.ppermute(value, 'dp', [(i, i ^ 1) for i in range(lax.axis_size('dp'))])]
    pallas_call x2, Pallas kernels: 28.5 us -> 25.6 us  [feed(): pl.pallas_call(ignoring(len(wait), functools.partial(feed_kernel, first,...]
    pallas_call x1, Pallas kernels: 16.2 us -> 13.4 us  [project_back(): pl.pallas_call(ignoring(len(wait), project_back_kernel), grid_spec=pltpu....]
where the time goes in v3:
time: 251 us; the launch traced here: 250 us
  Pallas kernels  130 us (52%)
  waiting for transfers between devices  66.6 us (27%)
  starting transfers between devices  36.1 us (14%)
  other arithmetic  9.43 us (4%)
  local copies, waits for them, and re-layouts  7.19 us (3%)
    all_to_all x4, waiting for transfers between devices, quarter_trade(): lax.all_to_all(parts, 'dp', 0, 0, axis_index_groups=[[0, 2, 4, 6], [1, 3,...  38 us
    pallas_call x2, Pallas kernels, attend_back(): pl.pallas_call(ignoring(len(wait), functools.partial(attend_back_kernel,...  29.2 us
    pallas_call x2, Pallas kernels, feed(): pl.pallas_call(ignoring(len(wait), functools.partial(feed_kernel, first,...  25.6 us
    all_to_all x4, starting transfers between devices, quarter_trade(): lax.all_to_all(parts, 'dp', 0, 0, axis_index_groups=[[0, 2, 4, 6], [1, 3,...  16.7 us
    pallas_call x2, Pallas kernels, attend(): pl.pallas_call(ignoring(len(wait), attend_kernel), grid_spec=pltpu.Prefet...  15.2 us
    ppermute x10, waiting for transfers between devices, chip_swap(): return lax.ppermute(value, 'mp', CHIP_SWAP)  14 us
    pallas_call x1, Pallas kernels, project_back(): pl.pallas_call(ignoring(len(wait), project_back_kernel), grid_spec=pltpu....  13.4 us
    ppermute x10, starting transfers between devices, chip_swap(): return lax.ppermute(value, 'mp', CHIP_SWAP)  10.5 us
  transfers between devices with their start and end apart: 33, of which 18 were waited for; matrix products, arithmetic and copies ran while one was open for 4% of the time, Pallas kernels for 50%

profile of v3, /device:TPU:0, one launch (start us, length us, event | category | flops | bytes accessed | tf_op | source)
XLA Modules:
  0.0 250.3 jit_solution(12067836368334481294)
XLA Ops:
  1.2 2.6 %collective-permute-start.4 = (bf16[192,768]{1,0:T(8,128)(2,1)}, bf16[192,768]{1,0:T(8,128)(2,1)S(1)}, u32[]{:S(2)}, u32[]{:S(2)}) collective-permute-start(bf16[192,768]{1,0:T(8,128)(2,1)} %refs_11_.4), channel_id=1, source_target_pairs={{0,2},{1,3},{2,0},{3,1},{4,6},{5,7},{6,4},{7,5},{8,10},{9,11},{10,... | collective-permute-start | bytes 884744 | tf_op jit(solution)/shard_map/ppermute | solution.py:778
  3.8 0.7 reshape.64.refs_5_.refs_7_.refs_12_.gain_ref
  4.5 0.7 reshape.65.refs_6_.refs_8_.refs_13_
  5.2 2.1 prepare.1
  7.3 4.9 %project.2 = (bf16[1024,768]{1,0:T(8,128)(2,1)}, bf16[192,1024]{1,0:T(8,128)(2,1)S(1)}, bf16[192,1024]{1,0:T(8,128)(2,1)S(1)}, bf16[192,1024]{1,0:T(8,128)(2,1)S(1)}) custom-call(s32[3]{0:T(128)S(1)} %pad_add_fusion.c_ref, bf16[2048,768]{1,0:T(8,128)(2,1)} %x_ref.1, s32[2,2048]{1,0:T(2,128)} %refs_11_.5, ...), custom_call_target="tpu_custom_call" | custom-call | flops 226492416 | bytes 1302528 | tf_op jit(solution)/shard_map/project/pallas_call | solution.py:152
  12.5 7.6 %attend.2 = (bf16[192,512]{1,0:T(8,128)(2,1)S(1)}, bf16[192,512]{1,0:T(8,128)(2,1)S(1)}, f32[192,1024]{1,0:T(8,128)}, f32[8,1024]{1,0:T(8,128)}) custom-call(s32[3]{0:T(128)S(1)} %pad_add_fusion.c_ref, bf16[192,1024]{1,0:T(8,128)(2,1)S(1)} %get-tuple-element.82.refs_0_.refs_3_.refs_1_, bf16[192,1024]{1,0:T(8,128)(2,1)S(1)} %get-tuple-element.83.refs_1_.refs_4_.refs_2_, ...), custom_call_target="tpu_custom_call" | custom-call | flops 402653184 | bytes 589824 | tf_op jit(solution)/shard_map/attend/pallas_call | solution.py:257
  20.8 0.9 collective-permute-done.1.refs_3_
  21.7 1.1 collective-permute-start.3
  22.8 0.7 copy-done.19
  23.5 4.9 %project.3 = (bf16[1024,768]{1,0:T(8,128)(2,1)}, bf16[192,1024]{1,0:T(8,128)(2,1)S(1)}, bf16[192,1024]{1,0:T(8,128)(2,1)S(1)}, bf16[192,1024]{1,0:T(8,128)(2,1)S(1)}) custom-call(s32[3]{0:T(128)S(1)} %pad_add_fusion.c_ref, f32[8,1024]{1,0:T(8,128)} %get-tuple-element.85.refs_0_.refs_7_, bf16[192,768]{1,0:T(8,128)(2,1)} %copy-done.19, ...), custom_call_target="tpu_custom_call" | custom-call | flops 226492416 | bytes 1302528 | tf_op jit(solution)/shard_map/project/pallas_call | solution.py:152
  28.5 7.6 %attend.3 = (bf16[192,512]{1,0:T(8,128)(2,1)S(1)}, bf16[192,512]{1,0:T(8,128)(2,1)S(1)}, f32[192,1024]{1,0:T(8,128)}, f32[8,1024]{1,0:T(8,128)}) custom-call(s32[3]{0:T(128)S(1)} %pad_add_fusion.c_ref, bf16[1024,768]{1,0:T(8,128)(2,1)} %get-tuple-element.86.refs_0_.refs_8_, bf16[192,1024]{1,0:T(8,128)(2,1)S(1)} %get-tuple-element.87.refs_1_.refs_3_.refs_5_, ...), custom_call_target="tpu_custom_call" | custom-call | flops 402653184 | bytes 589824 | tf_op jit(solution)/shard_map/attend/pallas_call | solution.py:257
  36.2 1.0 collective-permute-start.7
  37.3 4.4 %norm_two.2 = (f32[512,768]{1,0:T(8,128)}, bf16[512,768]{1,0:T(8,128)(2,1)}) custom-call(s32[3]{0:T(128)S(1)} %pad_add_fusion.c_ref, f32[8,1024]{1,0:T(8,128)} %get-tuple-element.90.refs_0_.refs_7_, bf16[2048,768]{1,0:T(8,128)(2,1)} %x_ref.1, bf16[192,512]{1,0:T(8,128)(2,1)S(1)} %get-tuple-element.91.refs_2_, ...), custom_call_target="tpu_custom_call" | custom-call | flops 150994944 | bytes 1179648 | tf_op jit(solution)/shard_map/norm_two/pallas_call | solution.py:314
  41.7 1.8 collective-permute-done.7.refs_4_
  43.5 0.9 collective-permute-start.9
  44.4 1.6 collective-permute-done.8.refs_1_
  46.0 12.6 %feed.2 = (bf16[512,768]{1,0:T(8,128)(2,1)}, bf16[512,768]{1,0:T(8,128)(2,1)}, bf16[512,768]{1,0:T(8,128)(2,1)}, bf16[512,768]{1,0:T(8,128)(2,1)S(1)}, f32[8,768...) custom-call(s32[3]{0:T(128)S(1)} %pad_add_fusion.c_ref, bf16[512,768]{1,0:T(8,128)(2,1)} %get-tuple-element.96.refs_0_, ...), custom_call_target="tpu_custom_call" | custom-call | flops 1811939328 | bytes 3342336 | tf_op jit(solution)/shard_map/feed/pallas_call | solution.py:434
  58.8 4.2 %norm_two.3 = (f32[512,768]{1,0:T(8,128)}, bf16[512,768]{1,0:T(8,128)(2,1)}) custom-call(s32[3]{0:T(128)S(1)} %pad_add_fusion.c_ref, f32[8,768]{1,0:T(8,128)} %get-tuple-element.97.refs_0_.refs_7_, bf16[2048,768]{1,0:T(8,128)(2,1)} %x_ref.1, bf16[192,512]{1,0:T(8,128)(2,1)S(1)} %get-tuple-element.95.refs_2_, ...), custom_call_target="tpu_custom_call" | custom-call | flops 150994944 | bytes 1179648 | tf_op jit(solution)/shard_map/norm_two/pallas_call | solution.py:314
  63.6 1.0 collective-permute-start.16
  64.6 0.9 collective-permute-done.11.refs_2_
  65.5 13.0 %feed.3 = (bf16[512,768]{1,0:T(8,128)(2,1)}, bf16[512,768]{1,0:T(8,128)(2,1)}, bf16[512,768]{1,0:T(8,128)(2,1)}, bf16[512,768]{1,0:T(8,128)(2,1)S(1)}, f32[8,768...) custom-call(s32[3]{0:T(128)S(1)} %pad_add_fusion.c_ref, bf16[512,768]{1,0:T(8,128)(2,1)} %copy-done.4, ...), custom_call_target="tpu_custom_call" | custom-call | flops 1811939328 | bytes 3342336 | tf_op jit(solution)/shard_map/feed/pallas_call | solution.py:434
  79.0 1.5 collective-permute-start.19
  80.5 2.8 %collective-permute-done.16.refs_2_ = bf16[512,768]{1,0:T(8,128)(2,1)S(1)} collective-permute-done((bf16[512,768]{1,0:T(8,128)(2,1)S(1)}, bf16[512,768]{1,0:T(8,128)(2,1)S(1)}, u32[]{:S(2)}, u32[]{:S(2)}) %collective-permute-start.16) | collective-permute-done | bytes 786464 | tf_op jit(solution)/shard_map/ppermute | solution.py:778
  83.3 1.1 copy-done.5
  84.4 4.1 %norm_two_back.2 = (f32[512,768]{1,0:T(8,128)}, bf16[512,768]{1,0:T(8,128)(2,1)S(1)}, f32[8,768]{1,0:T(8,128)}) custom-call(s32[3]{0:T(128)S(1)} %pad_add_fusion.c_ref, f32[8,768]{1,0:T(8,128)} %get-tuple-element.115.refs_0_.refs_16_, bf16[512,768]{1,0:T(8,128)(2,1)S(1)} %copy-done.5, bf16[512,768]{1,0:T(8,128)(2,1)S(1)} %collective-permute-done.16.refs_2_, ...), custom_call_target="tpu_custom_call" | custom-call | flops 1966080 | bytes 1572864 | tf_op jit(solution)/shard_map/norm_two_back/pallas_call | solution.py:500
  88.8 1.0 collective-permute-start.18
  90.8 14.5 %attend_back.2 = (bf16[576,1024]{1,0:T(8,128)(2,1)}, f32[192,768]{1,0:T(8,128)}) custom-call(s32[3]{0:T(128)S(1)} %pad_add_fusion.c_ref, bf16[512,768]{1,0:T(8,128)(2,1)} %copy-done.6, bf16[512,768]{1,0:T(8,128)(2,1)S(1)} %get-tuple-element.116.refs_1_, bf16[512,768]{1,0:T(8,128)(2,1)S(1)} %collective-permute-done.17.refs_2_, bf16[192,1024]{1,0:T(8,128)(2,1)} %copy-done.13, ...), custom_call_target="tpu_custom_call" | custom-call | flops 1308622848 | bytes 1671168 | tf_op jit(solution)/shard_map/attend_back/pallas_call | solution.py:596
  105.3 1.9 collective-permute-done.19.refs_3_
  107.2 1.6 collective-permute-done.18.refs_1_.refs_2_
  108.8 0.9 copy-done.17
  109.7 3.1 %add_parts.2.refs_0_ = bf16[4,192,768]{2,1,0:T(8,128)(2,1)} custom-call(s32[3]{0:T(128)S(1)} %pad_add_fusion.c_ref, f32[192,768]{1,0:T(8,128)} %get-tuple-element.118.refs_0_.refs_12_, bf16[512,768]{1,0:T(8,128)(2,1)} %copy-done.17, bf16[4,192,768]{2,1,0:T(8,128)(2,1)} %get-tuple-element.119.refs_2_, bf16[4,192,768]{2,1,0:T(8,128)(2,1)S(1)} %collective-permute-done.19.refs_3_), custom_call_target="tpu_custom_call" | custom-call | flops 147456 | bytes 884736 | tf_op jit(solution)/shard_map/add_parts/pallas_call | solution.py:798
  112.8 5.0 %all-to-all-start = ((bf16[4,192,768]{2,1,0:T(8,128)(2,1)}), bf16[4,192,768]{2,1,0:T(8,128)(2,1)S(1)}, u32[]{:S(2)}, u32[]{:S(2)}) async-start(bf16[4,192,768]{2,1,0:T(8,128)(2,1)} %add_parts.2.refs_0_), calls=%async_computation | async-start | bytes 2359296 | tf_op jit(solution)/shard_map/all_to_all | solution.py:885
  117.8 4.2 %norm_two_back.3 = (f32[512,768]{1,0:T(8,128)}, bf16[512,768]{1,0:T(8,128)(2,1)S(1)}, f32[8,768]{1,0:T(8,128)}) custom-call(s32[3]{0:T(128)S(1)} %pad_add_fusion.c_ref, bf16[4,192,768]{2,1,0:T(8,128)(2,1)} %add_parts.2.refs_0_, bf16[512,768]{1,0:T(8,128)(2,1)S(1)} %copy-done.7, bf16[512,768]{1,0:T(8,128)(2,1)S(1)} %copy-done.18, ...), custom_call_target="tpu_custom_call" | custom-call | flops 1966080 | bytes 1572864 | tf_op jit(solution)/shard_map/norm_two_back/pallas_call | solution.py:500
  122.0 1.8 broadcast_select_fusion.refs_0_
  123.8 1.0 collective-permute-start.14
  124.8 14.7 %attend_back.3 = (bf16[576,1024]{1,0:T(8,128)(2,1)}, f32[192,768]{1,0:T(8,128)}) custom-call(s32[3]{0:T(128)S(1)} %pad_add_fusion.c_ref, bf16[512,768]{1,0:T(8,128)(2,1)} %copy-done.28, bf16[512,768]{1,0:T(8,128)(2,1)S(1)} %get-tuple-element.122.refs_1_, bf16[512,768]{1,0:T(8,128)(2,1)S(1)} %collective-permute-done.20.refs_2_, bf16[192,1024]{1,0:T(8,128)(2,1)} %copy-done.15, ...), custom_call_target="tpu_custom_call" | custom-call | flops 1308622848 | bytes 1671168 | tf_op jit(solution)/shard_map/attend_back/pallas_call | solution.py:596
  139.5 4.3 %collective-permute-done.14.refs_1_ = bf16[512,768]{1,0:T(8,128)(2,1)S(1)} collective-permute-done((bf16[512,768]{1,0:T(8,128)(2,1)S(1)}, bf16[512,768]{1,0:T(8,128)(2,1)S(1)}, u32[]{:S(2)}, u32[]{:S(2)}) %collective-permute-start.14) | collective-permute-done | bytes 786464 | tf_op jit(solution)/shard_map/ppermute | solution.py:778
  143.8 2.4 all-to-all-done.refs_2_
  146.2 1.7 sum_parts.2.refs_0_
  147.9 3.7 %all-to-all-start.1 = ((bf16[4,192,768]{2,1,0:T(8,128)(2,1)}), bf16[4,192,768]{2,1,0:T(8,128)(2,1)S(1)}, u32[]{:S(2)}, u32[]{:S(2)}) async-start(bf16[4,192,768]{2,1,0:T(8,128)(2,1)} %sum_parts.2.refs_0_), calls=%async_computation.1 | async-start | bytes 2359296 | tf_op jit(solution)/shard_map/all_to_all | solution.py:885
  151.6 13.4 %project_back.1 = (bf16[512,768]{1,0:T(8,128)(2,1)}, bf16[512,768]{1,0:T(8,128)(2,1)}, bf16[512,768]{1,0:T(8,128)(2,1)}, bf16[512,768]{1,0:T(8,128)(2,1)}, f32[8...) custom-call(s32[3]{0:T(128)S(1)} %pad_add_fusion.c_ref, ...), custom_call_target="tpu_custom_call" | custom-call | flops 905969664 | bytes 4718592 | tf_op jit(solution)/shard_map/project_back/pallas_call | solution.py:719
  165.1 1.6 collective-permute-start.27
  166.7 13.4 %all-to-all-done.1.refs_0_.mine_ref = bf16[4,192,768]{2,1,0:T(8,128)(2,1)S(1)} async-done(((bf16[4,192,768]{2,1,0:T(8,128)(2,1)}), bf16[4,192,768]{2,1,0:T(8,128)(2,1)S(1)}, u32[]{:S(2)}, u32[]{:S(2)}) %all-to-all-start.1) | async-done | bytes 1179680 | tf_op jit(solution)/shard_map/all_to_all | solution.py:885
  180.0 1.5 collective-permute-start.26
  181.6 2.6 %add_parts.3 = bf16[4,96,768]{2,1,0:T(8,128)(2,1)} custom-call(s32[3]{0:T(128)S(1)} %pad_add_fusion.c_ref, bf16[4,192,768]{2,1,0:T(8,128)(2,1)} %copy-done.1, bf16[4,96,768]{2,1,0:T(8,128)(2,1)} %get-tuple-element.137.refs_1_, bf16[4,96,768]{2,1,0:T(8,128)(2,1)S(1)} %collective-permute-done.27.refs_2_), custom_call_target="tpu_custom_call" | custom-call | flops 73728 | bytes 442368 | tf_op jit(solution)/shard_map/add_parts/pallas_call | solution.py:798
  184.1 4.1 %all-to-all-start.2 = ((bf16[4,96,768]{2,1,0:T(8,128)(2,1)}), bf16[4,96,768]{2,1,0:T(8,128)(2,1)S(1)}, u32[]{:S(2)}, u32[]{:S(2)}) async-start(bf16[4,96,768]{2,1,0:T(8,128)(2,1)} %add_parts.3), calls=%async_computation.2 | async-start | bytes 1179648 | tf_op jit(solution)/shard_map/all_to_all | solution.py:885
  188.3 1.2 collective-permute-done.23
  189.5 0.9 collective-permute-start.24
  190.4 2.9 %collective-permute-done.24 = f32[8,768]{1,0:T(8,128)S(1)} collective-permute-done((f32[8,768]{1,0:T(8,128)S(1)}, f32[8,768]{1,0:T(8,128)S(1)}, u32[]{:S(2)}, u32[]{:S(2)}) %collective-permute-start.24) | collective-permute-done | bytes 24608 | tf_op jit(solution)/shard_map/ppermute | solution.py:778
  193.4 9.3 %all-to-all-done.2.refs_1_ = bf16[4,96,768]{2,1,0:T(8,128)(2,1)S(1)} async-done(((bf16[4,96,768]{2,1,0:T(8,128)(2,1)}), bf16[4,96,768]{2,1,0:T(8,128)(2,1)S(1)}, u32[]{:S(2)}, u32[]{:S(2)}) %all-to-all-start.2) | async-done | bytes 589856 | tf_op jit(solution)/shard_map/all_to_all | solution.py:885
  202.7 4.3 %collective-permute-done.26.refs_0_.theirs_ref = bf16[4,192,768]{2,1,0:T(8,128)(2,1)S(1)} collective-permute-done((bf16[4,192,768]{2,1,0:T(8,128)(2,1)S(1)}, bf16[4,192,768]{2,1,0:T(8,128)(2,1)S(1)}, u32[]{:S(2)}, u32[]{:S(2)}) %collective-permute-start.26) | collective-permute-done | bytes 1179680 | tf_op jit(solution)/shard_map/ppermute | solution.py:881
  207.0 1.0 copy-done.11
  208.0 1.5 sum_parts.3
  209.5 3.9 %all-to-all-start.3 = ((bf16[4,112,768]{2,1,0:T(8,128)(2,1)}), bf16[4,112,768]{2,1,0:T(8,128)(2,1)S(1)}, u32[]{:S(2)}, u32[]{:S(2)}) async-start(bf16[4,112,768]{2,1,0:T(8,128)(2,1)} %sum_parts.3), calls=%async_computation.3 | async-start | bytes 1376256 | tf_op jit(solution)/shard_map/all_to_all | solution.py:885
  213.4 2.3 add_convert_fusion
  215.7 0.9 collective-permute-start.25
  216.6 13.0 %all-to-all-done.3.mine_ref = bf16[4,112,768]{2,1,0:T(8,128)(2,1)S(1)} async-done(((bf16[4,112,768]{2,1,0:T(8,128)(2,1)}), bf16[4,112,768]{2,1,0:T(8,128)(2,1)S(1)}, u32[]{:S(2)}, u32[]{:S(2)}) %all-to-all-start.3) | async-done | bytes 688160 | tf_op jit(solution)/shard_map/all_to_all | solution.py:885
  229.6 1.5 collective-permute-start.28
  231.1 4.1 %add_convert_fusion.2 = bf16[512,768]{1,0:T(8,128)(2,1)} fusion(bf16[512,768]{1,0:T(8,128)(2,1)} %copy-done.29, f32[512,768]{1,0:T(8,128)} %get-tuple-element.102.refs_3_, f32[512,768]{1,0:T(8,128)} %get-tuple-element.103.refs_3_, f32[768]{0:T(1024)S(1)} %copy-done.32, pred[]{:T(512)S(6)} %ge.3, bf16[512,768]{1,0:T(8,128)(2,1)} %collective-permute-done.12, ...), kind=kLoop, calls=%fused_computation.2 | loop fusion | flops 6291456 | bytes 7867393 | tf_op jit(solution)/shard_map/convert_element_type | solution.py:1006
  235.8 3.7 %norm_one_back.1 = bf16[512,768]{1,0:T(8,128)(2,1)} custom-call(s32[1]{0:T(128)} %bitcast.6.m_ref, bf16[512,768]{1,0:T(8,128)(2,1)S(1)} %copy-done.23, bf16[512,768]{1,0:T(8,128)(2,1)S(1)} %collective-permute-done.21.got_ref, bf16[512,768]{1,0:T(8,128)(2,1)S(1)} %collective-permute-done.25.theirs_ref, bf16[2048,768]{1,0:T(8,128)(2,1)} %x_ref.1, ...), custom_call_target="tpu_custom_call" | custom-call | flops 1966080 | bytes 1572864 | tf_op jit(solution)/shard_map/norm_one_back/pallas_call | solution.py:751
  239.6 3.0 %place_parts.3 = (f32[768,768]{1,0:T(8,128)}, f32[768,768]{1,0:T(8,128)}) custom-call(s32[3]{0:T(128)S(1)} %pad_add_fusion.c_ref, bf16[4,192,768]{2,1,0:T(8,128)(2,1)S(1)} %copy-done.2, bf16[4,192,768]{2,1,0:T(8,128)(2,1)S(1)} %copy-done.12), custom_call_target="tpu_custom_call" | custom-call | flops 294912 | bytes 1769472 | tf_op jit(solution)/shard_map/place_parts/pallas_call | solution.py:868
  242.6 3.4 %collective-permute-done.28.theirs_ref = bf16[4,112,768]{2,1,0:T(8,128)(2,1)S(1)} collective-permute-done((bf16[4,112,768]{2,1,0:T(8,128)(2,1)S(1)}, bf16[4,112,768]{2,1,0:T(8,128)(2,1)S(1)}, u32[]{:S(2)}, u32[]{:S(2)}) %collective-permute-start.28) | collective-permute-done | bytes 688160 | tf_op jit(solution)/shard_map/ppermute | solution.py:881
  246.0 2.1 place_parts.2
  248.9 0.7 reshape_squeeze.9
  (120 shorter events, 6.7 us)
Async XLA Ops:
  0.6 22.1 %collective-permute-start = (bf16[192,768]{1,0:T(8,128)(2,1)}, bf16[192,768]{1,0:T(8,128)(2,1)S(1)}, u32[]{:S(2)}, u32[]{:S(2)}) collective-permute-start(bf16[192,768]{1,0:T(8,128)(2,1)} %refs_11_.4), channel_id=1, source_target_pairs={{0,1},{1,0},{2,3},{3,2},{4,5},{5,4},{6,7},{7,6},{8,9},{9,8},{10,11... | collective-permute-start | bytes 884744 | tf_op jit(solution)/shard_map/ppermute | solution.py:774
  1.2 19.2 %collective-permute-start.4 = (bf16[192,768]{1,0:T(8,128)(2,1)}, bf16[192,768]{1,0:T(8,128)(2,1)S(1)}, u32[]{:S(2)}, u32[]{:S(2)}) collective-permute-start(bf16[192,768]{1,0:T(8,128)(2,1)} %refs_11_.4), channel_id=1, source_target_pairs={{0,2},{1,3},{2,0},{3,1},{4,6},{5,7},{6,4},{7,5},{8,10},{9,11},{10,... | collective-permute-start | bytes 884744 | tf_op jit(solution)/shard_map/ppermute | solution.py:778
  7.3 4.9 %copy-start.24 = (s32[2048]{0:T(1024)S(1)}, s32[2048]{0:T(1024)}, u32[]{:S(2)}) copy-start(s32[2048]{0:T(1024)} %param.18) | copy-start | bytes 24580
  12.2 8.0 %copy-start.13 = (bf16[192,1024]{1,0:T(8,128)(2,1)}, bf16[192,1024]{1,0:T(8,128)(2,1)S(1)}, u32[]{:S(2)}) copy-start(bf16[192,1024]{1,0:T(8,128)(2,1)S(1)} %get-tuple-element.82.refs_0_.refs_3_.refs_1_) | copy-start | bytes 1179652
  12.2 8.0 %copy-start.14 = (bf16[192,1024]{1,0:T(8,128)(2,1)}, bf16[192,1024]{1,0:T(8,128)(2,1)S(1)}, u32[]{:S(2)}) copy-start(bf16[192,1024]{1,0:T(8,128)(2,1)S(1)} %get-tuple-element.83.refs_1_.refs_4_.refs_2_) | copy-start | bytes 1179652
  12.2 8.0 %copy-start.22 = (bf16[192,1024]{1,0:T(8,128)(2,1)}, bf16[192,1024]{1,0:T(8,128)(2,1)S(1)}, u32[]{:S(2)}) copy-start(bf16[192,1024]{1,0:T(8,128)(2,1)S(1)} %get-tuple-element.84.refs_2_.refs_5_) | copy-start | bytes 1179652
  12.5 15.9 %copy-start = (s32[2048,128]{1,0:T(8,128)}, s32[2048,128]{1,0:T(8,128)S(1)}, u32[]{:S(2)}) copy-start(s32[2048,128]{1,0:T(8,128)S(1)} %broadcast_in_dim.12.refs_5_.refs_6_.refs_10_) | copy-start | bytes 3145732
  20.2 1.5 collective-permute-start.1
  20.4 16.9 %collective-permute-start.5 = (bf16[192,768]{1,0:T(8,128)(2,1)S(1)}, bf16[192,768]{1,0:T(8,128)(2,1)S(1)}, u32[]{:S(2)}, u32[]{:S(2)}) collective-permute-start(bf16[192,768]{1,0:T(8,128)(2,1)S(1)} %collective-permute-done.4.refs_8_), channel_id=1, source_target_pairs={{0,1},{1,0},{2,3},{3,2},{4,5},{5,4},{6,7},{7,6},{8,9},{9,8},{10,11... | collective-permute-start | bytes 884744 | tf_op jit(solution)/shard_map/ppermute | solution.py:774
  20.7 16.5 %collective-permute-start.2 = (bf16[192,512]{1,0:T(8,128)(2,1)S(1)}, bf16[192,512]{1,0:T(8,128)(2,1)S(1)}, u32[]{:S(2)}, u32[]{:S(2)}) collective-permute-start(bf16[192,512]{1,0:T(8,128)(2,1)S(1)} %get-tuple-element.91.refs_2_), channel_id=1, source_target_pairs={{0,2},{1,3},{2,0},{3,1},{4,6},{5,7},{6,4},{7,5},{8,10},{9,11},{10,... | collective-permute-start | bytes 589832 | tf_op jit(solution)/shard_map/ppermute | solution.py:778
  21.7 15.6 %collective-permute-start.3 = (bf16[192,512]{1,0:T(8,128)(2,1)S(1)}, bf16[192,512]{1,0:T(8,128)(2,1)S(1)}, u32[]{:S(2)}, u32[]{:S(2)}) collective-permute-start(bf16[192,512]{1,0:T(8,128)(2,1)S(1)} %collective-permute-done.1.refs_3_), channel_id=1, source_target_pairs={{0,2},{1,3},{2,0},{3,1},{4,6},{5,7},{6,4},{7,5},{8,10},{9,11},{10,... | collective-permute-start | bytes 589832 | tf_op jit(solution)/shard_map/ppermute | solution.py:778
  28.4 7.7 %copy-start.15 = (bf16[192,1024]{1,0:T(8,128)(2,1)}, bf16[192,1024]{1,0:T(8,128)(2,1)S(1)}, u32[]{:S(2)}) copy-start(bf16[192,1024]{1,0:T(8,128)(2,1)S(1)} %get-tuple-element.87.refs_1_.refs_3_.refs_5_) | copy-start | bytes 1179652
  28.4 7.7 %copy-start.16 = (bf16[192,1024]{1,0:T(8,128)(2,1)}, bf16[192,1024]{1,0:T(8,128)(2,1)S(1)}, u32[]{:S(2)}) copy-start(bf16[192,1024]{1,0:T(8,128)(2,1)S(1)} %get-tuple-element.88.refs_2_.refs_4_.refs_6_) | copy-start | bytes 1179652
  28.4 7.7 %copy-start.21 = (bf16[192,1024]{1,0:T(8,128)(2,1)}, bf16[192,1024]{1,0:T(8,128)(2,1)S(1)}, u32[]{:S(2)}) copy-start(bf16[192,1024]{1,0:T(8,128)(2,1)S(1)} %get-tuple-element.89.refs_3_.refs_5_) | copy-start | bytes 1179652
  28.4 8.8 %copy-start.33 = (f32[768]{0:T(1024)S(1)}, f32[768]{0:T(1024)}, u32[]{:S(2)}) copy-start(f32[768]{0:T(1024)} %param.26) | copy-start | bytes 9220
  28.4 8.7 %copy-start.34 = (f32[768]{0:T(1024)S(1)}, f32[768]{0:T(1024)}, u32[]{:S(2)}) copy-start(f32[768]{0:T(1024)} %param.27) | copy-start | bytes 9220
  28.5 8.8 %copy-start.35 = (f32[768]{0:T(1024)S(1)}, f32[768]{0:T(1024)}, u32[]{:S(2)}) copy-start(f32[768]{0:T(1024)} %param.28) | copy-start | bytes 9220
  28.5 8.8 %copy-start.8 = (bf16[192,768]{1,0:T(8,128)(2,1)S(1)}, bf16[192,768]{1,0:T(8,128)(2,1)}, u32[]{:S(2)}) copy-start(bf16[192,768]{1,0:T(8,128)(2,1)} %refs_11_.4) | copy-start | bytes 884740
  28.5 8.8 %copy-start.20 = (bf16[192,768]{1,0:T(8,128)(2,1)S(1)}, bf16[192,768]{1,0:T(8,128)(2,1)}, u32[]{:S(2)}) copy-start(bf16[192,768]{1,0:T(8,128)(2,1)} %copy-done.19) | copy-start | bytes 884740
  36.1 5.6 %collective-permute-start.6 = (bf16[192,512]{1,0:T(8,128)(2,1)S(1)}, bf16[192,512]{1,0:T(8,128)(2,1)S(1)}, u32[]{:S(2)}, u32[]{:S(2)}) collective-permute-start(bf16[192,512]{1,0:T(8,128)(2,1)S(1)} %get-tuple-element.94), channel_id=1, source_target_pairs={{0,1},{1,0},{2,3},{3,2},{4,5},{5,4},{6,7},{7,6},{8,9},{9,8},{10,11... | collective-permute-start | bytes 589832 | tf_op jit(solution)/shard_map/ppermute | solution.py:774
  36.2 7.3 %collective-permute-start.7 = (bf16[192,512]{1,0:T(8,128)(2,1)S(1)}, bf16[192,512]{1,0:T(8,128)(2,1)S(1)}, u32[]{:S(2)}, u32[]{:S(2)}) collective-permute-start(bf16[192,512]{1,0:T(8,128)(2,1)S(1)} %get-tuple-element.95.refs_2_), channel_id=1, source_target_pairs={{0,2},{1,3},{2,0},{3,1},{4,6},{5,7},{6,4},{7,5},{8,10},{9,11},{10,... | collective-permute-start | bytes 589832 | tf_op jit(solution)/shard_map/ppermute | solution.py:778
  37.3 7.2 %copy-start.36 = (f32[768]{0:T(1024)S(1)}, f32[768]{0:T(1024)}, u32[]{:S(2)}) copy-start(f32[768]{0:T(1024)} %param.30) | copy-start | bytes 9220
  37.3 8.7 %copy-start.9 = (bf16[768,768]{1,0:T(8,128)(2,1)S(1)}, bf16[768,768]{1,0:T(8,128)(2,1)}, u32[]{:S(2)}) copy-start(bf16[768,768]{1,0:T(8,128)(2,1)} %refs_4_.3) | copy-start | bytes 3538948
  37.3 8.7 %copy-start.10 = (bf16[768,768]{1,0:T(8,128)(2,1)S(1)}, bf16[768,768]{1,0:T(8,128)(2,1)}, u32[]{:S(2)}) copy-start(bf16[768,768]{1,0:T(8,128)(2,1)} %refs_6_.5) | copy-start | bytes 3538948
  43.5 2.5 collective-permute-start.8
  43.5 15.1 %collective-permute-start.9 = (bf16[192,512]{1,0:T(8,128)(2,1)S(1)}, bf16[192,512]{1,0:T(8,128)(2,1)S(1)}, u32[]{:S(2)}, u32[]{:S(2)}) collective-permute-start(bf16[192,512]{1,0:T(8,128)(2,1)S(1)} %collective-permute-done.6.refs_3_), channel_id=1, source_target_pairs={{0,2},{1,3},{2,0},{3,1},{4,6},{5,7},{6,4},{7,5},{8,10},{9,11},{10,... | collective-permute-start | bytes 589832 | tf_op jit(solution)/shard_map/ppermute | solution.py:778
  58.6 4.8 %collective-permute-start.10 = (bf16[512,768]{1,0:T(8,128)(2,1)}, bf16[512,768]{1,0:T(8,128)(2,1)S(1)}, u32[]{:S(2)}, u32[]{:S(2)}) collective-permute-start(bf16[512,768]{1,0:T(8,128)(2,1)} %get-tuple-element.105), channel_id=1, source_target_pairs={{0,1},{1,0},{2,3},{3,2},{4,5},{5,4},{6,7},{7,6},{8,9},{9,8},{10,11... | collective-permute-start | bytes 2359304 | tf_op jit(solution)/shard_map/ppermute | solution.py:774
  63.0 2.5 %copy-start.25 = (f32[8,768]{1,0:T(8,128)S(1)}, f32[8,768]{1,0:T(8,128)}, u32[]{:S(2)}) copy-start(f32[8,768]{1,0:T(8,128)} %get-tuple-element.97.refs_0_.refs_7_) | copy-start | bytes 73732
  63.0 2.5 collective-permute-start.11
  63.6 1.9 copy-start.4
  63.6 19.6 %collective-permute-start.16 = (bf16[512,768]{1,0:T(8,128)(2,1)S(1)}, bf16[512,768]{1,0:T(8,128)(2,1)S(1)}, u32[]{:S(2)}, u32[]{:S(2)}) collective-permute-start(bf16[512,768]{1,0:T(8,128)(2,1)S(1)} %add_convert_fusion.5.refs_0_.refs_1_), channel_id=1, source_target_pairs={{0,2},{1,3},{2,0},{3,1},{4,6},{5,7},{6,4},{7,5},{8,10},{9,11},{10,... | collective-permute-start | bytes 2359304 | tf_op jit(solution)/shard_map/ppermute | solution.py:778
  78.6 10.0 %collective-permute-start.15 = (bf16[512,768]{1,0:T(8,128)(2,1)}, bf16[512,768]{1,0:T(8,128)(2,1)S(1)}, u32[]{:S(2)}, u32[]{:S(2)}) collective-permute-start(bf16[512,768]{1,0:T(8,128)(2,1)} %get-tuple-element.114), channel_id=1, source_target_pairs={{0,1},{1,0},{2,3},{3,2},{4,5},{5,4},{6,7},{7,6},{8,9},{9,8},{10,11... | collective-permute-start | bytes 2359304 | tf_op jit(solution)/shard_map/ppermute | solution.py:774
  79.0 28.2 %collective-permute-start.19 = (bf16[4,192,768]{2,1,0:T(8,128)(2,1)}, bf16[4,192,768]{2,1,0:T(8,128)(2,1)S(1)}, u32[]{:S(2)}, u32[]{:S(2)}) collective-permute-start(bf16[4,192,768]{2,1,0:T(8,128)(2,1)} %get-tuple-element.120), channel_id=1, source_target_pairs={{0,4},{4,0},{8,12},{12,8},{16,20},{20,16},{24,28},{28,24},{1,5},{5... | collective-permute-start | bytes 3538952 | tf_op jit(solution)/shard_map/ppermute | solution.py:881
  88.6 2.3 collective-permute-start.17
  88.8 2.1 copy-start.6
  88.8 20.0 %collective-permute-start.18 = (bf16[512,768]{1,0:T(8,128)(2,1)S(1)}, bf16[512,768]{1,0:T(8,128)(2,1)S(1)}, u32[]{:S(2)}, u32[]{:S(2)}) collective-permute-start(bf16[512,768]{1,0:T(8,128)(2,1)S(1)} %add_convert_fusion.1.refs_0_.refs_1_), channel_id=1, source_target_pairs={{0,2},{1,3},{2,0},{3,1},{4,6},{5,7},{6,4},{7,5},{8,10},{9,11},{10,... | collective-permute-start | bytes 2359304 | tf_op jit(solution)/shard_map/ppermute | solution.py:778
  89.8 32.2 %collective-permute-start.13 = (bf16[512,768]{1,0:T(8,128)(2,1)}, bf16[512,768]{1,0:T(8,128)(2,1)}, u32[]{:S(2)}, u32[]{:S(2)}) collective-permute-start(bf16[512,768]{1,0:T(8,128)(2,1)} %get-tuple-element.112), channel_id=1, source_target_pairs={{0,1},{1,0},{2,3},{3,2},{4,5},{5,4},{6,7},{7,6},{8,9},{9,8},{10,11... | collective-permute-start | bytes 2359304 | tf_op jit(solution)/shard_map/ppermute | solution.py:774
  90.0 32.0 %collective-permute-start.12 = (bf16[512,768]{1,0:T(8,128)(2,1)}, bf16[512,768]{1,0:T(8,128)(2,1)}, u32[]{:S(2)}, u32[]{:S(2)}) collective-permute-start(bf16[512,768]{1,0:T(8,128)(2,1)} %get-tuple-element.110), channel_id=1, source_target_pairs={{0,1},{1,0},{2,3},{3,2},{4,5},{5,4},{6,7},{7,6},{8,9},{9,8},{10,11... | collective-permute-start | bytes 2359304 | tf_op jit(solution)/shard_map/ppermute | solution.py:774
  112.7 5.0 %copy-start.7 = (bf16[512,768]{1,0:T(8,128)(2,1)S(1)}, bf16[512,768]{1,0:T(8,128)(2,1)}, u32[]{:S(2)}) copy-start(bf16[512,768]{1,0:T(8,128)(2,1)} %copy-done.6) | copy-start | bytes 2359300
  112.7 5.0 %copy-start.18 = (bf16[512,768]{1,0:T(8,128)(2,1)S(1)}, bf16[512,768]{1,0:T(8,128)(2,1)}, u32[]{:S(2)}) copy-start(bf16[512,768]{1,0:T(8,128)(2,1)} %copy-done.17) | copy-start | bytes 2359300
  112.8 33.4 %all-to-all-start = ((bf16[4,192,768]{2,1,0:T(8,128)(2,1)}), bf16[4,192,768]{2,1,0:T(8,128)(2,1)S(1)}, u32[]{:S(2)}, u32[]{:S(2)}) async-start(bf16[4,192,768]{2,1,0:T(8,128)(2,1)} %add_parts.2.refs_0_), calls=%async_computation | async-start | bytes 2359296 | tf_op jit(solution)/shard_map/all_to_all | solution.py:885
  117.8 4.2 %copy-start.26 = (bf16[512,768]{1,0:T(8,128)(2,1)S(1)}, bf16[512,768]{1,0:T(8,128)(2,1)}, u32[]{:S(2)}) copy-start(bf16[512,768]{1,0:T(8,128)(2,1)} %get-tuple-element.111) | copy-start | bytes 2359300
  117.8 4.2 %copy-start.27 = (bf16[512,768]{1,0:T(8,128)(2,1)S(1)}, bf16[512,768]{1,0:T(8,128)(2,1)}, u32[]{:S(2)}) copy-start(bf16[512,768]{1,0:T(8,128)(2,1)} %get-tuple-element.109) | copy-start | bytes 2359300
  121.9 2.9 %collective-permute-start.20 = (bf16[512,768]{1,0:T(8,128)(2,1)S(1)}, bf16[512,768]{1,0:T(8,128)(2,1)S(1)}, u32[]{:S(2)}, u32[]{:S(2)}) collective-permute-start(bf16[512,768]{1,0:T(8,128)(2,1)S(1)} %get-tuple-element.122.refs_1_), channel_id=1, source_target_pairs={{0,1},{1,0},{2,3},{3,2},{4,5},{5,4},{6,7},{7,6},{8,9},{9,8},{10,11... | collective-permute-start | bytes 2359304 | tf_op jit(solution)/shard_map/ppermute | solution.py:774
  123.8 20.0 %collective-permute-start.14 = (bf16[512,768]{1,0:T(8,128)(2,1)S(1)}, bf16[512,768]{1,0:T(8,128)(2,1)S(1)}, u32[]{:S(2)}, u32[]{:S(2)}) collective-permute-start(bf16[512,768]{1,0:T(8,128)(2,1)S(1)} %broadcast_select_fusion.refs_0_), channel_id=1, source_target_pairs={{0,2},{1,3},{2,0},{3,1},{4,6},{5,7},{6,4},{7,5},{8,10},{9,11},{10,... | collective-permute-start | bytes 2359304 | tf_op jit(solution)/shard_map/ppermute | solution.py:778
  143.8 2.4 copy-start.29
  147.9 3.7 %copy-start.3 = (bf16[768,3,192]{0,2,1:T(8,128)(2,1)S(1)}, bf16[768,3,192]{0,2,1:T(8,128)(2,1)}, u32[]{:S(2)}) copy-start(bf16[768,3,192]{0,2,1:T(8,128)(2,1)} %param.22) | copy-start | bytes 2654212
  147.9 32.1 %all-to-all-start.1 = ((bf16[4,192,768]{2,1,0:T(8,128)(2,1)}), bf16[4,192,768]{2,1,0:T(8,128)(2,1)S(1)}, u32[]{:S(2)}, u32[]{:S(2)}) async-start(bf16[4,192,768]{2,1,0:T(8,128)(2,1)} %sum_parts.2.refs_0_), calls=%async_computation.1 | async-start | bytes 2359296 | tf_op jit(solution)/shard_map/all_to_all | solution.py:885
  165.1 16.5 %collective-permute-start.27 = (bf16[4,96,768]{2,1,0:T(8,128)(2,1)}, bf16[4,96,768]{2,1,0:T(8,128)(2,1)S(1)}, u32[]{:S(2)}, u32[]{:S(2)}) collective-permute-start(bf16[4,96,768]{2,1,0:T(8,128)(2,1)} %get-tuple-element.138), channel_id=1, source_target_pairs={{0,4},{4,0},{8,12},{12,8},{16,20},{20,16},{24,28},{28,24},{1,5},{5... | collective-permute-start | bytes 1769480 | tf_op jit(solution)/shard_map/ppermute | solution.py:881
  180.0 26.9 %collective-permute-start.26 = (bf16[4,192,768]{2,1,0:T(8,128)(2,1)S(1)}, bf16[4,192,768]{2,1,0:T(8,128)(2,1)S(1)}, u32[]{:S(2)}, u32[]{:S(2)}) collective-permute-start(bf16[4,192,768]{2,1,0:T(8,128)(2,1)S(1)} %all-to-all-done.1.refs_0_.mine_ref), channel_id=1, source_target_pairs={{0,4},{4,0},{8,12},{12,8},{16,20},{20,16},{24,28},{28,24},{1,5},{5... | collective-permute-start | bytes 3538952 | tf_op jit(solution)/shard_map/ppermute | solution.py:881
  181.6 6.7 %copy-start.31 = (f32[8,768]{1,0:T(8,128)S(1)}, f32[8,768]{1,0:T(8,128)}, u32[]{:S(2)}) copy-start(f32[8,768]{1,0:T(8,128)} %get-tuple-element.133) | copy-start | bytes 73732
  184.1 18.6 %all-to-all-start.2 = ((bf16[4,96,768]{2,1,0:T(8,128)(2,1)}), bf16[4,96,768]{2,1,0:T(8,128)(2,1)S(1)}, u32[]{:S(2)}, u32[]{:S(2)}) async-start(bf16[4,96,768]{2,1,0:T(8,128)(2,1)} %add_parts.3), calls=%async_computation.2 | async-start | bytes 1179648 | tf_op jit(solution)/shard_map/all_to_all | solution.py:885
  188.2 1.2 collective-permute-start.23
  189.5 3.8 %collective-permute-start.24 = (f32[8,768]{1,0:T(8,128)S(1)}, f32[8,768]{1,0:T(8,128)S(1)}, u32[]{:S(2)}, u32[]{:S(2)}) collective-permute-start(f32[8,768]{1,0:T(8,128)S(1)} %select_add_fusion.1), channel_id=1, source_target_pairs={{0,2},{1,3},{2,0},{3,1},{4,6},{5,7},{6,4},{7,5},{8,10},{9,11},{10,... | collective-permute-start | bytes 73736 | tf_op jit(solution)/shard_map/ppermute | solution.py:778
  190.4 23.0 %collective-permute-start.22 = (bf16[512,768]{1,0:T(8,128)(2,1)}, bf16[512,768]{1,0:T(8,128)(2,1)}, u32[]{:S(2)}, u32[]{:S(2)}) collective-permute-start(bf16[512,768]{1,0:T(8,128)(2,1)} %get-tuple-element.132), channel_id=1, source_target_pairs={{0,1},{1,0},{2,3},{3,2},{4,5},{5,4},{6,7},{7,6},{8,9},{9,8},{10,11... | collective-permute-start | bytes 2359304 | tf_op jit(solution)/shard_map/ppermute | solution.py:774
  209.4 4.0 %copy-start.30 = (bf16[512,768]{1,0:T(8,128)(2,1)S(1)}, bf16[512,768]{1,0:T(8,128)(2,1)}, u32[]{:S(2)}) copy-start(bf16[512,768]{1,0:T(8,128)(2,1)} %get-tuple-element.131) | copy-start | bytes 2359300
  209.4 21.7 %copy-start.32 = (f32[768]{0:T(1024)S(1)}, f32[768]{0:T(1024)}, u32[]{:S(2)}) copy-start(f32[768]{0:T(1024)} %param.32) | copy-start | bytes 9220
  209.5 20.2 %all-to-all-start.3 = ((bf16[4,112,768]{2,1,0:T(8,128)(2,1)}), bf16[4,112,768]{2,1,0:T(8,128)(2,1)S(1)}, u32[]{:S(2)}, u32[]{:S(2)}) async-start(bf16[4,112,768]{2,1,0:T(8,128)(2,1)} %sum_parts.3), calls=%async_computation.3 | async-start | bytes 1376256 | tf_op jit(solution)/shard_map/all_to_all | solution.py:885
  213.3 21.9 %collective-permute-start.21 = (bf16[512,768]{1,0:T(8,128)(2,1)}, bf16[512,768]{1,0:T(8,128)(2,1)S(1)}, u32[]{:S(2)}, u32[]{:S(2)}) collective-permute-start(bf16[512,768]{1,0:T(8,128)(2,1)} %get-tuple-element.130), channel_id=1, source_target_pairs={{0,1},{1,0},{2,3},{3,2},{4,5},{5,4},{6,7},{7,6},{8,9},{9,8},{10,11... | collective-permute-start | bytes 2359304 | tf_op jit(solution)/shard_map/ppermute | solution.py:774
  215.7 20.1 %copy-start.23 = (bf16[512,768]{1,0:T(8,128)(2,1)S(1)}, bf16[512,768]{1,0:T(8,128)(2,1)}, u32[]{:S(2)}) copy-start(bf16[512,768]{1,0:T(8,128)(2,1)} %get-tuple-element.129.mine_ref) | copy-start | bytes 2359300
  215.7 20.1 %collective-permute-start.25 = (bf16[512,768]{1,0:T(8,128)(2,1)}, bf16[512,768]{1,0:T(8,128)(2,1)S(1)}, u32[]{:S(2)}, u32[]{:S(2)}) collective-permute-start(bf16[512,768]{1,0:T(8,128)(2,1)} %add_convert_fusion), channel_id=1, source_target_pairs={{0,2},{1,3},{2,0},{3,1},{4,6},{5,7},{6,4},{7,5},{8,10},{9,11},{10,... | collective-permute-start | bytes 2359304 | tf_op jit(solution)/shard_map/ppermute | solution.py:778
  229.6 16.4 %collective-permute-start.28 = (bf16[4,112,768]{2,1,0:T(8,128)(2,1)S(1)}, bf16[4,112,768]{2,1,0:T(8,128)(2,1)S(1)}, u32[]{:S(2)}, u32[]{:S(2)}) collective-permute-start(bf16[4,112,768]{2,1,0:T(8,128)(2,1)S(1)} %all-to-all-done.3.mine_ref), channel_id=1, source_target_pairs={{0,4},{4,0},{8,12},{12,8},{16,20},{20,16},{24,28},{28,24},{1,5},{5... | collective-permute-start | bytes 2064392 | tf_op jit(solution)/shard_map/ppermute | solution.py:881
  235.8 3.7 %copy-start.2 = (bf16[4,192,768]{2,1,0:T(8,128)(2,1)S(1)}, bf16[4,192,768]{2,1,0:T(8,128)(2,1)}, u32[]{:S(2)}) copy-start(bf16[4,192,768]{2,1,0:T(8,128)(2,1)} %copy-done.1) | copy-start | bytes 3538948
  235.8 3.7 %copy-start.12 = (bf16[4,192,768]{2,1,0:T(8,128)(2,1)S(1)}, bf16[4,192,768]{2,1,0:T(8,128)(2,1)}, u32[]{:S(2)}) copy-start(bf16[4,192,768]{2,1,0:T(8,128)(2,1)} %copy-done.11) | copy-start | bytes 3538948
  (6 other events, 6.3 us)

commit v4 on v3

--- a/solution.py
+++ b/solution.py
@@ -844,7 +844,7 @@
 
 
 def place_parts_kernel(with_small, c_ref, mine_ref, theirs_ref, *refs):
-    outs = refs[: len(refs) - with_small]
+    outs = refs[: len(refs) - 3 * with_small]
     count = mine_ref.shape[0]
     small = None
     for ref, half in ((mine_ref, c_ref[1]), (theirs_ref, 1 - c_ref[1])):
@@ -859,14 +859,23 @@
                 part = ref[k, at : at + 8, :].astype(f32) + ref[k, at + 8 : at + 16, :].astype(f32)
                 small = part if small is None else small + part
     if with_small:
-        refs[-1][...] = small
-
-
-def place_parts(core, mine, theirs, splits, with_small=False):
+        small_ref, bias_ref, rope_ref = refs[-3:]
+        small_ref[...] = small
+        width = bias_ref.shape[1]
+        heads = rope_ref.shape[0]
+        for k in range(3):
+            bias_ref[k : k + 1, :] = small[7:8, k * width : (k + 1) * width]
+        for h in range(heads):
+            for k in range(2):
+                at = 3 * width + (k * heads + h) * HALF
+                rope_ref[h : h + 1, k * HALF : (k + 1) * HALF] = small[7:8, at : at + HALF]
+
+
+def place_parts(core, mine, theirs, splits, with_small=()):
     d = mine.shape[2]
-    shapes = [(rows, d) for rows in splits] + [(8, d)] * with_small
-    return pl.pallas_call(
-        functools.partial(place_parts_kernel, with_small),
+    shapes = [(rows, d) for rows in splits] + list(with_small)
+    return pl.pallas_call(
+        functools.partial(place_parts_kernel, bool(with_small)),
         grid_spec=pltpu.PrefetchScalarGridSpec(
             num_scalar_prefetch=1, grid=(1,), in_specs=[full(mine.shape)] * 2, out_specs=[full(t) for t in shapes],
         ),
@@ -959,7 +968,7 @@
     )
     event = dwo
     if tree:
-        feed_part = add_parts(core, feed_keep, feed_got, wait=[dwo, n2_far1])
+        feed_part = add_low(feed_keep, after(feed_got, dwo, n2_far1))
         event = feed_part
         feed_got = quarter_trade(feed_part)
     rgrad1, branch1, small_two = norm_two_back(
@@ -1007,18 +1016,17 @@
     grad_rows = norm_one_back(place_arr, n1_keep, n1_got, theirs, patches, rgrad0, rgrad1, gain1)
     up_grad, down_grad = place_parts(core, feed_all, feed_other, (d, units))
     (grad_other,) = hold([grad_other], grad_rows)
-    qkv_grad, out_grad_w, small = place_parts(core, grad_sum, grad_other, (3 * width, width), True)
-    turns = heads * HALF
-    by_col = small[7, 3 * width : 3 * width + turns].reshape(heads, HALF)
-    by_row = small[7, 3 * width + turns : 3 * width + 2 * turns].reshape(heads, HALF)
+    qkv_grad, out_grad_w, small, bias_grad, rope_grad = place_parts(
+        core, grad_sum, grad_other, (3 * width, width), ((8, d), (3, width), (heads, HD))
+    )
     return (
         out_rows,
         grad_rows,
         small[0],
         small[1],
         qkv_grad.reshape(3, width, d).transpose(2, 0, 1),
-        small[7, : 3 * width].reshape(3, width),
-        jnp.concatenate([by_col, by_row], axis=-1),
+        bias_grad,
+        rope_grad,
         out_grad_w,
         small[4],
         small[2],

time: 251 us -> 247 us (0.984)
    pallas_call x2 -> x1, Pallas kernels: 5.64 us -> 2.61 us  [add_parts(): pl.pallas_call(ignoring(len(wait), add_kernel), grid_spec=pltpu.PrefetchS...]
  transfers between devices with their start and end apart: 33 -> 33, of which waited for: 18 -> 18; matrix products, arithmetic and copies ran while one was open for 4% -> 5% of each run, Pallas kernels for 50% -> 51%
where the time goes in v4:
time: 247 us; the launch traced here: 246 us
  Pallas kernels  129 us (52%)
  waiting for transfers between devices  65 us (26%)
  starting transfers between devices  36.1 us (15%)
  other arithmetic  9.99 us (4%)
  local copies, waits for them, and re-layouts  5.38 us (2%)
    all_to_all x4, waiting for transfers between devices, quarter_trade(): lax.all_to_all(parts, 'dp', 0, 0, axis_index_groups=[[0, 2, 4, 6], [1, 3,...  38 us
    pallas_call x2, Pallas kernels, attend_back(): pl.pallas_call(ignoring(len(wait), functools.partial(attend_back_kernel,...  30.6 us
    pallas_call x2, Pallas kernels, feed(): pl.pallas_call(ignoring(len(wait), functools.partial(feed_kernel, first,...  25.8 us
    all_to_all x4, starting transfers between devices, quarter_trade(): lax.all_to_all(parts, 'dp', 0, 0, axis_index_groups=[[0, 2, 4, 6], [1, 3,...  16.7 us
    pallas_call x2, Pallas kernels, attend(): pl.pallas_call(ignoring(len(wait), attend_kernel), grid_spec=pltpu.Prefet...  15.3 us
    pallas_call x1, Pallas kernels, project_back(): pl.pallas_call(ignoring(len(wait), project_back_kernel), grid_spec=pltpu....  13.5 us
    ppermute x10, waiting for transfers between devices, chip_swap(): return lax.ppermute(value, 'mp', CHIP_SWAP)  12.3 us
    ppermute x10, starting transfers between devices, chip_swap(): return lax.ppermute(value, 'mp', CHIP_SWAP)  10.5 us
  transfers between devices with their start and end apart: 33, of which 18 were waited for; matrix products, arithmetic and copies ran while one was open for 5% of the time, Pallas kernels for 51%

profile of v4, /device:TPU:0, one launch (start us, length us, event | category | flops | bytes accessed | tf_op | source)
XLA Modules:
  0.0 246.1 jit_solution(1879496400197411017)
XLA Ops:
  1.2 2.6 %collective-permute-start.4 = (bf16[192,768]{1,0:T(8,128)(2,1)}, bf16[192,768]{1,0:T(8,128)(2,1)S(1)}, u32[]{:S(2)}, u32[]{:S(2)}) collective-permute-start(bf16[192,768]{1,0:T(8,128)(2,1)} %refs_11_.4), channel_id=1, source_target_pairs={{0,2},{1,3},{2,0},{3,1},{4,6},{5,7},{6,4},{7,5},{8,10},{9,11},{10,... | collective-permute-start | bytes 884744 | tf_op jit(solution)/shard_map/ppermute | solution.py:778
  3.8 0.7 reshape.64.refs_5_.refs_7_.refs_12_.gain_ref
  4.5 0.7 reshape.65.refs_6_.refs_8_.refs_13_
  5.2 2.1 prepare.1
  7.3 4.9 %project.2 = (bf16[1024,768]{1,0:T(8,128)(2,1)}, bf16[192,1024]{1,0:T(8,128)(2,1)S(1)}, bf16[192,1024]{1,0:T(8,128)(2,1)S(1)}, bf16[192,1024]{1,0:T(8,128)(2,1)S(1)}) custom-call(s32[3]{0:T(128)S(1)} %pad_add_fusion.c_ref, bf16[2048,768]{1,0:T(8,128)(2,1)} %x_ref.1, s32[2,2048]{1,0:T(2,128)} %refs_11_.5, ...), custom_call_target="tpu_custom_call" | custom-call | flops 226492416 | bytes 1302528 | tf_op jit(solution)/shard_map/project/pallas_call | solution.py:152
  12.6 7.6 %attend.2 = (bf16[192,512]{1,0:T(8,128)(2,1)S(1)}, bf16[192,512]{1,0:T(8,128)(2,1)S(1)}, f32[192,1024]{1,0:T(8,128)}, f32[8,1024]{1,0:T(8,128)}) custom-call(s32[3]{0:T(128)S(1)} %pad_add_fusion.c_ref, bf16[192,1024]{1,0:T(8,128)(2,1)S(1)} %get-tuple-element.85.refs_0_.refs_3_.refs_1_, bf16[192,1024]{1,0:T(8,128)(2,1)S(1)} %get-tuple-element.86.refs_1_.refs_4_.refs_2_, ...), custom_call_target="tpu_custom_call" | custom-call | flops 402653184 | bytes 589824 | tf_op jit(solution)/shard_map/attend/pallas_call | solution.py:257
  20.9 0.9 collective-permute-done.1.refs_3_
  21.7 1.1 collective-permute-start.3
  22.8 0.7 copy-done.17
  23.5 4.9 %project.3 = (bf16[1024,768]{1,0:T(8,128)(2,1)}, bf16[192,1024]{1,0:T(8,128)(2,1)S(1)}, bf16[192,1024]{1,0:T(8,128)(2,1)S(1)}, bf16[192,1024]{1,0:T(8,128)(2,1)S(1)}) custom-call(s32[3]{0:T(128)S(1)} %pad_add_fusion.c_ref, f32[8,1024]{1,0:T(8,128)} %get-tuple-element.88.refs_0_.refs_7_, bf16[192,768]{1,0:T(8,128)(2,1)} %copy-done.17, ...), custom_call_target="tpu_custom_call" | custom-call | flops 226492416 | bytes 1302528 | tf_op jit(solution)/shard_map/project/pallas_call | solution.py:152
  28.5 7.6 %attend.3 = (bf16[192,512]{1,0:T(8,128)(2,1)S(1)}, bf16[192,512]{1,0:T(8,128)(2,1)S(1)}, f32[192,1024]{1,0:T(8,128)}, f32[8,1024]{1,0:T(8,128)}) custom-call(s32[3]{0:T(128)S(1)} %pad_add_fusion.c_ref, bf16[1024,768]{1,0:T(8,128)(2,1)} %get-tuple-element.89.refs_0_.refs_8_, bf16[192,1024]{1,0:T(8,128)(2,1)S(1)} %get-tuple-element.90.refs_1_.refs_3_.refs_5_, ...), custom_call_target="tpu_custom_call" | custom-call | flops 402653184 | bytes 589824 | tf_op jit(solution)/shard_map/attend/pallas_call | solution.py:257
  36.3 1.0 collective-permute-start.7
  37.4 4.4 %norm_two.2 = (f32[512,768]{1,0:T(8,128)}, bf16[512,768]{1,0:T(8,128)(2,1)}) custom-call(s32[3]{0:T(128)S(1)} %pad_add_fusion.c_ref, f32[8,1024]{1,0:T(8,128)} %get-tuple-element.93.refs_0_.refs_7_, bf16[2048,768]{1,0:T(8,128)(2,1)} %x_ref.1, bf16[192,512]{1,0:T(8,128)(2,1)S(1)} %get-tuple-element.94.refs_2_, ...), custom_call_target="tpu_custom_call" | custom-call | flops 150994944 | bytes 1179648 | tf_op jit(solution)/shard_map/norm_two/pallas_call | solution.py:314
  41.8 1.8 collective-permute-done.7.refs_4_
  43.6 0.9 collective-permute-start.9
  44.5 1.6 collective-permute-done.8.refs_1_
  46.1 12.7 %feed.2 = (bf16[512,768]{1,0:T(8,128)(2,1)}, bf16[512,768]{1,0:T(8,128)(2,1)}, bf16[512,768]{1,0:T(8,128)(2,1)}, bf16[512,768]{1,0:T(8,128)(2,1)S(1)}, f32[8,768...) custom-call(s32[3]{0:T(128)S(1)} %pad_add_fusion.c_ref, bf16[512,768]{1,0:T(8,128)(2,1)} %get-tuple-element.99.refs_0_, ...), custom_call_target="tpu_custom_call" | custom-call | flops 1811939328 | bytes 3342336 | tf_op jit(solution)/shard_map/feed/pallas_call | solution.py:434
  59.0 4.2 %norm_two.3 = (f32[512,768]{1,0:T(8,128)}, bf16[512,768]{1,0:T(8,128)(2,1)}) custom-call(s32[3]{0:T(128)S(1)} %pad_add_fusion.c_ref, f32[8,768]{1,0:T(8,128)} %get-tuple-element.100.refs_0_.refs_7_, bf16[2048,768]{1,0:T(8,128)(2,1)} %x_ref.1, bf16[192,512]{1,0:T(8,128)(2,1)S(1)} %get-tuple-element.98.refs_2_, ...), custom_call_target="tpu_custom_call" | custom-call | flops 150994944 | bytes 1179648 | tf_op jit(solution)/shard_map/norm_two/pallas_call | solution.py:314
  63.8 1.0 collective-permute-start.17
  64.8 0.9 collective-permute-done.11.refs_2_
  65.7 13.2 %feed.3 = (bf16[512,768]{1,0:T(8,128)(2,1)}, bf16[512,768]{1,0:T(8,128)(2,1)}, bf16[512,768]{1,0:T(8,128)(2,1)}, bf16[512,768]{1,0:T(8,128)(2,1)S(1)}, f32[8,768...) custom-call(s32[3]{0:T(128)S(1)} %pad_add_fusion.c_ref, bf16[512,768]{1,0:T(8,128)(2,1)} %copy-done.4, ...), custom_call_target="tpu_custom_call" | custom-call | flops 1811939328 | bytes 3342336 | tf_op jit(solution)/shard_map/feed/pallas_call | solution.py:434
  79.3 1.5 collective-permute-start.15
  80.8 2.6 %collective-permute-done.17.refs_2_ = bf16[512,768]{1,0:T(8,128)(2,1)S(1)} collective-permute-done((bf16[512,768]{1,0:T(8,128)(2,1)S(1)}, bf16[512,768]{1,0:T(8,128)(2,1)S(1)}, u32[]{:S(2)}, u32[]{:S(2)}) %collective-permute-start.17) | collective-permute-done | bytes 786464 | tf_op jit(solution)/shard_map/ppermute | solution.py:778
  83.5 1.1 copy-done.5
  84.6 4.2 %norm_two_back.2 = (f32[512,768]{1,0:T(8,128)}, bf16[512,768]{1,0:T(8,128)(2,1)S(1)}, f32[8,768]{1,0:T(8,128)}) custom-call(s32[3]{0:T(128)S(1)} %pad_add_fusion.c_ref, f32[8,768]{1,0:T(8,128)} %get-tuple-element.120.refs_0_.refs_16_, bf16[512,768]{1,0:T(8,128)(2,1)S(1)} %copy-done.5, bf16[512,768]{1,0:T(8,128)(2,1)S(1)} %collective-permute-done.17.refs_2_, ...), custom_call_target="tpu_custom_call" | custom-call | flops 1966080 | bytes 1572864 | tf_op jit(solution)/shard_map/norm_two_back/pallas_call | solution.py:500
  89.0 1.0 collective-permute-start.19
  90.5 0.6 collective-permute-done.18.refs_2_
  91.0 14.5 %attend_back.2 = (bf16[576,1024]{1,0:T(8,128)(2,1)}, f32[192,768]{1,0:T(8,128)}) custom-call(s32[3]{0:T(128)S(1)} %pad_add_fusion.c_ref, bf16[512,768]{1,0:T(8,128)(2,1)} %copy-done.6, bf16[512,768]{1,0:T(8,128)(2,1)S(1)} %get-tuple-element.121.refs_1_, bf16[512,768]{1,0:T(8,128)(2,1)S(1)} %collective-permute-done.18.refs_2_, bf16[192,1024]{1,0:T(8,128)(2,1)} %copy-done.13, ...), custom_call_target="tpu_custom_call" | custom-call | flops 1308622848 | bytes 1671168 | tf_op jit(solution)/shard_map/attend_back/pallas_call | solution.py:596
  105.6 1.9 collective-permute-done.15
  107.5 1.5 collective-permute-done.19.refs_2_
  109.0 1.3 add_convert_fusion.refs_0_
  110.3 5.0 %all-to-all-start = ((bf16[4,192,768]{2,1,0:T(8,128)(2,1)}), bf16[4,192,768]{2,1,0:T(8,128)(2,1)S(1)}, u32[]{:S(2)}, u32[]{:S(2)}) async-start(bf16[4,192,768]{2,1,0:T(8,128)(2,1)} %add_convert_fusion.refs_0_), calls=%async_computation | async-start | bytes 2359296 | tf_op jit(solution)/shard_map/all_to_all | solution.py:894
  115.3 4.2 %norm_two_back.3 = (f32[512,768]{1,0:T(8,128)}, bf16[512,768]{1,0:T(8,128)(2,1)S(1)}, f32[8,768]{1,0:T(8,128)}) custom-call(s32[3]{0:T(128)S(1)} %pad_add_fusion.c_ref, bf16[4,192,768]{2,1,0:T(8,128)(2,1)} %add_convert_fusion.refs_0_, bf16[512,768]{1,0:T(8,128)(2,1)S(1)} %copy-done.7, bf16[512,768]{1,0:T(8,128)(2,1)S(1)} %collective-permute-done.19.refs_2_, ...), custom_call_target="tpu_custom_call" | custom-call | flops 1966080 | bytes 1572864 | tf_op jit(solution)/shard_map/norm_two_back/pallas_call | solution.py:500
  119.5 1.8 broadcast_select_fusion.refs_0_
  121.3 1.0 collective-permute-start.14
  122.3 16.1 %attend_back.3 = (bf16[576,1024]{1,0:T(8,128)(2,1)}, f32[192,768]{1,0:T(8,128)}) custom-call(s32[3]{0:T(128)S(1)} %pad_add_fusion.c_ref, bf16[512,768]{1,0:T(8,128)(2,1)} %copy-done.26, bf16[512,768]{1,0:T(8,128)(2,1)S(1)} %get-tuple-element.126.refs_1_, bf16[512,768]{1,0:T(8,128)(2,1)S(1)} %collective-permute-done.20.refs_2_, bf16[192,1024]{1,0:T(8,128)(2,1)} %copy-done.15, ...), custom_call_target="tpu_custom_call" | custom-call | flops 1308622848 | bytes 1671168 | tf_op jit(solution)/shard_map/attend_back/pallas_call | solution.py:596
  138.4 2.9 %collective-permute-done.14.refs_1_ = bf16[512,768]{1,0:T(8,128)(2,1)S(1)} collective-permute-done((bf16[512,768]{1,0:T(8,128)(2,1)S(1)}, bf16[512,768]{1,0:T(8,128)(2,1)S(1)}, u32[]{:S(2)}, u32[]{:S(2)}) %collective-permute-start.14) | collective-permute-done | bytes 786464 | tf_op jit(solution)/shard_map/ppermute | solution.py:778
  141.3 2.4 all-to-all-done.refs_2_
  143.7 1.7 sum_parts.2.refs_0_
  145.4 3.7 %all-to-all-start.1 = ((bf16[4,192,768]{2,1,0:T(8,128)(2,1)}), bf16[4,192,768]{2,1,0:T(8,128)(2,1)S(1)}, u32[]{:S(2)}, u32[]{:S(2)}) async-start(bf16[4,192,768]{2,1,0:T(8,128)(2,1)} %sum_parts.2.refs_0_), calls=%async_computation.1 | async-start | bytes 2359296 | tf_op jit(solution)/shard_map/all_to_all | solution.py:894
  149.1 13.5 %project_back.1 = (bf16[512,768]{1,0:T(8,128)(2,1)}, bf16[512,768]{1,0:T(8,128)(2,1)}, bf16[512,768]{1,0:T(8,128)(2,1)}, bf16[512,768]{1,0:T(8,128)(2,1)}, f32[8...) custom-call(s32[3]{0:T(128)S(1)} %pad_add_fusion.c_ref, ...), custom_call_target="tpu_custom_call" | custom-call | flops 905969664 | bytes 4718592 | tf_op jit(solution)/shard_map/project_back/pallas_call | solution.py:719
  162.6 1.6 collective-permute-start.27
  164.2 13.3 %all-to-all-done.1.refs_0_.mine_ref = bf16[4,192,768]{2,1,0:T(8,128)(2,1)S(1)} async-done(((bf16[4,192,768]{2,1,0:T(8,128)(2,1)}), bf16[4,192,768]{2,1,0:T(8,128)(2,1)S(1)}, u32[]{:S(2)}, u32[]{:S(2)}) %all-to-all-start.1) | async-done | bytes 1179680 | tf_op jit(solution)/shard_map/all_to_all | solution.py:894
  177.5 1.5 collective-permute-start.26
  179.0 2.6 %add_parts.1 = bf16[4,96,768]{2,1,0:T(8,128)(2,1)} custom-call(s32[3]{0:T(128)S(1)} %pad_add_fusion.c_ref, bf16[4,192,768]{2,1,0:T(8,128)(2,1)} %copy-done.1, bf16[4,96,768]{2,1,0:T(8,128)(2,1)} %get-tuple-element.141.refs_1_, bf16[4,96,768]{2,1,0:T(8,128)(2,1)S(1)} %collective-permute-done.27.refs_2_), custom_call_target="tpu_custom_call" | custom-call | flops 73728 | bytes 442368 | tf_op jit(solution)/shard_map/add_parts/pallas_call | solution.py:798
  181.6 4.2 %all-to-all-start.2 = ((bf16[4,96,768]{2,1,0:T(8,128)(2,1)}), bf16[4,96,768]{2,1,0:T(8,128)(2,1)S(1)}, u32[]{:S(2)}, u32[]{:S(2)}) async-start(bf16[4,96,768]{2,1,0:T(8,128)(2,1)} %add_parts.1), calls=%async_computation.2 | async-start | bytes 1179648 | tf_op jit(solution)/shard_map/all_to_all | solution.py:894
  185.8 1.2 collective-permute-done.23
  187.1 0.9 collective-permute-start.24
  188.0 2.9 %collective-permute-done.24 = f32[8,768]{1,0:T(8,128)S(1)} collective-permute-done((f32[8,768]{1,0:T(8,128)S(1)}, f32[8,768]{1,0:T(8,128)S(1)}, u32[]{:S(2)}, u32[]{:S(2)}) %collective-permute-start.24) | collective-permute-done | bytes 24608 | tf_op jit(solution)/shard_map/ppermute | solution.py:778
  191.0 9.2 %all-to-all-done.2.refs_1_ = bf16[4,96,768]{2,1,0:T(8,128)(2,1)S(1)} async-done(((bf16[4,96,768]{2,1,0:T(8,128)(2,1)}), bf16[4,96,768]{2,1,0:T(8,128)(2,1)S(1)}, u32[]{:S(2)}, u32[]{:S(2)}) %all-to-all-start.2) | async-done | bytes 589856 | tf_op jit(solution)/shard_map/all_to_all | solution.py:894
  200.2 4.2 %collective-permute-done.26.refs_0_.theirs_ref = bf16[4,192,768]{2,1,0:T(8,128)(2,1)S(1)} collective-permute-done((bf16[4,192,768]{2,1,0:T(8,128)(2,1)S(1)}, bf16[4,192,768]{2,1,0:T(8,128)(2,1)S(1)}, u32[]{:S(2)}, u32[]{:S(2)}) %collective-permute-start.26) | collective-permute-done | bytes 1179680 | tf_op jit(solution)/shard_map/ppermute | solution.py:890
  204.4 1.0 copy-done.11
  205.4 1.4 sum_parts.3
  206.9 3.9 %all-to-all-start.3 = ((bf16[4,112,768]{2,1,0:T(8,128)(2,1)}), bf16[4,112,768]{2,1,0:T(8,128)(2,1)S(1)}, u32[]{:S(2)}, u32[]{:S(2)}) async-start(bf16[4,112,768]{2,1,0:T(8,128)(2,1)} %sum_parts.3), calls=%async_computation.3 | async-start | bytes 1376256 | tf_op jit(solution)/shard_map/all_to_all | solution.py:894
  210.9 2.2 add_convert_fusion.1
  213.1 0.9 collective-permute-start.25
  214.0 13.1 %all-to-all-done.3.mine_ref = bf16[4,112,768]{2,1,0:T(8,128)(2,1)S(1)} async-done(((bf16[4,112,768]{2,1,0:T(8,128)(2,1)}), bf16[4,112,768]{2,1,0:T(8,128)(2,1)S(1)}, u32[]{:S(2)}, u32[]{:S(2)}) %all-to-all-start.3) | async-done | bytes 688160 | tf_op jit(solution)/shard_map/all_to_all | solution.py:894
  227.0 1.5 collective-permute-start.28
  228.6 4.1 %add_convert_fusion.3 = bf16[512,768]{1,0:T(8,128)(2,1)} fusion(bf16[512,768]{1,0:T(8,128)(2,1)} %copy-done.27, f32[512,768]{1,0:T(8,128)} %get-tuple-element.105.refs_3_, f32[512,768]{1,0:T(8,128)} %get-tuple-element.106.refs_3_, f32[768]{0:T(1024)S(1)} %copy-done.31, pred[]{:T(512)S(6)} %ge.3, bf16[512,768]{1,0:T(8,128)(2,1)} %collective-permute-done.12, ...), kind=kLoop, calls=%fused_computation.3 | loop fusion | flops 6291456 | bytes 7867393 | tf_op jit(solution)/shard_map/convert_element_type | solution.py:1015
  233.2 3.7 %norm_one_back.1 = bf16[512,768]{1,0:T(8,128)(2,1)} custom-call(s32[1]{0:T(128)} %bitcast.6.m_ref, bf16[512,768]{1,0:T(8,128)(2,1)S(1)} %copy-done.21, bf16[512,768]{1,0:T(8,128)(2,1)S(1)} %collective-permute-done.21.got_ref, bf16[512,768]{1,0:T(8,128)(2,1)S(1)} %collective-permute-done.25.theirs_ref, bf16[2048,768]{1,0:T(8,128)(2,1)} %x_ref.1, ...), custom_call_target="tpu_custom_call" | custom-call | flops 1966080 | bytes 1572864 | tf_op jit(solution)/shard_map/norm_one_back/pallas_call | solution.py:751
  236.9 3.0 %place_parts.3 = (f32[768,768]{1,0:T(8,128)}, f32[768,768]{1,0:T(8,128)}) custom-call(s32[3]{0:T(128)S(1)} %pad_add_fusion.c_ref, bf16[4,192,768]{2,1,0:T(8,128)(2,1)S(1)} %copy-done.2, bf16[4,192,768]{2,1,0:T(8,128)(2,1)S(1)} %copy-done.12), custom_call_target="tpu_custom_call" | custom-call | flops 294912 | bytes 1769472 | tf_op jit(solution)/shard_map/place_parts/pallas_call | solution.py:877
  239.9 3.5 %collective-permute-done.28.theirs_ref = bf16[4,112,768]{2,1,0:T(8,128)(2,1)S(1)} collective-permute-done((bf16[4,112,768]{2,1,0:T(8,128)(2,1)S(1)}, bf16[4,112,768]{2,1,0:T(8,128)(2,1)S(1)}, u32[]{:S(2)}, u32[]{:S(2)}) %collective-permute-start.28) | collective-permute-done | bytes 688160 | tf_op jit(solution)/shard_map/ppermute | solution.py:890
  243.4 2.0 place_parts.2
  245.4 0.7 slice_reduce_fusion
  (112 shorter events, 4.5 us)
Async XLA Ops:
  0.6 22.2 %collective-permute-start = (bf16[192,768]{1,0:T(8,128)(2,1)}, bf16[192,768]{1,0:T(8,128)(2,1)S(1)}, u32[]{:S(2)}, u32[]{:S(2)}) collective-permute-start(bf16[192,768]{1,0:T(8,128)(2,1)} %refs_11_.4), channel_id=1, source_target_pairs={{0,1},{1,0},{2,3},{3,2},{4,5},{5,4},{6,7},{7,6},{8,9},{9,8},{10,11... | collective-permute-start | bytes 884744 | tf_op jit(solution)/shard_map/ppermute | solution.py:774
  1.2 19.3 %collective-permute-start.4 = (bf16[192,768]{1,0:T(8,128)(2,1)}, bf16[192,768]{1,0:T(8,128)(2,1)S(1)}, u32[]{:S(2)}, u32[]{:S(2)}) collective-permute-start(bf16[192,768]{1,0:T(8,128)(2,1)} %refs_11_.4), channel_id=1, source_target_pairs={{0,2},{1,3},{2,0},{3,1},{4,6},{5,7},{6,4},{7,5},{8,10},{9,11},{10,... | collective-permute-start | bytes 884744 | tf_op jit(solution)/shard_map/ppermute | solution.py:778
  7.3 4.9 %copy-start.22 = (s32[2048]{0:T(1024)S(1)}, s32[2048]{0:T(1024)}, u32[]{:S(2)}) copy-start(s32[2048]{0:T(1024)} %param.18) | copy-start | bytes 24580
  12.2 8.0 %copy-start.13 = (bf16[192,1024]{1,0:T(8,128)(2,1)}, bf16[192,1024]{1,0:T(8,128)(2,1)S(1)}, u32[]{:S(2)}) copy-start(bf16[192,1024]{1,0:T(8,128)(2,1)S(1)} %get-tuple-element.85.refs_0_.refs_3_.refs_1_) | copy-start | bytes 1179652
  12.2 8.0 %copy-start.14 = (bf16[192,1024]{1,0:T(8,128)(2,1)}, bf16[192,1024]{1,0:T(8,128)(2,1)S(1)}, u32[]{:S(2)}) copy-start(bf16[192,1024]{1,0:T(8,128)(2,1)S(1)} %get-tuple-element.86.refs_1_.refs_4_.refs_2_) | copy-start | bytes 1179652
  12.2 8.0 %copy-start.20 = (bf16[192,1024]{1,0:T(8,128)(2,1)}, bf16[192,1024]{1,0:T(8,128)(2,1)S(1)}, u32[]{:S(2)}) copy-start(bf16[192,1024]{1,0:T(8,128)(2,1)S(1)} %get-tuple-element.87.refs_2_.refs_5_) | copy-start | bytes 1179652
  12.5 15.9 %copy-start = (s32[2048,128]{1,0:T(8,128)}, s32[2048,128]{1,0:T(8,128)S(1)}, u32[]{:S(2)}) copy-start(s32[2048,128]{1,0:T(8,128)S(1)} %broadcast_in_dim.12.refs_5_.refs_6_.refs_10_) | copy-start | bytes 3145732
  20.2 1.5 collective-permute-start.1
  20.4 16.9 %collective-permute-start.5 = (bf16[192,768]{1,0:T(8,128)(2,1)S(1)}, bf16[192,768]{1,0:T(8,128)(2,1)S(1)}, u32[]{:S(2)}, u32[]{:S(2)}) collective-permute-start(bf16[192,768]{1,0:T(8,128)(2,1)S(1)} %collective-permute-done.4.refs_8_), channel_id=1, source_target_pairs={{0,1},{1,0},{2,3},{3,2},{4,5},{5,4},{6,7},{7,6},{8,9},{9,8},{10,11... | collective-permute-start | bytes 884744 | tf_op jit(solution)/shard_map/ppermute | solution.py:774
  20.8 16.5 %collective-permute-start.2 = (bf16[192,512]{1,0:T(8,128)(2,1)S(1)}, bf16[192,512]{1,0:T(8,128)(2,1)S(1)}, u32[]{:S(2)}, u32[]{:S(2)}) collective-permute-start(bf16[192,512]{1,0:T(8,128)(2,1)S(1)} %get-tuple-element.94.refs_2_), channel_id=1, source_target_pairs={{0,2},{1,3},{2,0},{3,1},{4,6},{5,7},{6,4},{7,5},{8,10},{9,11},{10,... | collective-permute-start | bytes 589832 | tf_op jit(solution)/shard_map/ppermute | solution.py:778
  21.7 15.6 %collective-permute-start.3 = (bf16[192,512]{1,0:T(8,128)(2,1)S(1)}, bf16[192,512]{1,0:T(8,128)(2,1)S(1)}, u32[]{:S(2)}, u32[]{:S(2)}) collective-permute-start(bf16[192,512]{1,0:T(8,128)(2,1)S(1)} %collective-permute-done.1.refs_3_), channel_id=1, source_target_pairs={{0,2},{1,3},{2,0},{3,1},{4,6},{5,7},{6,4},{7,5},{8,10},{9,11},{10,... | collective-permute-start | bytes 589832 | tf_op jit(solution)/shard_map/ppermute | solution.py:778
  28.5 7.7 %copy-start.15 = (bf16[192,1024]{1,0:T(8,128)(2,1)}, bf16[192,1024]{1,0:T(8,128)(2,1)S(1)}, u32[]{:S(2)}) copy-start(bf16[192,1024]{1,0:T(8,128)(2,1)S(1)} %get-tuple-element.90.refs_1_.refs_3_.refs_5_) | copy-start | bytes 1179652
  28.5 7.7 %copy-start.16 = (bf16[192,1024]{1,0:T(8,128)(2,1)}, bf16[192,1024]{1,0:T(8,128)(2,1)S(1)}, u32[]{:S(2)}) copy-start(bf16[192,1024]{1,0:T(8,128)(2,1)S(1)} %get-tuple-element.91.refs_2_.refs_4_.refs_6_) | copy-start | bytes 1179652
  28.5 7.7 %copy-start.19 = (bf16[192,1024]{1,0:T(8,128)(2,1)}, bf16[192,1024]{1,0:T(8,128)(2,1)S(1)}, u32[]{:S(2)}) copy-start(bf16[192,1024]{1,0:T(8,128)(2,1)S(1)} %get-tuple-element.92.refs_3_.refs_5_) | copy-start | bytes 1179652
  28.5 8.8 %copy-start.32 = (f32[768]{0:T(1024)S(1)}, f32[768]{0:T(1024)}, u32[]{:S(2)}) copy-start(f32[768]{0:T(1024)} %param.26) | copy-start | bytes 9220
  28.5 8.8 %copy-start.33 = (f32[768]{0:T(1024)S(1)}, f32[768]{0:T(1024)}, u32[]{:S(2)}) copy-start(f32[768]{0:T(1024)} %param.27) | copy-start | bytes 9220
  28.5 8.8 %copy-start.34 = (f32[768]{0:T(1024)S(1)}, f32[768]{0:T(1024)}, u32[]{:S(2)}) copy-start(f32[768]{0:T(1024)} %param.28) | copy-start | bytes 9220
  28.5 8.8 %copy-start.8 = (bf16[192,768]{1,0:T(8,128)(2,1)S(1)}, bf16[192,768]{1,0:T(8,128)(2,1)}, u32[]{:S(2)}) copy-start(bf16[192,768]{1,0:T(8,128)(2,1)} %refs_11_.4) | copy-start | bytes 884740
  28.5 8.8 %copy-start.18 = (bf16[192,768]{1,0:T(8,128)(2,1)S(1)}, bf16[192,768]{1,0:T(8,128)(2,1)}, u32[]{:S(2)}) copy-start(bf16[192,768]{1,0:T(8,128)(2,1)} %copy-done.17) | copy-start | bytes 884740
  36.2 5.6 %collective-permute-start.6 = (bf16[192,512]{1,0:T(8,128)(2,1)S(1)}, bf16[192,512]{1,0:T(8,128)(2,1)S(1)}, u32[]{:S(2)}, u32[]{:S(2)}) collective-permute-start(bf16[192,512]{1,0:T(8,128)(2,1)S(1)} %get-tuple-element.97), channel_id=1, source_target_pairs={{0,1},{1,0},{2,3},{3,2},{4,5},{5,4},{6,7},{7,6},{8,9},{9,8},{10,11... | collective-permute-start | bytes 589832 | tf_op jit(solution)/shard_map/ppermute | solution.py:774
  36.3 7.3 %collective-permute-start.7 = (bf16[192,512]{1,0:T(8,128)(2,1)S(1)}, bf16[192,512]{1,0:T(8,128)(2,1)S(1)}, u32[]{:S(2)}, u32[]{:S(2)}) collective-permute-start(bf16[192,512]{1,0:T(8,128)(2,1)S(1)} %get-tuple-element.98.refs_2_), channel_id=1, source_target_pairs={{0,2},{1,3},{2,0},{3,1},{4,6},{5,7},{6,4},{7,5},{8,10},{9,11},{10,... | collective-permute-start | bytes 589832 | tf_op jit(solution)/shard_map/ppermute | solution.py:778
  37.3 7.2 %copy-start.35 = (f32[768]{0:T(1024)S(1)}, f32[768]{0:T(1024)}, u32[]{:S(2)}) copy-start(f32[768]{0:T(1024)} %param.30) | copy-start | bytes 9220
  37.4 8.7 %copy-start.9 = (bf16[768,768]{1,0:T(8,128)(2,1)S(1)}, bf16[768,768]{1,0:T(8,128)(2,1)}, u32[]{:S(2)}) copy-start(bf16[768,768]{1,0:T(8,128)(2,1)} %refs_4_.3) | copy-start | bytes 3538948
  37.4 8.7 %copy-start.10 = (bf16[768,768]{1,0:T(8,128)(2,1)S(1)}, bf16[768,768]{1,0:T(8,128)(2,1)}, u32[]{:S(2)}) copy-start(bf16[768,768]{1,0:T(8,128)(2,1)} %refs_6_.5) | copy-start | bytes 3538948
  43.6 2.5 %collective-permute-start.8 = (bf16[512,768]{1,0:T(8,128)(2,1)}, bf16[512,768]{1,0:T(8,128)(2,1)S(1)}, u32[]{:S(2)}, u32[]{:S(2)}) collective-permute-start(bf16[512,768]{1,0:T(8,128)(2,1)} %get-tuple-element.99.refs_0_), channel_id=1, source_target_pairs={{0,1},{1,0},{2,3},{3,2},{4,5},{5,4},{6,7},{7,6},{8,9},{9,8},{10,11... | collective-permute-start | bytes 2359304 | tf_op jit(solution)/shard_map/ppermute | solution.py:774
  43.6 15.2 %collective-permute-start.9 = (bf16[192,512]{1,0:T(8,128)(2,1)S(1)}, bf16[192,512]{1,0:T(8,128)(2,1)S(1)}, u32[]{:S(2)}, u32[]{:S(2)}) collective-permute-start(bf16[192,512]{1,0:T(8,128)(2,1)S(1)} %collective-permute-done.6.refs_3_), channel_id=1, source_target_pairs={{0,2},{1,3},{2,0},{3,1},{4,6},{5,7},{6,4},{7,5},{8,10},{9,11},{10,... | collective-permute-start | bytes 589832 | tf_op jit(solution)/shard_map/ppermute | solution.py:778
  58.8 4.8 %collective-permute-start.10 = (bf16[512,768]{1,0:T(8,128)(2,1)}, bf16[512,768]{1,0:T(8,128)(2,1)S(1)}, u32[]{:S(2)}, u32[]{:S(2)}) collective-permute-start(bf16[512,768]{1,0:T(8,128)(2,1)} %get-tuple-element.108), channel_id=1, source_target_pairs={{0,1},{1,0},{2,3},{3,2},{4,5},{5,4},{6,7},{7,6},{8,9},{9,8},{10,11... | collective-permute-start | bytes 2359304 | tf_op jit(solution)/shard_map/ppermute | solution.py:774
  63.2 2.5 %copy-start.23 = (f32[8,768]{1,0:T(8,128)S(1)}, f32[8,768]{1,0:T(8,128)}, u32[]{:S(2)}) copy-start(f32[8,768]{1,0:T(8,128)} %get-tuple-element.100.refs_0_.refs_7_) | copy-start | bytes 73732
  63.2 2.5 %collective-permute-start.11 = (bf16[512,768]{1,0:T(8,128)(2,1)}, bf16[512,768]{1,0:T(8,128)(2,1)S(1)}, u32[]{:S(2)}, u32[]{:S(2)}) collective-permute-start(bf16[512,768]{1,0:T(8,128)(2,1)} %get-tuple-element.109.refs_1_), channel_id=1, source_target_pairs={{0,1},{1,0},{2,3},{3,2},{4,5},{5,4},{6,7},{7,6},{8,9},{9,8},{10,11... | collective-permute-start | bytes 2359304 | tf_op jit(solution)/shard_map/ppermute | solution.py:774
  63.8 1.9 copy-start.4
  63.8 19.6 %collective-permute-start.17 = (bf16[512,768]{1,0:T(8,128)(2,1)S(1)}, bf16[512,768]{1,0:T(8,128)(2,1)S(1)}, u32[]{:S(2)}, u32[]{:S(2)}) collective-permute-start(bf16[512,768]{1,0:T(8,128)(2,1)S(1)} %add_convert_fusion.6.refs_0_.refs_1_), channel_id=1, source_target_pairs={{0,2},{1,3},{2,0},{3,1},{4,6},{5,7},{6,4},{7,5},{8,10},{9,11},{10,... | collective-permute-start | bytes 2359304 | tf_op jit(solution)/shard_map/ppermute | solution.py:778
  78.8 9.9 %collective-permute-start.16 = (bf16[512,768]{1,0:T(8,128)(2,1)}, bf16[512,768]{1,0:T(8,128)(2,1)S(1)}, u32[]{:S(2)}, u32[]{:S(2)}) collective-permute-start(bf16[512,768]{1,0:T(8,128)(2,1)} %get-tuple-element.119), channel_id=1, source_target_pairs={{0,1},{1,0},{2,3},{3,2},{4,5},{5,4},{6,7},{7,6},{8,9},{9,8},{10,11... | collective-permute-start | bytes 2359304 | tf_op jit(solution)/shard_map/ppermute | solution.py:774
  79.3 28.2 %collective-permute-start.15 = (bf16[4,192,768]{2,1,0:T(8,128)(2,1)}, bf16[4,192,768]{2,1,0:T(8,128)(2,1)S(1)}, u32[]{:S(2)}, u32[]{:S(2)}) collective-permute-start(bf16[4,192,768]{2,1,0:T(8,128)(2,1)} %get-tuple-element.117), channel_id=1, source_target_pairs={{0,4},{4,0},{8,12},{12,8},{16,20},{20,16},{24,28},{28,24},{1,5},{5... | collective-permute-start | bytes 3538952 | tf_op jit(solution)/shard_map/ppermute | solution.py:890
  88.8 2.3 collective-permute-start.18
  89.0 2.1 copy-start.6
  89.0 20.0 %collective-permute-start.19 = (bf16[512,768]{1,0:T(8,128)(2,1)S(1)}, bf16[512,768]{1,0:T(8,128)(2,1)S(1)}, u32[]{:S(2)}, u32[]{:S(2)}) collective-permute-start(bf16[512,768]{1,0:T(8,128)(2,1)S(1)} %add_convert_fusion.2.refs_0_.refs_1_), channel_id=1, source_target_pairs={{0,2},{1,3},{2,0},{3,1},{4,6},{5,7},{6,4},{7,5},{8,10},{9,11},{10,... | collective-permute-start | bytes 2359304 | tf_op jit(solution)/shard_map/ppermute | solution.py:778
  90.0 29.5 %collective-permute-start.13 = (bf16[512,768]{1,0:T(8,128)(2,1)}, bf16[512,768]{1,0:T(8,128)(2,1)}, u32[]{:S(2)}, u32[]{:S(2)}) collective-permute-start(bf16[512,768]{1,0:T(8,128)(2,1)} %get-tuple-element.115), channel_id=1, source_target_pairs={{0,1},{1,0},{2,3},{3,2},{4,5},{5,4},{6,7},{7,6},{8,9},{9,8},{10,11... | collective-permute-start | bytes 2359304 | tf_op jit(solution)/shard_map/ppermute | solution.py:774
  90.2 29.3 %collective-permute-start.12 = (bf16[512,768]{1,0:T(8,128)(2,1)}, bf16[512,768]{1,0:T(8,128)(2,1)}, u32[]{:S(2)}, u32[]{:S(2)}) collective-permute-start(bf16[512,768]{1,0:T(8,128)(2,1)} %get-tuple-element.113), channel_id=1, source_target_pairs={{0,1},{1,0},{2,3},{3,2},{4,5},{5,4},{6,7},{7,6},{8,9},{9,8},{10,11... | collective-permute-start | bytes 2359304 | tf_op jit(solution)/shard_map/ppermute | solution.py:774
  91.0 17.9 %copy-start.28 = (bf16[4,192,768]{2,1,0:T(8,128)(2,1)S(1)}, bf16[4,192,768]{2,1,0:T(8,128)(2,1)}, u32[]{:S(2)}) copy-start(bf16[4,192,768]{2,1,0:T(8,128)(2,1)} %get-tuple-element.116) | copy-start | bytes 3538948
  110.3 5.0 %copy-start.7 = (bf16[512,768]{1,0:T(8,128)(2,1)S(1)}, bf16[512,768]{1,0:T(8,128)(2,1)}, u32[]{:S(2)}) copy-start(bf16[512,768]{1,0:T(8,128)(2,1)} %copy-done.6) | copy-start | bytes 2359300
  110.3 33.4 %all-to-all-start = ((bf16[4,192,768]{2,1,0:T(8,128)(2,1)}), bf16[4,192,768]{2,1,0:T(8,128)(2,1)S(1)}, u32[]{:S(2)}, u32[]{:S(2)}) async-start(bf16[4,192,768]{2,1,0:T(8,128)(2,1)} %add_convert_fusion.refs_0_), calls=%async_computation | async-start | bytes 2359296 | tf_op jit(solution)/shard_map/all_to_all | solution.py:894
  115.3 4.2 %copy-start.24 = (bf16[512,768]{1,0:T(8,128)(2,1)S(1)}, bf16[512,768]{1,0:T(8,128)(2,1)}, u32[]{:S(2)}) copy-start(bf16[512,768]{1,0:T(8,128)(2,1)} %get-tuple-element.114) | copy-start | bytes 2359300
  115.3 4.2 %copy-start.25 = (bf16[512,768]{1,0:T(8,128)(2,1)S(1)}, bf16[512,768]{1,0:T(8,128)(2,1)}, u32[]{:S(2)}) copy-start(bf16[512,768]{1,0:T(8,128)(2,1)} %get-tuple-element.112) | copy-start | bytes 2359300
  119.5 2.8 %collective-permute-start.20 = (bf16[512,768]{1,0:T(8,128)(2,1)S(1)}, bf16[512,768]{1,0:T(8,128)(2,1)S(1)}, u32[]{:S(2)}, u32[]{:S(2)}) collective-permute-start(bf16[512,768]{1,0:T(8,128)(2,1)S(1)} %get-tuple-element.126.refs_1_), channel_id=1, source_target_pairs={{0,1},{1,0},{2,3},{3,2},{4,5},{5,4},{6,7},{7,6},{8,9},{9,8},{10,11... | collective-permute-start | bytes 2359304 | tf_op jit(solution)/shard_map/ppermute | solution.py:774
  121.3 20.0 %collective-permute-start.14 = (bf16[512,768]{1,0:T(8,128)(2,1)S(1)}, bf16[512,768]{1,0:T(8,128)(2,1)S(1)}, u32[]{:S(2)}, u32[]{:S(2)}) collective-permute-start(bf16[512,768]{1,0:T(8,128)(2,1)S(1)} %broadcast_select_fusion.refs_0_), channel_id=1, source_target_pairs={{0,2},{1,3},{2,0},{3,1},{4,6},{5,7},{6,4},{7,5},{8,10},{9,11},{10,... | collective-permute-start | bytes 2359304 | tf_op jit(solution)/shard_map/ppermute | solution.py:778
  141.3 2.4 copy-start.27
  145.4 3.7 %copy-start.3 = (bf16[768,3,192]{0,2,1:T(8,128)(2,1)S(1)}, bf16[768,3,192]{0,2,1:T(8,128)(2,1)}, u32[]{:S(2)}) copy-start(bf16[768,3,192]{0,2,1:T(8,128)(2,1)} %param.22) | copy-start | bytes 2654212
  145.4 32.1 %all-to-all-start.1 = ((bf16[4,192,768]{2,1,0:T(8,128)(2,1)}), bf16[4,192,768]{2,1,0:T(8,128)(2,1)S(1)}, u32[]{:S(2)}, u32[]{:S(2)}) async-start(bf16[4,192,768]{2,1,0:T(8,128)(2,1)} %sum_parts.2.refs_0_), calls=%async_computation.1 | async-start | bytes 2359296 | tf_op jit(solution)/shard_map/all_to_all | solution.py:894
  162.6 16.4 %collective-permute-start.27 = (bf16[4,96,768]{2,1,0:T(8,128)(2,1)}, bf16[4,96,768]{2,1,0:T(8,128)(2,1)S(1)}, u32[]{:S(2)}, u32[]{:S(2)}) collective-permute-start(bf16[4,96,768]{2,1,0:T(8,128)(2,1)} %get-tuple-element.142), channel_id=1, source_target_pairs={{0,4},{4,0},{8,12},{12,8},{16,20},{20,16},{24,28},{28,24},{1,5},{5... | collective-permute-start | bytes 1769480 | tf_op jit(solution)/shard_map/ppermute | solution.py:890
  177.5 26.9 %collective-permute-start.26 = (bf16[4,192,768]{2,1,0:T(8,128)(2,1)S(1)}, bf16[4,192,768]{2,1,0:T(8,128)(2,1)S(1)}, u32[]{:S(2)}, u32[]{:S(2)}) collective-permute-start(bf16[4,192,768]{2,1,0:T(8,128)(2,1)S(1)} %all-to-all-done.1.refs_0_.mine_ref), channel_id=1, source_target_pairs={{0,4},{4,0},{8,12},{12,8},{16,20},{20,16},{24,28},{28,24},{1,5},{5... | collective-permute-start | bytes 3538952 | tf_op jit(solution)/shard_map/ppermute | solution.py:890
  179.0 6.8 %copy-start.30 = (f32[8,768]{1,0:T(8,128)S(1)}, f32[8,768]{1,0:T(8,128)}, u32[]{:S(2)}) copy-start(f32[8,768]{1,0:T(8,128)} %get-tuple-element.137) | copy-start | bytes 73732
  181.6 18.6 %all-to-all-start.2 = ((bf16[4,96,768]{2,1,0:T(8,128)(2,1)}), bf16[4,96,768]{2,1,0:T(8,128)(2,1)S(1)}, u32[]{:S(2)}, u32[]{:S(2)}) async-start(bf16[4,96,768]{2,1,0:T(8,128)(2,1)} %add_parts.1), calls=%async_computation.2 | async-start | bytes 1179648 | tf_op jit(solution)/shard_map/all_to_all | solution.py:894
  185.8 1.2 collective-permute-start.23
  187.1 3.8 %collective-permute-start.24 = (f32[8,768]{1,0:T(8,128)S(1)}, f32[8,768]{1,0:T(8,128)S(1)}, u32[]{:S(2)}, u32[]{:S(2)}) collective-permute-start(f32[8,768]{1,0:T(8,128)S(1)} %select_add_fusion.1), channel_id=1, source_target_pairs={{0,2},{1,3},{2,0},{3,1},{4,6},{5,7},{6,4},{7,5},{8,10},{9,11},{10,... | collective-permute-start | bytes 73736 | tf_op jit(solution)/shard_map/ppermute | solution.py:778
  188.0 22.8 %collective-permute-start.22 = (bf16[512,768]{1,0:T(8,128)(2,1)}, bf16[512,768]{1,0:T(8,128)(2,1)}, u32[]{:S(2)}, u32[]{:S(2)}) collective-permute-start(bf16[512,768]{1,0:T(8,128)(2,1)} %get-tuple-element.136), channel_id=1, source_target_pairs={{0,1},{1,0},{2,3},{3,2},{4,5},{5,4},{6,7},{7,6},{8,9},{9,8},{10,11... | collective-permute-start | bytes 2359304 | tf_op jit(solution)/shard_map/ppermute | solution.py:774
  206.9 4.0 %copy-start.29 = (bf16[512,768]{1,0:T(8,128)(2,1)S(1)}, bf16[512,768]{1,0:T(8,128)(2,1)}, u32[]{:S(2)}) copy-start(bf16[512,768]{1,0:T(8,128)(2,1)} %get-tuple-element.135) | copy-start | bytes 2359300
  206.9 21.7 %copy-start.31 = (f32[768]{0:T(1024)S(1)}, f32[768]{0:T(1024)}, u32[]{:S(2)}) copy-start(f32[768]{0:T(1024)} %param.32) | copy-start | bytes 9220
  206.9 20.2 %all-to-all-start.3 = ((bf16[4,112,768]{2,1,0:T(8,128)(2,1)}), bf16[4,112,768]{2,1,0:T(8,128)(2,1)S(1)}, u32[]{:S(2)}, u32[]{:S(2)}) async-start(bf16[4,112,768]{2,1,0:T(8,128)(2,1)} %sum_parts.3), calls=%async_computation.3 | async-start | bytes 1376256 | tf_op jit(solution)/shard_map/all_to_all | solution.py:894
  210.8 21.9 %collective-permute-start.21 = (bf16[512,768]{1,0:T(8,128)(2,1)}, bf16[512,768]{1,0:T(8,128)(2,1)S(1)}, u32[]{:S(2)}, u32[]{:S(2)}) collective-permute-start(bf16[512,768]{1,0:T(8,128)(2,1)} %get-tuple-element.134), channel_id=1, source_target_pairs={{0,1},{1,0},{2,3},{3,2},{4,5},{5,4},{6,7},{7,6},{8,9},{9,8},{10,11... | collective-permute-start | bytes 2359304 | tf_op jit(solution)/shard_map/ppermute | solution.py:774
  213.1 20.1 %copy-start.21 = (bf16[512,768]{1,0:T(8,128)(2,1)S(1)}, bf16[512,768]{1,0:T(8,128)(2,1)}, u32[]{:S(2)}) copy-start(bf16[512,768]{1,0:T(8,128)(2,1)} %get-tuple-element.133.mine_ref) | copy-start | bytes 2359300
  213.1 20.1 %collective-permute-start.25 = (bf16[512,768]{1,0:T(8,128)(2,1)}, bf16[512,768]{1,0:T(8,128)(2,1)S(1)}, u32[]{:S(2)}, u32[]{:S(2)}) collective-permute-start(bf16[512,768]{1,0:T(8,128)(2,1)} %add_convert_fusion.1), channel_id=1, source_target_pairs={{0,2},{1,3},{2,0},{3,1},{4,6},{5,7},{6,4},{7,5},{8,10},{9,11},{10,... | collective-permute-start | bytes 2359304 | tf_op jit(solution)/shard_map/ppermute | solution.py:778
  227.0 16.4 %collective-permute-start.28 = (bf16[4,112,768]{2,1,0:T(8,128)(2,1)S(1)}, bf16[4,112,768]{2,1,0:T(8,128)(2,1)S(1)}, u32[]{:S(2)}, u32[]{:S(2)}) collective-permute-start(bf16[4,112,768]{2,1,0:T(8,128)(2,1)S(1)} %all-to-all-done.3.mine_ref), channel_id=1, source_target_pairs={{0,4},{4,0},{8,12},{12,8},{16,20},{20,16},{24,28},{28,24},{1,5},{5... | collective-permute-start | bytes 2064392 | tf_op jit(solution)/shard_map/ppermute | solution.py:890
  233.2 3.7 %copy-start.2 = (bf16[4,192,768]{2,1,0:T(8,128)(2,1)S(1)}, bf16[4,192,768]{2,1,0:T(8,128)(2,1)}, u32[]{:S(2)}) copy-start(bf16[4,192,768]{2,1,0:T(8,128)(2,1)} %copy-done.1) | copy-start | bytes 3538948
  233.2 3.7 %copy-start.12 = (bf16[4,192,768]{2,1,0:T(8,128)(2,1)S(1)}, bf16[4,192,768]{2,1,0:T(8,128)(2,1)}, u32[]{:S(2)}) copy-start(bf16[4,192,768]{2,1,0:T(8,128)(2,1)} %copy-done.11) | copy-start | bytes 3538948
  (5 other events, 5.4 us)

commit v5 on v4

--- a/solution.py
+++ b/solution.py
@@ -998,7 +998,7 @@
         grad_got = half_swap(grad_send)
         grad_got = quarter_trade(add_parts(core, grad_keep, grad_got, wait=[feed_all]))
         feed_other = half_swap(feed_all)
-        grad_sum = quarter_trade(sum_parts(core, grad_got, small, wait=[feed_other]))
+        grad_sum = quarter_trade(sum_parts(core, after(grad_got, feed_other), small))
         grad_other = half_swap(grad_sum)
     else:
         small, grad_send, grad_keep, feed_send, feed_keep = lax.psum(

time: 247 us -> 246 us (level)
  transfers between devices with their start and end apart: 33 -> 33, of which waited for: 18 -> 18; matrix products, arithmetic and copies ran while one was open for 5% -> 5% of each run, Pallas kernels for 51% -> 50%
where the time goes in v5:
time: 246 us; the launch traced here: 245 us
  Pallas kernels  127 us (52%)
  waiting for transfers between devices  66.1 us (27%)
  starting transfers between devices  36.1 us (15%)
  other arithmetic  10 us (4%)
  local copies, waits for them, and re-layouts  4.36 us (2%)
    all_to_all x4, waiting for transfers between devices, quarter_trade(): lax.all_to_all(parts, 'dp', 0, 0, axis_index_groups=[[0, 2, 4, 6], [1, 3,...  37.8 us
    pallas_call x2, Pallas kernels, attend_back(): pl.pallas_call(ignoring(len(wait), functools.partial(attend_back_kernel,...  29.2 us
    pallas_call x2, Pallas kernels, feed(): pl.pallas_call(ignoring(len(wait), functools.partial(feed_kernel, first,...  25.8 us
    all_to_all x4, starting transfers between devices, quarter_trade(): lax.all_to_all(parts, 'dp', 0, 0, axis_index_groups=[[0, 2, 4, 6], [1, 3,...  16.7 us
    pallas_call x2, Pallas kernels, attend(): pl.pallas_call(ignoring(len(wait), attend_kernel), grid_spec=pltpu.Prefet...  15.3 us
    ppermute x10, waiting for transfers between devices, chip_swap(): return lax.ppermute(value, 'mp', CHIP_SWAP)  14.3 us
    pallas_call x1, Pallas kernels, project_back(): pl.pallas_call(ignoring(len(wait), project_back_kernel), grid_spec=pltpu....  13.5 us
    ppermute x10, starting transfers between devices, chip_swap(): return lax.ppermute(value, 'mp', CHIP_SWAP)  10.5 us
  transfers between devices with their start and end apart: 33, of which 18 were waited for; matrix products, arithmetic and copies ran while one was open for 5% of the time, Pallas kernels for 50%

profile of v5, /device:TPU:0, one launch (start us, length us, event | category | flops | bytes accessed | tf_op | source)
XLA Modules:
  0.0 245.1 jit_solution(8622145968885080785)
XLA Ops:
  1.2 2.6 %collective-permute-start.4 = (bf16[192,768]{1,0:T(8,128)(2,1)}, bf16[192,768]{1,0:T(8,128)(2,1)S(1)}, u32[]{:S(2)}, u32[]{:S(2)}) collective-permute-start(bf16[192,768]{1,0:T(8,128)(2,1)} %refs_11_.4), channel_id=1, source_target_pairs={{0,2},{1,3},{2,0},{3,1},{4,6},{5,7},{6,4},{7,5},{8,10},{9,11},{10,... | collective-permute-start | bytes 884744 | tf_op jit(solution)/shard_map/ppermute | solution.py:778
  3.8 0.7 reshape.64.refs_5_.refs_7_.refs_12_.gain_ref
  4.5 0.7 reshape.65.refs_6_.refs_8_.refs_13_
  5.2 2.1 prepare.1
  7.3 4.9 %project.2 = (bf16[1024,768]{1,0:T(8,128)(2,1)}, bf16[192,1024]{1,0:T(8,128)(2,1)S(1)}, bf16[192,1024]{1,0:T(8,128)(2,1)S(1)}, bf16[192,1024]{1,0:T(8,128)(2,1)S(1)}) custom-call(s32[3]{0:T(128)S(1)} %pad_add_fusion.c_ref, bf16[2048,768]{1,0:T(8,128)(2,1)} %x_ref.1, s32[2,2048]{1,0:T(2,128)} %refs_11_.5, ...), custom_call_target="tpu_custom_call" | custom-call | flops 226492416 | bytes 1302528 | tf_op jit(solution)/shard_map/project/pallas_call | solution.py:152
  12.6 7.6 %attend.2 = (bf16[192,512]{1,0:T(8,128)(2,1)S(1)}, bf16[192,512]{1,0:T(8,128)(2,1)S(1)}, f32[192,1024]{1,0:T(8,128)}, f32[8,1024]{1,0:T(8,128)}) custom-call(s32[3]{0:T(128)S(1)} %pad_add_fusion.c_ref, bf16[192,1024]{1,0:T(8,128)(2,1)S(1)} %get-tuple-element.86.refs_0_.refs_3_.refs_1_, bf16[192,1024]{1,0:T(8,128)(2,1)S(1)} %get-tuple-element.87.refs_1_.refs_4_.refs_2_, ...), custom_call_target="tpu_custom_call" | custom-call | flops 402653184 | bytes 589824 | tf_op jit(solution)/shard_map/attend/pallas_call | solution.py:257
  20.9 0.9 collective-permute-done.1.refs_3_
  21.7 1.1 collective-permute-start.3
  22.8 0.7 copy-done.15
  23.5 4.9 %project.3 = (bf16[1024,768]{1,0:T(8,128)(2,1)}, bf16[192,1024]{1,0:T(8,128)(2,1)S(1)}, bf16[192,1024]{1,0:T(8,128)(2,1)S(1)}, bf16[192,1024]{1,0:T(8,128)(2,1)S(1)}) custom-call(s32[3]{0:T(128)S(1)} %pad_add_fusion.c_ref, f32[8,1024]{1,0:T(8,128)} %get-tuple-element.89.refs_0_.refs_7_, bf16[192,768]{1,0:T(8,128)(2,1)} %copy-done.15, ...), custom_call_target="tpu_custom_call" | custom-call | flops 226492416 | bytes 1302528 | tf_op jit(solution)/shard_map/project/pallas_call | solution.py:152
  28.5 7.6 %attend.3 = (bf16[192,512]{1,0:T(8,128)(2,1)S(1)}, bf16[192,512]{1,0:T(8,128)(2,1)S(1)}, f32[192,1024]{1,0:T(8,128)}, f32[8,1024]{1,0:T(8,128)}) custom-call(s32[3]{0:T(128)S(1)} %pad_add_fusion.c_ref, bf16[1024,768]{1,0:T(8,128)(2,1)} %get-tuple-element.90.refs_0_.refs_8_, bf16[192,1024]{1,0:T(8,128)(2,1)S(1)} %get-tuple-element.91.refs_1_.refs_3_.refs_5_, ...), custom_call_target="tpu_custom_call" | custom-call | flops 402653184 | bytes 589824 | tf_op jit(solution)/shard_map/attend/pallas_call | solution.py:257
  36.3 1.0 collective-permute-start.7
  37.4 4.4 %norm_two.2 = (f32[512,768]{1,0:T(8,128)}, bf16[512,768]{1,0:T(8,128)(2,1)}) custom-call(s32[3]{0:T(128)S(1)} %pad_add_fusion.c_ref, f32[8,1024]{1,0:T(8,128)} %get-tuple-element.94.refs_0_.refs_7_, bf16[2048,768]{1,0:T(8,128)(2,1)} %x_ref.1, bf16[192,512]{1,0:T(8,128)(2,1)S(1)} %get-tuple-element.95.refs_2_, ...), custom_call_target="tpu_custom_call" | custom-call | flops 150994944 | bytes 1179648 | tf_op jit(solution)/shard_map/norm_two/pallas_call | solution.py:314
  41.8 1.8 collective-permute-done.7.refs_4_
  43.6 0.9 collective-permute-start.9
  44.5 1.6 collective-permute-done.8.refs_1_
  46.1 12.7 %feed.2 = (bf16[512,768]{1,0:T(8,128)(2,1)}, bf16[512,768]{1,0:T(8,128)(2,1)}, bf16[512,768]{1,0:T(8,128)(2,1)}, bf16[512,768]{1,0:T(8,128)(2,1)S(1)}, f32[8,768...) custom-call(s32[3]{0:T(128)S(1)} %pad_add_fusion.c_ref, bf16[512,768]{1,0:T(8,128)(2,1)} %get-tuple-element.100.refs_0_, ...), custom_call_target="tpu_custom_call" | custom-call | flops 1811939328 | bytes 3342336 | tf_op jit(solution)/shard_map/feed/pallas_call | solution.py:434
  58.9 4.2 %norm_two.3 = (f32[512,768]{1,0:T(8,128)}, bf16[512,768]{1,0:T(8,128)(2,1)}) custom-call(s32[3]{0:T(128)S(1)} %pad_add_fusion.c_ref, f32[8,768]{1,0:T(8,128)} %get-tuple-element.101.refs_0_.refs_7_, bf16[2048,768]{1,0:T(8,128)(2,1)} %x_ref.1, bf16[192,512]{1,0:T(8,128)(2,1)S(1)} %get-tuple-element.99.refs_2_, ...), custom_call_target="tpu_custom_call" | custom-call | flops 150994944 | bytes 1179648 | tf_op jit(solution)/shard_map/norm_two/pallas_call | solution.py:314
  63.8 1.0 collective-permute-start.17
  64.8 0.9 collective-permute-done.11.refs_2_
  65.7 13.1 %feed.3 = (bf16[512,768]{1,0:T(8,128)(2,1)}, bf16[512,768]{1,0:T(8,128)(2,1)}, bf16[512,768]{1,0:T(8,128)(2,1)}, bf16[512,768]{1,0:T(8,128)(2,1)S(1)}, f32[8,768...) custom-call(s32[3]{0:T(128)S(1)} %pad_add_fusion.c_ref, bf16[512,768]{1,0:T(8,128)(2,1)} %copy-done.4, ...), custom_call_target="tpu_custom_call" | custom-call | flops 1811939328 | bytes 3342336 | tf_op jit(solution)/shard_map/feed/pallas_call | solution.py:434
  79.3 1.5 collective-permute-start.15
  80.8 2.7 %collective-permute-done.17.refs_2_ = bf16[512,768]{1,0:T(8,128)(2,1)S(1)} collective-permute-done((bf16[512,768]{1,0:T(8,128)(2,1)S(1)}, bf16[512,768]{1,0:T(8,128)(2,1)S(1)}, u32[]{:S(2)}, u32[]{:S(2)}) %collective-permute-start.17) | collective-permute-done | bytes 786464 | tf_op jit(solution)/shard_map/ppermute | solution.py:778
  83.5 1.1 copy-done.5
  84.6 4.2 %norm_two_back.2 = (f32[512,768]{1,0:T(8,128)}, bf16[512,768]{1,0:T(8,128)(2,1)S(1)}, f32[8,768]{1,0:T(8,128)}) custom-call(s32[3]{0:T(128)S(1)} %pad_add_fusion.c_ref, f32[8,768]{1,0:T(8,128)} %get-tuple-element.121.refs_0_.refs_16_, bf16[512,768]{1,0:T(8,128)(2,1)S(1)} %copy-done.5, bf16[512,768]{1,0:T(8,128)(2,1)S(1)} %collective-permute-done.17.refs_2_, ...), custom_call_target="tpu_custom_call" | custom-call | flops 1966080 | bytes 1572864 | tf_op jit(solution)/shard_map/norm_two_back/pallas_call | solution.py:500
  89.0 1.0 collective-permute-start.19
  90.5 0.6 collective-permute-done.18.refs_2_
  91.0 14.5 %attend_back.2 = (bf16[576,1024]{1,0:T(8,128)(2,1)}, f32[192,768]{1,0:T(8,128)}) custom-call(s32[3]{0:T(128)S(1)} %pad_add_fusion.c_ref, bf16[512,768]{1,0:T(8,128)(2,1)} %copy-done.6, bf16[512,768]{1,0:T(8,128)(2,1)S(1)} %get-tuple-element.122.refs_1_, bf16[512,768]{1,0:T(8,128)(2,1)S(1)} %collective-permute-done.18.refs_2_, bf16[192,1024]{1,0:T(8,128)(2,1)} %copy-done.11, ...), custom_call_target="tpu_custom_call" | custom-call | flops 1308622848 | bytes 1671168 | tf_op jit(solution)/shard_map/attend_back/pallas_call | solution.py:596
  105.6 1.9 collective-permute-done.15
  107.5 1.5 collective-permute-done.19.refs_2_
  109.0 1.3 add_convert_fusion.refs_0_
  110.3 5.0 %all-to-all-start = ((bf16[4,192,768]{2,1,0:T(8,128)(2,1)}), bf16[4,192,768]{2,1,0:T(8,128)(2,1)S(1)}, u32[]{:S(2)}, u32[]{:S(2)}) async-start(bf16[4,192,768]{2,1,0:T(8,128)(2,1)} %add_convert_fusion.refs_0_), calls=%async_computation | async-start | bytes 2359296 | tf_op jit(solution)/shard_map/all_to_all | solution.py:894
  115.3 4.1 %norm_two_back.3 = (f32[512,768]{1,0:T(8,128)}, bf16[512,768]{1,0:T(8,128)(2,1)S(1)}, f32[8,768]{1,0:T(8,128)}) custom-call(s32[3]{0:T(128)S(1)} %pad_add_fusion.c_ref, bf16[4,192,768]{2,1,0:T(8,128)(2,1)} %add_convert_fusion.refs_0_, bf16[512,768]{1,0:T(8,128)(2,1)S(1)} %copy-done.7, bf16[512,768]{1,0:T(8,128)(2,1)S(1)} %collective-permute-done.19.refs_2_, ...), custom_call_target="tpu_custom_call" | custom-call | flops 1966080 | bytes 1572864 | tf_op jit(solution)/shard_map/norm_two_back/pallas_call | solution.py:500
  119.5 1.8 broadcast_select_fusion.refs_0_
  121.3 1.0 collective-permute-start.14
  122.3 14.7 %attend_back.3 = (bf16[576,1024]{1,0:T(8,128)(2,1)}, f32[192,768]{1,0:T(8,128)}) custom-call(s32[3]{0:T(128)S(1)} %pad_add_fusion.c_ref, bf16[512,768]{1,0:T(8,128)(2,1)} %copy-done.25, bf16[512,768]{1,0:T(8,128)(2,1)S(1)} %get-tuple-element.127.refs_1_, bf16[512,768]{1,0:T(8,128)(2,1)S(1)} %collective-permute-done.20.refs_2_, bf16[192,1024]{1,0:T(8,128)(2,1)} %copy-done.13, ...), custom_call_target="tpu_custom_call" | custom-call | flops 1308622848 | bytes 1671168 | tf_op jit(solution)/shard_map/attend_back/pallas_call | solution.py:596
  136.9 4.3 %collective-permute-done.14.refs_1_ = bf16[512,768]{1,0:T(8,128)(2,1)S(1)} collective-permute-done((bf16[512,768]{1,0:T(8,128)(2,1)S(1)}, bf16[512,768]{1,0:T(8,128)(2,1)S(1)}, u32[]{:S(2)}, u32[]{:S(2)}) %collective-permute-start.14) | collective-permute-done | bytes 786464 | tf_op jit(solution)/shard_map/ppermute | solution.py:778
  141.3 2.4 all-to-all-done.refs_2_
  143.7 1.7 sum_parts.2.refs_0_
  145.4 3.7 %all-to-all-start.1 = ((bf16[4,192,768]{2,1,0:T(8,128)(2,1)}), bf16[4,192,768]{2,1,0:T(8,128)(2,1)S(1)}, u32[]{:S(2)}, u32[]{:S(2)}) async-start(bf16[4,192,768]{2,1,0:T(8,128)(2,1)} %sum_parts.2.refs_0_), calls=%async_computation.1 | async-start | bytes 2359296 | tf_op jit(solution)/shard_map/all_to_all | solution.py:894
  149.1 13.5 %project_back.1 = (bf16[512,768]{1,0:T(8,128)(2,1)}, bf16[512,768]{1,0:T(8,128)(2,1)}, bf16[512,768]{1,0:T(8,128)(2,1)}, bf16[512,768]{1,0:T(8,128)(2,1)}, f32[8...) custom-call(s32[3]{0:T(128)S(1)} %pad_add_fusion.c_ref, ...), custom_call_target="tpu_custom_call" | custom-call | flops 905969664 | bytes 4718592 | tf_op jit(solution)/shard_map/project_back/pallas_call | solution.py:719
  162.6 1.6 collective-permute-start.26
  164.2 13.3 %all-to-all-done.1.refs_0_.mine_ref = bf16[4,192,768]{2,1,0:T(8,128)(2,1)S(1)} async-done(((bf16[4,192,768]{2,1,0:T(8,128)(2,1)}), bf16[4,192,768]{2,1,0:T(8,128)(2,1)S(1)}, u32[]{:S(2)}, u32[]{:S(2)}) %all-to-all-start.1) | async-done | bytes 1179680 | tf_op jit(solution)/shard_map/all_to_all | solution.py:894
  177.5 1.5 collective-permute-start.27
  179.0 2.6 %add_parts.1 = bf16[4,96,768]{2,1,0:T(8,128)(2,1)} custom-call(s32[3]{0:T(128)S(1)} %pad_add_fusion.c_ref, bf16[4,192,768]{2,1,0:T(8,128)(2,1)} %copy-done.1, bf16[4,96,768]{2,1,0:T(8,128)(2,1)} %get-tuple-element.142.refs_1_, bf16[4,96,768]{2,1,0:T(8,128)(2,1)S(1)} %collective-permute-done.26.refs_2_), custom_call_target="tpu_custom_call" | custom-call | flops 73728 | bytes 442368 | tf_op jit(solution)/shard_map/add_parts/pallas_call | solution.py:798
  181.6 4.2 %all-to-all-start.2 = ((bf16[4,96,768]{2,1,0:T(8,128)(2,1)}), bf16[4,96,768]{2,1,0:T(8,128)(2,1)S(1)}, u32[]{:S(2)}, u32[]{:S(2)}) async-start(bf16[4,96,768]{2,1,0:T(8,128)(2,1)} %add_parts.1), calls=%async_computation.2 | async-start | bytes 1179648 | tf_op jit(solution)/shard_map/all_to_all | solution.py:894
  185.8 1.2 collective-permute-done.23
  187.1 0.9 collective-permute-start.24
  188.0 2.9 %collective-permute-done.24 = f32[8,768]{1,0:T(8,128)S(1)} collective-permute-done((f32[8,768]{1,0:T(8,128)S(1)}, f32[8,768]{1,0:T(8,128)S(1)}, u32[]{:S(2)}, u32[]{:S(2)}) %collective-permute-start.24) | collective-permute-done | bytes 24608 | tf_op jit(solution)/shard_map/ppermute | solution.py:778
  191.0 9.2 %all-to-all-done.2.refs_0_ = bf16[4,96,768]{2,1,0:T(8,128)(2,1)S(1)} async-done(((bf16[4,96,768]{2,1,0:T(8,128)(2,1)}), bf16[4,96,768]{2,1,0:T(8,128)(2,1)S(1)}, u32[]{:S(2)}, u32[]{:S(2)}) %all-to-all-start.2) | async-done | bytes 589856 | tf_op jit(solution)/shard_map/all_to_all | solution.py:894
  200.2 4.2 %collective-permute-done.27.theirs_ref = bf16[4,192,768]{2,1,0:T(8,128)(2,1)S(1)} collective-permute-done((bf16[4,192,768]{2,1,0:T(8,128)(2,1)S(1)}, bf16[4,192,768]{2,1,0:T(8,128)(2,1)S(1)}, u32[]{:S(2)}, u32[]{:S(2)}) %collective-permute-start.27) | collective-permute-done | bytes 1179680 | tf_op jit(solution)/shard_map/ppermute | solution.py:890
  204.4 1.5 sum_parts.3
  205.9 3.9 %all-to-all-start.3 = ((bf16[4,112,768]{2,1,0:T(8,128)(2,1)}), bf16[4,112,768]{2,1,0:T(8,128)(2,1)S(1)}, u32[]{:S(2)}, u32[]{:S(2)}) async-start(bf16[4,112,768]{2,1,0:T(8,128)(2,1)} %sum_parts.3), calls=%async_computation.3 | async-start | bytes 1376256 | tf_op jit(solution)/shard_map/all_to_all | solution.py:894
  209.8 2.4 add_convert_fusion.1
  212.3 0.9 collective-permute-start.25
  213.2 12.8 %all-to-all-done.3.mine_ref = bf16[4,112,768]{2,1,0:T(8,128)(2,1)S(1)} async-done(((bf16[4,112,768]{2,1,0:T(8,128)(2,1)}), bf16[4,112,768]{2,1,0:T(8,128)(2,1)S(1)}, u32[]{:S(2)}, u32[]{:S(2)}) %all-to-all-start.3) | async-done | bytes 688160 | tf_op jit(solution)/shard_map/all_to_all | solution.py:894
  226.0 1.5 collective-permute-start.28
  227.6 3.9 %add_convert_fusion.3 = bf16[512,768]{1,0:T(8,128)(2,1)} fusion(bf16[512,768]{1,0:T(8,128)(2,1)} %copy-done.26, f32[512,768]{1,0:T(8,128)} %get-tuple-element.106.refs_3_, f32[512,768]{1,0:T(8,128)} %get-tuple-element.107.refs_3_, f32[768]{0:T(1024)S(1)} %copy-done.29, pred[]{:T(512)S(6)} %ge.3, bf16[512,768]{1,0:T(8,128)(2,1)} %collective-permute-done.12, ...), kind=kLoop, calls=%fused_computation.3 | loop fusion | flops 6291456 | bytes 7867393 | tf_op jit(solution)/shard_map/convert_element_type | solution.py:1015
  231.4 1.1 collective-permute-done.25.theirs_ref
  232.5 4.0 %norm_one_back.1 = bf16[512,768]{1,0:T(8,128)(2,1)} custom-call(s32[1]{0:T(128)} %bitcast.6.m_ref, bf16[512,768]{1,0:T(8,128)(2,1)S(1)} %copy-done.19, bf16[512,768]{1,0:T(8,128)(2,1)} %collective-permute-done.21.got_ref, bf16[512,768]{1,0:T(8,128)(2,1)} %collective-permute-done.25.theirs_ref, bf16[2048,768]{1,0:T(8,128)(2,1)} %x_ref.1, ...), custom_call_target="tpu_custom_call" | custom-call | flops 1966080 | bytes 1572864 | tf_op jit(solution)/shard_map/norm_one_back/pallas_call | solution.py:751
  236.6 3.0 %place_parts.3 = (f32[768,768]{1,0:T(8,128)}, f32[768,768]{1,0:T(8,128)}) custom-call(s32[3]{0:T(128)S(1)} %pad_add_fusion.c_ref, bf16[4,192,768]{2,1,0:T(8,128)(2,1)S(1)} %copy-done.2, bf16[4,192,768]{2,1,0:T(8,128)(2,1)S(1)} %collective-permute-done.27.theirs_ref), custom_call_target="tpu_custom_call" | custom-call | flops 294912 | bytes 1769472 | tf_op jit(solution)/shard_map/place_parts/pallas_call | solution.py:877
  239.6 2.8 %collective-permute-done.28.theirs_ref = bf16[4,112,768]{2,1,0:T(8,128)(2,1)S(1)} collective-permute-done((bf16[4,112,768]{2,1,0:T(8,128)(2,1)S(1)}, bf16[4,112,768]{2,1,0:T(8,128)(2,1)S(1)}, u32[]{:S(2)}, u32[]{:S(2)}) %collective-permute-start.28) | collective-permute-done | bytes 688160 | tf_op jit(solution)/shard_map/ppermute | solution.py:890
  242.4 2.0 place_parts.2
  244.4 0.7 slice_reduce_fusion
  (108 shorter events, 4.0 us)
Async XLA Ops:
  0.6 22.2 %collective-permute-start = (bf16[192,768]{1,0:T(8,128)(2,1)}, bf16[192,768]{1,0:T(8,128)(2,1)S(1)}, u32[]{:S(2)}, u32[]{:S(2)}) collective-permute-start(bf16[192,768]{1,0:T(8,128)(2,1)} %refs_11_.4), channel_id=1, source_target_pairs={{0,1},{1,0},{2,3},{3,2},{4,5},{5,4},{6,7},{7,6},{8,9},{9,8},{10,11... | collective-permute-start | bytes 884744 | tf_op jit(solution)/shard_map/ppermute | solution.py:774
  1.2 19.3 %collective-permute-start.4 = (bf16[192,768]{1,0:T(8,128)(2,1)}, bf16[192,768]{1,0:T(8,128)(2,1)S(1)}, u32[]{:S(2)}, u32[]{:S(2)}) collective-permute-start(bf16[192,768]{1,0:T(8,128)(2,1)} %refs_11_.4), channel_id=1, source_target_pairs={{0,2},{1,3},{2,0},{3,1},{4,6},{5,7},{6,4},{7,5},{8,10},{9,11},{10,... | collective-permute-start | bytes 884744 | tf_op jit(solution)/shard_map/ppermute | solution.py:778
  7.3 4.9 %copy-start.20 = (s32[2048]{0:T(1024)S(1)}, s32[2048]{0:T(1024)}, u32[]{:S(2)}) copy-start(s32[2048]{0:T(1024)} %param.18) | copy-start | bytes 24580
  12.2 8.0 %copy-start.11 = (bf16[192,1024]{1,0:T(8,128)(2,1)}, bf16[192,1024]{1,0:T(8,128)(2,1)S(1)}, u32[]{:S(2)}) copy-start(bf16[192,1024]{1,0:T(8,128)(2,1)S(1)} %get-tuple-element.86.refs_0_.refs_3_.refs_1_) | copy-start | bytes 1179652
  12.2 8.0 %copy-start.12 = (bf16[192,1024]{1,0:T(8,128)(2,1)}, bf16[192,1024]{1,0:T(8,128)(2,1)S(1)}, u32[]{:S(2)}) copy-start(bf16[192,1024]{1,0:T(8,128)(2,1)S(1)} %get-tuple-element.87.refs_1_.refs_4_.refs_2_) | copy-start | bytes 1179652
  12.2 8.0 %copy-start.18 = (bf16[192,1024]{1,0:T(8,128)(2,1)}, bf16[192,1024]{1,0:T(8,128)(2,1)S(1)}, u32[]{:S(2)}) copy-start(bf16[192,1024]{1,0:T(8,128)(2,1)S(1)} %get-tuple-element.88.refs_2_.refs_5_) | copy-start | bytes 1179652
  12.5 15.9 %copy-start = (s32[2048,128]{1,0:T(8,128)}, s32[2048,128]{1,0:T(8,128)S(1)}, u32[]{:S(2)}) copy-start(s32[2048,128]{1,0:T(8,128)S(1)} %broadcast_in_dim.12.refs_5_.refs_6_.refs_10_) | copy-start | bytes 3145732
  20.2 1.5 collective-permute-start.1
  20.4 16.9 %collective-permute-start.5 = (bf16[192,768]{1,0:T(8,128)(2,1)S(1)}, bf16[192,768]{1,0:T(8,128)(2,1)S(1)}, u32[]{:S(2)}, u32[]{:S(2)}) collective-permute-start(bf16[192,768]{1,0:T(8,128)(2,1)S(1)} %collective-permute-done.4.refs_8_), channel_id=1, source_target_pairs={{0,1},{1,0},{2,3},{3,2},{4,5},{5,4},{6,7},{7,6},{8,9},{9,8},{10,11... | collective-permute-start | bytes 884744 | tf_op jit(solution)/shard_map/ppermute | solution.py:774
  20.8 16.5 %collective-permute-start.2 = (bf16[192,512]{1,0:T(8,128)(2,1)S(1)}, bf16[192,512]{1,0:T(8,128)(2,1)S(1)}, u32[]{:S(2)}, u32[]{:S(2)}) collective-permute-start(bf16[192,512]{1,0:T(8,128)(2,1)S(1)} %get-tuple-element.95.refs_2_), channel_id=1, source_target_pairs={{0,2},{1,3},{2,0},{3,1},{4,6},{5,7},{6,4},{7,5},{8,10},{9,11},{10,... | collective-permute-start | bytes 589832 | tf_op jit(solution)/shard_map/ppermute | solution.py:778
  21.7 15.6 %collective-permute-start.3 = (bf16[192,512]{1,0:T(8,128)(2,1)S(1)}, bf16[192,512]{1,0:T(8,128)(2,1)S(1)}, u32[]{:S(2)}, u32[]{:S(2)}) collective-permute-start(bf16[192,512]{1,0:T(8,128)(2,1)S(1)} %collective-permute-done.1.refs_3_), channel_id=1, source_target_pairs={{0,2},{1,3},{2,0},{3,1},{4,6},{5,7},{6,4},{7,5},{8,10},{9,11},{10,... | collective-permute-start | bytes 589832 | tf_op jit(solution)/shard_map/ppermute | solution.py:778
  28.5 7.7 %copy-start.13 = (bf16[192,1024]{1,0:T(8,128)(2,1)}, bf16[192,1024]{1,0:T(8,128)(2,1)S(1)}, u32[]{:S(2)}) copy-start(bf16[192,1024]{1,0:T(8,128)(2,1)S(1)} %get-tuple-element.91.refs_1_.refs_3_.refs_5_) | copy-start | bytes 1179652
  28.5 7.7 %copy-start.14 = (bf16[192,1024]{1,0:T(8,128)(2,1)}, bf16[192,1024]{1,0:T(8,128)(2,1)S(1)}, u32[]{:S(2)}) copy-start(bf16[192,1024]{1,0:T(8,128)(2,1)S(1)} %get-tuple-element.92.refs_2_.refs_4_.refs_6_) | copy-start | bytes 1179652
  28.5 7.7 %copy-start.17 = (bf16[192,1024]{1,0:T(8,128)(2,1)}, bf16[192,1024]{1,0:T(8,128)(2,1)S(1)}, u32[]{:S(2)}) copy-start(bf16[192,1024]{1,0:T(8,128)(2,1)S(1)} %get-tuple-element.93.refs_3_.refs_5_) | copy-start | bytes 1179652
  28.5 8.8 %copy-start.30 = (f32[768]{0:T(1024)S(1)}, f32[768]{0:T(1024)}, u32[]{:S(2)}) copy-start(f32[768]{0:T(1024)} %param.26) | copy-start | bytes 9220
  28.5 8.8 %copy-start.31 = (f32[768]{0:T(1024)S(1)}, f32[768]{0:T(1024)}, u32[]{:S(2)}) copy-start(f32[768]{0:T(1024)} %param.27) | copy-start | bytes 9220
  28.5 8.8 %copy-start.32 = (f32[768]{0:T(1024)S(1)}, f32[768]{0:T(1024)}, u32[]{:S(2)}) copy-start(f32[768]{0:T(1024)} %param.28) | copy-start | bytes 9220
  28.5 8.8 %copy-start.8 = (bf16[192,768]{1,0:T(8,128)(2,1)S(1)}, bf16[192,768]{1,0:T(8,128)(2,1)}, u32[]{:S(2)}) copy-start(bf16[192,768]{1,0:T(8,128)(2,1)} %refs_11_.4) | copy-start | bytes 884740
  28.5 8.8 %copy-start.16 = (bf16[192,768]{1,0:T(8,128)(2,1)S(1)}, bf16[192,768]{1,0:T(8,128)(2,1)}, u32[]{:S(2)}) copy-start(bf16[192,768]{1,0:T(8,128)(2,1)} %copy-done.15) | copy-start | bytes 884740
  36.2 5.6 %collective-permute-start.6 = (bf16[192,512]{1,0:T(8,128)(2,1)S(1)}, bf16[192,512]{1,0:T(8,128)(2,1)S(1)}, u32[]{:S(2)}, u32[]{:S(2)}) collective-permute-start(bf16[192,512]{1,0:T(8,128)(2,1)S(1)} %get-tuple-element.98), channel_id=1, source_target_pairs={{0,1},{1,0},{2,3},{3,2},{4,5},{5,4},{6,7},{7,6},{8,9},{9,8},{10,11... | collective-permute-start | bytes 589832 | tf_op jit(solution)/shard_map/ppermute | solution.py:774
  36.3 7.3 %collective-permute-start.7 = (bf16[192,512]{1,0:T(8,128)(2,1)S(1)}, bf16[192,512]{1,0:T(8,128)(2,1)S(1)}, u32[]{:S(2)}, u32[]{:S(2)}) collective-permute-start(bf16[192,512]{1,0:T(8,128)(2,1)S(1)} %get-tuple-element.99.refs_2_), channel_id=1, source_target_pairs={{0,2},{1,3},{2,0},{3,1},{4,6},{5,7},{6,4},{7,5},{8,10},{9,11},{10,... | collective-permute-start | bytes 589832 | tf_op jit(solution)/shard_map/ppermute | solution.py:778
  37.3 7.2 %copy-start.33 = (f32[768]{0:T(1024)S(1)}, f32[768]{0:T(1024)}, u32[]{:S(2)}) copy-start(f32[768]{0:T(1024)} %param.30) | copy-start | bytes 9220
  37.4 8.7 %copy-start.9 = (bf16[768,768]{1,0:T(8,128)(2,1)S(1)}, bf16[768,768]{1,0:T(8,128)(2,1)}, u32[]{:S(2)}) copy-start(bf16[768,768]{1,0:T(8,128)(2,1)} %refs_4_.3) | copy-start | bytes 3538948
  37.4 8.7 %copy-start.10 = (bf16[768,768]{1,0:T(8,128)(2,1)S(1)}, bf16[768,768]{1,0:T(8,128)(2,1)}, u32[]{:S(2)}) copy-start(bf16[768,768]{1,0:T(8,128)(2,1)} %refs_6_.5) | copy-start | bytes 3538948
  43.6 2.5 %collective-permute-start.8 = (bf16[512,768]{1,0:T(8,128)(2,1)}, bf16[512,768]{1,0:T(8,128)(2,1)S(1)}, u32[]{:S(2)}, u32[]{:S(2)}) collective-permute-start(bf16[512,768]{1,0:T(8,128)(2,1)} %get-tuple-element.100.refs_0_), channel_id=1, source_target_pairs={{0,1},{1,0},{2,3},{3,2},{4,5},{5,4},{6,7},{7,6},{8,9},{9,8},{10,11... | collective-permute-start | bytes 2359304 | tf_op jit(solution)/shard_map/ppermute | solution.py:774
  43.6 15.2 %collective-permute-start.9 = (bf16[192,512]{1,0:T(8,128)(2,1)S(1)}, bf16[192,512]{1,0:T(8,128)(2,1)S(1)}, u32[]{:S(2)}, u32[]{:S(2)}) collective-permute-start(bf16[192,512]{1,0:T(8,128)(2,1)S(1)} %collective-permute-done.6.refs_3_), channel_id=1, source_target_pairs={{0,2},{1,3},{2,0},{3,1},{4,6},{5,7},{6,4},{7,5},{8,10},{9,11},{10,... | collective-permute-start | bytes 589832 | tf_op jit(solution)/shard_map/ppermute | solution.py:778
  58.8 4.8 %collective-permute-start.10 = (bf16[512,768]{1,0:T(8,128)(2,1)}, bf16[512,768]{1,0:T(8,128)(2,1)S(1)}, u32[]{:S(2)}, u32[]{:S(2)}) collective-permute-start(bf16[512,768]{1,0:T(8,128)(2,1)} %get-tuple-element.109), channel_id=1, source_target_pairs={{0,1},{1,0},{2,3},{3,2},{4,5},{5,4},{6,7},{7,6},{8,9},{9,8},{10,11... | collective-permute-start | bytes 2359304 | tf_op jit(solution)/shard_map/ppermute | solution.py:774
  63.2 2.5 %copy-start.21 = (f32[8,768]{1,0:T(8,128)S(1)}, f32[8,768]{1,0:T(8,128)}, u32[]{:S(2)}) copy-start(f32[8,768]{1,0:T(8,128)} %get-tuple-element.101.refs_0_.refs_7_) | copy-start | bytes 73732
  63.2 2.5 %collective-permute-start.11 = (bf16[512,768]{1,0:T(8,128)(2,1)}, bf16[512,768]{1,0:T(8,128)(2,1)S(1)}, u32[]{:S(2)}, u32[]{:S(2)}) collective-permute-start(bf16[512,768]{1,0:T(8,128)(2,1)} %get-tuple-element.110.refs_1_), channel_id=1, source_target_pairs={{0,1},{1,0},{2,3},{3,2},{4,5},{5,4},{6,7},{7,6},{8,9},{9,8},{10,11... | collective-permute-start | bytes 2359304 | tf_op jit(solution)/shard_map/ppermute | solution.py:774
  63.8 1.9 copy-start.4
  63.8 19.7 %collective-permute-start.17 = (bf16[512,768]{1,0:T(8,128)(2,1)S(1)}, bf16[512,768]{1,0:T(8,128)(2,1)S(1)}, u32[]{:S(2)}, u32[]{:S(2)}) collective-permute-start(bf16[512,768]{1,0:T(8,128)(2,1)S(1)} %add_convert_fusion.6.refs_0_.refs_1_), channel_id=1, source_target_pairs={{0,2},{1,3},{2,0},{3,1},{4,6},{5,7},{6,4},{7,5},{8,10},{9,11},{10,... | collective-permute-start | bytes 2359304 | tf_op jit(solution)/shard_map/ppermute | solution.py:778
  78.8 9.9 %collective-permute-start.16 = (bf16[512,768]{1,0:T(8,128)(2,1)}, bf16[512,768]{1,0:T(8,128)(2,1)S(1)}, u32[]{:S(2)}, u32[]{:S(2)}) collective-permute-start(bf16[512,768]{1,0:T(8,128)(2,1)} %get-tuple-element.120), channel_id=1, source_target_pairs={{0,1},{1,0},{2,3},{3,2},{4,5},{5,4},{6,7},{7,6},{8,9},{9,8},{10,11... | collective-permute-start | bytes 2359304 | tf_op jit(solution)/shard_map/ppermute | solution.py:774
  79.3 28.2 %collective-permute-start.15 = (bf16[4,192,768]{2,1,0:T(8,128)(2,1)}, bf16[4,192,768]{2,1,0:T(8,128)(2,1)S(1)}, u32[]{:S(2)}, u32[]{:S(2)}) collective-permute-start(bf16[4,192,768]{2,1,0:T(8,128)(2,1)} %get-tuple-element.118), channel_id=1, source_target_pairs={{0,4},{4,0},{8,12},{12,8},{16,20},{20,16},{24,28},{28,24},{1,5},{5... | collective-permute-start | bytes 3538952 | tf_op jit(solution)/shard_map/ppermute | solution.py:890
  88.7 2.3 collective-permute-start.18
  89.0 2.1 copy-start.6
  89.0 20.0 %collective-permute-start.19 = (bf16[512,768]{1,0:T(8,128)(2,1)S(1)}, bf16[512,768]{1,0:T(8,128)(2,1)S(1)}, u32[]{:S(2)}, u32[]{:S(2)}) collective-permute-start(bf16[512,768]{1,0:T(8,128)(2,1)S(1)} %add_convert_fusion.2.refs_0_.refs_1_), channel_id=1, source_target_pairs={{0,2},{1,3},{2,0},{3,1},{4,6},{5,7},{6,4},{7,5},{8,10},{9,11},{10,... | collective-permute-start | bytes 2359304 | tf_op jit(solution)/shard_map/ppermute | solution.py:778
  90.0 29.5 %collective-permute-start.13 = (bf16[512,768]{1,0:T(8,128)(2,1)}, bf16[512,768]{1,0:T(8,128)(2,1)}, u32[]{:S(2)}, u32[]{:S(2)}) collective-permute-start(bf16[512,768]{1,0:T(8,128)(2,1)} %get-tuple-element.116), channel_id=1, source_target_pairs={{0,1},{1,0},{2,3},{3,2},{4,5},{5,4},{6,7},{7,6},{8,9},{9,8},{10,11... | collective-permute-start | bytes 2359304 | tf_op jit(solution)/shard_map/ppermute | solution.py:774
  90.2 29.3 %collective-permute-start.12 = (bf16[512,768]{1,0:T(8,128)(2,1)}, bf16[512,768]{1,0:T(8,128)(2,1)}, u32[]{:S(2)}, u32[]{:S(2)}) collective-permute-start(bf16[512,768]{1,0:T(8,128)(2,1)} %get-tuple-element.114), channel_id=1, source_target_pairs={{0,1},{1,0},{2,3},{3,2},{4,5},{5,4},{6,7},{7,6},{8,9},{9,8},{10,11... | collective-permute-start | bytes 2359304 | tf_op jit(solution)/shard_map/ppermute | solution.py:774
  91.0 17.9 %copy-start.27 = (bf16[4,192,768]{2,1,0:T(8,128)(2,1)S(1)}, bf16[4,192,768]{2,1,0:T(8,128)(2,1)}, u32[]{:S(2)}) copy-start(bf16[4,192,768]{2,1,0:T(8,128)(2,1)} %get-tuple-element.117) | copy-start | bytes 3538948
  110.3 5.0 %copy-start.7 = (bf16[512,768]{1,0:T(8,128)(2,1)S(1)}, bf16[512,768]{1,0:T(8,128)(2,1)}, u32[]{:S(2)}) copy-start(bf16[512,768]{1,0:T(8,128)(2,1)} %copy-done.6) | copy-start | bytes 2359300
  110.3 33.4 %all-to-all-start = ((bf16[4,192,768]{2,1,0:T(8,128)(2,1)}), bf16[4,192,768]{2,1,0:T(8,128)(2,1)S(1)}, u32[]{:S(2)}, u32[]{:S(2)}) async-start(bf16[4,192,768]{2,1,0:T(8,128)(2,1)} %add_convert_fusion.refs_0_), calls=%async_computation | async-start | bytes 2359296 | tf_op jit(solution)/shard_map/all_to_all | solution.py:894
  115.3 4.2 %copy-start.22 = (bf16[512,768]{1,0:T(8,128)(2,1)S(1)}, bf16[512,768]{1,0:T(8,128)(2,1)}, u32[]{:S(2)}) copy-start(bf16[512,768]{1,0:T(8,128)(2,1)} %get-tuple-element.115) | copy-start | bytes 2359300
  115.3 4.2 %copy-start.24 = (bf16[512,768]{1,0:T(8,128)(2,1)S(1)}, bf16[512,768]{1,0:T(8,128)(2,1)}, u32[]{:S(2)}) copy-start(bf16[512,768]{1,0:T(8,128)(2,1)} %get-tuple-element.113) | copy-start | bytes 2359300
  119.5 2.8 %collective-permute-start.20 = (bf16[512,768]{1,0:T(8,128)(2,1)S(1)}, bf16[512,768]{1,0:T(8,128)(2,1)S(1)}, u32[]{:S(2)}, u32[]{:S(2)}) collective-permute-start(bf16[512,768]{1,0:T(8,128)(2,1)S(1)} %get-tuple-element.127.refs_1_), channel_id=1, source_target_pairs={{0,1},{1,0},{2,3},{3,2},{4,5},{5,4},{6,7},{7,6},{8,9},{9,8},{10,11... | collective-permute-start | bytes 2359304 | tf_op jit(solution)/shard_map/ppermute | solution.py:774
  121.3 20.0 %collective-permute-start.14 = (bf16[512,768]{1,0:T(8,128)(2,1)S(1)}, bf16[512,768]{1,0:T(8,128)(2,1)S(1)}, u32[]{:S(2)}, u32[]{:S(2)}) collective-permute-start(bf16[512,768]{1,0:T(8,128)(2,1)S(1)} %broadcast_select_fusion.refs_0_), channel_id=1, source_target_pairs={{0,2},{1,3},{2,0},{3,1},{4,6},{5,7},{6,4},{7,5},{8,10},{9,11},{10,... | collective-permute-start | bytes 2359304 | tf_op jit(solution)/shard_map/ppermute | solution.py:778
  141.3 2.4 copy-start.26
  145.4 3.7 %copy-start.3 = (bf16[768,3,192]{0,2,1:T(8,128)(2,1)S(1)}, bf16[768,3,192]{0,2,1:T(8,128)(2,1)}, u32[]{:S(2)}) copy-start(bf16[768,3,192]{0,2,1:T(8,128)(2,1)} %param.22) | copy-start | bytes 2654212
  145.4 32.1 %all-to-all-start.1 = ((bf16[4,192,768]{2,1,0:T(8,128)(2,1)}), bf16[4,192,768]{2,1,0:T(8,128)(2,1)S(1)}, u32[]{:S(2)}, u32[]{:S(2)}) async-start(bf16[4,192,768]{2,1,0:T(8,128)(2,1)} %sum_parts.2.refs_0_), calls=%async_computation.1 | async-start | bytes 2359296 | tf_op jit(solution)/shard_map/all_to_all | solution.py:894
  162.6 16.4 %collective-permute-start.26 = (bf16[4,96,768]{2,1,0:T(8,128)(2,1)}, bf16[4,96,768]{2,1,0:T(8,128)(2,1)S(1)}, u32[]{:S(2)}, u32[]{:S(2)}) collective-permute-start(bf16[4,96,768]{2,1,0:T(8,128)(2,1)} %get-tuple-element.143), channel_id=1, source_target_pairs={{0,4},{4,0},{8,12},{12,8},{16,20},{20,16},{24,28},{28,24},{1,5},{5... | collective-permute-start | bytes 1769480 | tf_op jit(solution)/shard_map/ppermute | solution.py:890
  177.5 1.5 copy-start.1
  177.5 26.9 %collective-permute-start.27 = (bf16[4,192,768]{2,1,0:T(8,128)(2,1)S(1)}, bf16[4,192,768]{2,1,0:T(8,128)(2,1)S(1)}, u32[]{:S(2)}, u32[]{:S(2)}) collective-permute-start(bf16[4,192,768]{2,1,0:T(8,128)(2,1)S(1)} %all-to-all-done.1.refs_0_.mine_ref), channel_id=1, source_target_pairs={{0,4},{4,0},{8,12},{12,8},{16,20},{20,16},{24,28},{28,24},{1,5},{5... | collective-permute-start | bytes 3538952 | tf_op jit(solution)/shard_map/ppermute | solution.py:890
  179.0 6.8 %copy-start.28 = (f32[8,768]{1,0:T(8,128)S(1)}, f32[8,768]{1,0:T(8,128)}, u32[]{:S(2)}) copy-start(f32[8,768]{1,0:T(8,128)} %get-tuple-element.138) | copy-start | bytes 73732
  181.6 18.6 %all-to-all-start.2 = ((bf16[4,96,768]{2,1,0:T(8,128)(2,1)}), bf16[4,96,768]{2,1,0:T(8,128)(2,1)S(1)}, u32[]{:S(2)}, u32[]{:S(2)}) async-start(bf16[4,96,768]{2,1,0:T(8,128)(2,1)} %add_parts.1), calls=%async_computation.2 | async-start | bytes 1179648 | tf_op jit(solution)/shard_map/all_to_all | solution.py:894
  185.8 1.2 collective-permute-start.23
  187.1 3.8 %collective-permute-start.24 = (f32[8,768]{1,0:T(8,128)S(1)}, f32[8,768]{1,0:T(8,128)S(1)}, u32[]{:S(2)}, u32[]{:S(2)}) collective-permute-start(f32[8,768]{1,0:T(8,128)S(1)} %select_add_fusion.1), channel_id=1, source_target_pairs={{0,2},{1,3},{2,0},{3,1},{4,6},{5,7},{6,4},{7,5},{8,10},{9,11},{10,... | collective-permute-start | bytes 73736 | tf_op jit(solution)/shard_map/ppermute | solution.py:778
  188.0 21.8 %collective-permute-start.22 = (bf16[512,768]{1,0:T(8,128)(2,1)}, bf16[512,768]{1,0:T(8,128)(2,1)}, u32[]{:S(2)}, u32[]{:S(2)}) collective-permute-start(bf16[512,768]{1,0:T(8,128)(2,1)} %get-tuple-element.137), channel_id=1, source_target_pairs={{0,1},{1,0},{2,3},{3,2},{4,5},{5,4},{6,7},{7,6},{8,9},{9,8},{10,11... | collective-permute-start | bytes 2359304 | tf_op jit(solution)/shard_map/ppermute | solution.py:774
  205.9 21.7 %copy-start.23 = (bf16[512,768]{1,0:T(8,128)(2,1)S(1)}, bf16[512,768]{1,0:T(8,128)(2,1)}, u32[]{:S(2)}) copy-start(bf16[512,768]{1,0:T(8,128)(2,1)} %get-tuple-element.115) | copy-start | bytes 2359300
  205.9 21.7 %copy-start.29 = (f32[768]{0:T(1024)S(1)}, f32[768]{0:T(1024)}, u32[]{:S(2)}) copy-start(f32[768]{0:T(1024)} %param.32) | copy-start | bytes 9220
  205.9 20.2 %all-to-all-start.3 = ((bf16[4,112,768]{2,1,0:T(8,128)(2,1)}), bf16[4,112,768]{2,1,0:T(8,128)(2,1)S(1)}, u32[]{:S(2)}, u32[]{:S(2)}) async-start(bf16[4,112,768]{2,1,0:T(8,128)(2,1)} %sum_parts.3), calls=%async_computation.3 | async-start | bytes 1376256 | tf_op jit(solution)/shard_map/all_to_all | solution.py:894
  209.8 21.7 %collective-permute-start.21 = (bf16[512,768]{1,0:T(8,128)(2,1)}, bf16[512,768]{1,0:T(8,128)(2,1)}, u32[]{:S(2)}, u32[]{:S(2)}) collective-permute-start(bf16[512,768]{1,0:T(8,128)(2,1)} %get-tuple-element.135), channel_id=1, source_target_pairs={{0,1},{1,0},{2,3},{3,2},{4,5},{5,4},{6,7},{7,6},{8,9},{9,8},{10,11... | collective-permute-start | bytes 2359304 | tf_op jit(solution)/shard_map/ppermute | solution.py:774
  212.3 20.3 %copy-start.19 = (bf16[512,768]{1,0:T(8,128)(2,1)S(1)}, bf16[512,768]{1,0:T(8,128)(2,1)}, u32[]{:S(2)}) copy-start(bf16[512,768]{1,0:T(8,128)(2,1)} %get-tuple-element.134.mine_ref) | copy-start | bytes 2359300
  212.3 20.2 %collective-permute-start.25 = (bf16[512,768]{1,0:T(8,128)(2,1)}, bf16[512,768]{1,0:T(8,128)(2,1)}, u32[]{:S(2)}, u32[]{:S(2)}) collective-permute-start(bf16[512,768]{1,0:T(8,128)(2,1)} %add_convert_fusion.1), channel_id=1, source_target_pairs={{0,2},{1,3},{2,0},{3,1},{4,6},{5,7},{6,4},{7,5},{8,10},{9,11},{10,... | collective-permute-start | bytes 2359304 | tf_op jit(solution)/shard_map/ppermute | solution.py:778
  226.0 16.4 %collective-permute-start.28 = (bf16[4,112,768]{2,1,0:T(8,128)(2,1)S(1)}, bf16[4,112,768]{2,1,0:T(8,128)(2,1)S(1)}, u32[]{:S(2)}, u32[]{:S(2)}) collective-permute-start(bf16[4,112,768]{2,1,0:T(8,128)(2,1)S(1)} %all-to-all-done.3.mine_ref), channel_id=1, source_target_pairs={{0,4},{4,0},{8,12},{12,8},{16,20},{20,16},{24,28},{28,24},{1,5},{5... | collective-permute-start | bytes 2064392 | tf_op jit(solution)/shard_map/ppermute | solution.py:890
  232.5 4.0 %copy-start.2 = (bf16[4,192,768]{2,1,0:T(8,128)(2,1)S(1)}, bf16[4,192,768]{2,1,0:T(8,128)(2,1)}, u32[]{:S(2)}) copy-start(bf16[4,192,768]{2,1,0:T(8,128)(2,1)} %copy-done.1) | copy-start | bytes 3538948
  (3 other events, 2.9 us)
